TPU v7x, 32 devices: a whole 2x2x4 slice. The times are simulated.
32 devices in a mesh: ctx: 16 (over z, y, core), fsdp: 2 (over x).
Axes of the slice: x: 2, y: 2, z: 4, core: 2. Of those that a mesh axis runs over, the one named last changes fastest.
Arguments:
- layer_input: float32 [4096, 1024], P(('ctx', 'fsdp')), may hold values from -6 to 6
- grad_output: float32 [4096, 1024], P(('ctx', 'fsdp')), may hold values from -6 to 6
- positions: int32 [4096], replicated, may hold values from 0 to 4095, as said below
- w_query: bfloat16 [1024, 2048], P(('ctx', 'fsdp')), may hold values from -0.1875 to 0.1875
- w_key: bfloat16 [1024, 2048], P(('ctx', 'fsdp')), may hold values from -0.1875 to 0.1875
- w_value: bfloat16 [1024, 2048], P(('ctx', 'fsdp')), may hold values from -0.1875 to 0.1875
- w_out: bfloat16 [2048, 1024], P(('ctx', 'fsdp')), may hold values from -0.125 to 0.125
- w_gate: bfloat16 [1024, 4096], P(('ctx', 'fsdp')), may hold values from -0.1875 to 0.1875
- w_up: bfloat16 [1024, 4096], P(('ctx', 'fsdp')), may hold values from -0.1875 to 0.1875
- w_down: bfloat16 [4096, 1024], P(('ctx', 'fsdp')), may hold values from -0.09375 to 0.09375
- gain_query: bfloat16 [2048], P(('ctx', 'fsdp')), may hold values from 0.5 to 1.5
- gain_key: bfloat16 [2048], P(('ctx', 'fsdp')), may hold values from 0.5 to 1.5
- gain_attn: bfloat16 [1024], P(('ctx', 'fsdp')), may hold values from 0.5 to 1.5
- gain_mlp: bfloat16 [1024], P(('ctx', 'fsdp')), may hold values from 0.5 to 1.5
Outputs:
- output: float32 [4096, 1024], P(('ctx', 'fsdp'))
- grad_input: float32 [4096, 1024], P(('ctx', 'fsdp'))
- grad_w_query: float32 [1024, 2048], P('fsdp')
- grad_w_key: float32 [1024, 2048], P('fsdp')
- grad_w_value: float32 [1024, 2048], P('fsdp')
- grad_w_out: float32 [2048, 1024], P('fsdp')
- grad_w_gate: float32 [1024, 4096], P('fsdp')
- grad_w_up: float32 [1024, 4096], P('fsdp')
- grad_w_down: float32 [4096, 1024], P('fsdp')
- grad_gain_query: float32 [2048], P('fsdp')
- grad_gain_key: float32 [2048], P('fsdp')
- grad_gain_attn: float32 [1024], P('fsdp')
- grad_gain_mlp: float32 [1024], P('fsdp')
Inputs may be any that keep to these rules, and one draw needn't show every extreme that they name: positions holds each of 0 to 4095 once. The 128 rows of device d (rows d * 128 onward, devices in the order ctx then fsdp) are two sequence blocks of 64 consecutive positions: block p first and block 63 - p second, for some p below 32 that differs from device to device.
All inputs are finite; a program needn't handle non-finite values.
Results may differ from a plain program's by a relative error of at most 0.023.
Values may be sent and summed in bfloat16 or wider, within the bound.
No kernel may reach another device: no remote copies, remote signals or barrier semaphores. Data moves between devices by JAX's collectives and lax.ppermute only.
A program may use at most 768 MiB of HBM per device.

v0:
```python
import math

import jax
import jax.numpy as jnp
from jax import lax
from jax.sharding import PartitionSpec as P

H = 16
HD = 128


EPS = 1e-06
THETA = 500000.0
NEG = -1e30


def norm_forward(value, gain):
    recip = lax.rsqrt(jnp.mean(value * value, axis=-1, keepdims=True) + EPS)
    return (value * recip * gain.astype(jnp.float32), recip)


def norm_backward(value, recip, gain, grad_out):
    scaled = grad_out * gain.astype(jnp.float32)
    width = value.shape[-1]
    grad_in = (
        recip * scaled
        - value * (recip * recip * recip) * jnp.sum(scaled * value, axis=-1, keepdims=True) / width
    )
    grad_gain = jnp.sum(grad_out * value * recip, axis=0)
    return (grad_in, grad_gain)


def rotary_tables(where, head_size):
    half = head_size // 2
    freqs = THETA ** (-(2.0 * jnp.arange(half, dtype=jnp.float32)) / head_size)
    angles = where.astype(jnp.float32)[:, None] * freqs[None, :]
    return (jnp.cos(angles)[:, None, :], jnp.sin(angles)[:, None, :])


def rotate(flat, cosine, sine, heads, head_size):
    half = head_size // 2
    table = flat.reshape(flat.shape[0], heads, head_size)
    first = table[..., :half]
    second = table[..., half:]
    joined = jnp.concatenate(
        [first * cosine - second * sine, second * cosine + first * sine], axis=-1
    )
    return joined.reshape(flat.shape[0], heads * head_size)


def unrotate(flat, cosine, sine, heads, head_size):
    half = head_size // 2
    table = flat.reshape(flat.shape[0], heads, head_size)
    first = table[..., :half]
    second = table[..., half:]
    joined = jnp.concatenate(
        [first * cosine + second * sine, second * cosine - first * sine], axis=-1
    )
    return joined.reshape(flat.shape[0], heads * head_size)


def block_size():
    return 512


def per_device(
    layer_input,
    grad_output,
    positions,
    w_query,
    w_key,
    w_value,
    w_out,
    w_gate,
    w_up,
    w_down,
    gain_query,
    gain_key,
    gain_attn,
    gain_mlp,
):
    f32 = jnp.float32
    bf16 = jnp.bfloat16
    rows = layer_input.shape[0]
    heads = H
    head_size = HD
    width = heads * head_size
    scale = 1.0 / math.sqrt(head_size)
    first_row = lax.axis_index(("ctx", "fsdp")) * rows
    my_pos = lax.dynamic_slice_in_dim(positions, first_row, rows)
    cosine, sine = rotary_tables(my_pos, head_size)
    full_query, full_key, full_value, full_out, full_gq, full_gk, full_ga = (
        lax.all_gather(w_query, ("ctx", "fsdp"), axis=0, tiled=True),
        lax.all_gather(w_key, ("ctx", "fsdp"), axis=0, tiled=True),
        lax.all_gather(w_value, ("ctx", "fsdp"), axis=0, tiled=True),
        lax.all_gather(w_out, ("ctx", "fsdp"), axis=0, tiled=True),
        lax.all_gather(gain_query, ("ctx", "fsdp"), axis=0, tiled=True),
        lax.all_gather(gain_key, ("ctx", "fsdp"), axis=0, tiled=True),
        lax.all_gather(gain_attn, ("ctx", "fsdp"), axis=0, tiled=True),
    )
    xb = layer_input.astype(bf16)
    query_pre = jnp.dot(xb, full_query, preferred_element_type=f32)
    key_pre = jnp.dot(xb, full_key, preferred_element_type=f32)
    query_normed, q_recip = norm_forward(query_pre, full_gq)
    key_normed, k_recip = norm_forward(key_pre, full_gk)
    query = rotate(query_normed, cosine, sine, heads, head_size).astype(bf16)
    key = rotate(key_normed, cosine, sine, heads, head_size).astype(bf16)
    value = jnp.dot(xb, full_value, preferred_element_type=f32).astype(bf16)
    q3 = query.reshape(rows, heads, head_size)
    k3 = key.reshape(rows, heads, head_size)
    v3 = value.reshape(rows, heads, head_size)
    start_state = (
        jnp.full((heads, rows), NEG, f32),
        jnp.zeros((heads, rows), f32),
        jnp.zeros((rows, heads, head_size), f32),
    )
    keys_in = lax.all_gather(key, ("ctx", "fsdp"), axis=0, tiled=True)
    values_in = lax.all_gather(value, ("ctx", "fsdp"), axis=0, tiled=True)
    count = keys_in.shape[0]
    size = block_size()

    def attend_step(state, index):
        top_run, total_run, accum = state
        low = index * size
        kb = lax.dynamic_slice_in_dim(keys_in, low, size).reshape(size, heads, head_size)
        vb = lax.dynamic_slice_in_dim(values_in, low, size).reshape(size, heads, head_size)
        pb = lax.dynamic_slice_in_dim(positions, low, size)
        scores = jnp.einsum("qhd,khd->hqk", q3, kb, preferred_element_type=f32) * scale
        allowed = pb[None, None, :] <= my_pos[None, :, None]
        scores = jnp.where(allowed, scores, NEG)
        top_new = jnp.maximum(top_run, jnp.max(scores, axis=-1))
        probs = jnp.where(allowed, jnp.exp(scores - top_new[:, :, None]), 0.0)
        factor = jnp.exp(top_run - top_new)
        total_new = total_run * factor + jnp.sum(probs, axis=-1)
        accum_new = accum * factor.T[:, :, None] + jnp.einsum(
            "hqk,khd->qhd", probs.astype(bf16), vb, preferred_element_type=f32
        )
        return ((top_new, total_new, accum_new), None)

    state, _ = lax.scan(attend_step, start_state, jnp.arange(count // size, dtype=jnp.int32))
    top_run, total_run, accum = state
    lse = top_run + jnp.log(total_run)
    attended = (accum / total_run.T[:, :, None]).reshape(rows, width).astype(bf16)
    full_gate, full_up, full_down, full_gm = (
        lax.all_gather(w_gate, ("ctx", "fsdp"), axis=0, tiled=True),
        lax.all_gather(w_up, ("ctx", "fsdp"), axis=0, tiled=True),
        lax.all_gather(w_down, ("ctx", "fsdp"), axis=0, tiled=True),
        lax.all_gather(gain_mlp, ("ctx", "fsdp"), axis=0, tiled=True),
    )
    proj = jnp.dot(attended, full_out, preferred_element_type=f32)
    attn_branch, a_recip = norm_forward(proj, full_ga)
    mid = layer_input + attn_branch
    midb = mid.astype(bf16)
    gate = jnp.dot(midb, full_gate, preferred_element_type=f32)
    up = jnp.dot(midb, full_up, preferred_element_type=f32)
    sig = jax.nn.sigmoid(gate)
    silu = gate * sig
    hidden = (silu * up).astype(bf16)
    down = jnp.dot(hidden, full_down, preferred_element_type=f32)
    mlp_branch, m_recip = norm_forward(down, full_gm)
    output = mid + mlp_branch
    d_down_f, local_gm = norm_backward(down, m_recip, full_gm, grad_output)
    d_down = d_down_f.astype(bf16)
    local_wd = jnp.dot(hidden.T, d_down, preferred_element_type=f32)
    d_hidden = jnp.dot(d_down, full_down.T, preferred_element_type=f32)
    d_gate = (d_hidden * up * sig * (1.0 + gate * (1.0 - sig))).astype(bf16)
    d_up = (d_hidden * silu).astype(bf16)
    local_wg = jnp.dot(midb.T, d_gate, preferred_element_type=f32)
    local_wu = jnp.dot(midb.T, d_up, preferred_element_type=f32)
    d_mid = (
        grad_output
        + jnp.dot(d_gate, full_gate.T, preferred_element_type=f32)
        + jnp.dot(d_up, full_up.T, preferred_element_type=f32)
    )
    d_proj_f, local_ga = norm_backward(proj, a_recip, full_ga, d_mid)
    d_proj = d_proj_f.astype(bf16)
    local_wo = jnp.dot(attended.T, d_proj, preferred_element_type=f32)
    d_att = jnp.dot(d_proj, full_out.T, preferred_element_type=f32).astype(bf16)
    da3 = d_att.reshape(rows, heads, head_size)
    delta_rows = jnp.sum(
        da3.astype(f32) * attended.reshape(rows, heads, head_size).astype(f32), axis=-1
    )
    delta_local = delta_rows.T
    lse_all, delta_all = (
        lax.all_gather(lse.T, ("ctx", "fsdp"), axis=0, tiled=True),
        lax.all_gather(delta_rows, ("ctx", "fsdp"), axis=0, tiled=True),
    )
    zero_rows = jnp.zeros((rows, heads, head_size), f32)
    query_keys_in = lax.all_gather(key, ("ctx", "fsdp"), axis=0, tiled=True)
    query_values_in = lax.all_gather(value, ("ctx", "fsdp"), axis=0, tiled=True)
    count = query_keys_in.shape[0]
    query_size = block_size()

    def query_step(accum, index):
        low = index * query_size
        kb = lax.dynamic_slice_in_dim(query_keys_in, low, query_size).reshape(
            query_size, heads, head_size
        )
        vb = lax.dynamic_slice_in_dim(query_values_in, low, query_size).reshape(
            query_size, heads, head_size
        )
        pb = lax.dynamic_slice_in_dim(positions, low, query_size)
        scores = jnp.einsum("qhd,khd->hqk", q3, kb, preferred_element_type=f32) * scale
        allowed = pb[None, None, :] <= my_pos[None, :, None]
        probs = jnp.where(allowed, jnp.exp(scores - lse[:, :, None]), 0.0)
        dprob = jnp.einsum("qhd,khd->hqk", da3, vb, preferred_element_type=f32)
        dscore = (probs * (dprob - delta_local[:, :, None])).astype(bf16)
        return (accum + jnp.einsum("hqk,khd->qhd", dscore, kb, preferred_element_type=f32), None)

    accum, _ = lax.scan(query_step, zero_rows, jnp.arange(count // query_size, dtype=jnp.int32))
    queries_in = lax.all_gather(query, ("ctx", "fsdp"), axis=0, tiled=True)
    cotangents_in = lax.all_gather(d_att, ("ctx", "fsdp"), axis=0, tiled=True)
    count = queries_in.shape[0]
    key_size = block_size()

    def key_step(state, index):
        dk_run, dv_run = state
        low = index * key_size
        qb = lax.dynamic_slice_in_dim(queries_in, low, key_size).reshape(key_size, heads, head_size)
        db = lax.dynamic_slice_in_dim(cotangents_in, low, key_size).reshape(
            key_size, heads, head_size
        )
        pb = lax.dynamic_slice_in_dim(positions, low, key_size)
        lse_b = lax.dynamic_slice_in_dim(lse_all, low, key_size)
        delta_b = lax.dynamic_slice_in_dim(delta_all, low, key_size)
        scores = jnp.einsum("qhd,khd->hqk", qb, k3, preferred_element_type=f32) * scale
        allowed = my_pos[None, None, :] <= pb[None, :, None]
        probs = jnp.where(allowed, jnp.exp(scores - lse_b.T[:, :, None]), 0.0)
        dv_new = dv_run + jnp.einsum(
            "hqk,qhd->khd", probs.astype(bf16), db, preferred_element_type=f32
        )
        dprob = jnp.einsum("qhd,khd->hqk", db, v3, preferred_element_type=f32)
        dscore = (probs * (dprob - delta_b.T[:, :, None])).astype(bf16)
        dk_new = dk_run + jnp.einsum("hqk,qhd->khd", dscore, qb, preferred_element_type=f32)
        return ((dk_new, dv_new), None)

    state, _ = lax.scan(
        key_step, (zero_rows, zero_rows), jnp.arange(count // key_size, dtype=jnp.int32)
    )
    dk_acc, dv_acc = state
    d_query_rot = (accum * scale).reshape(rows, width)
    d_key_rot = (dk_acc * scale).reshape(rows, width)
    d_value = dv_acc.reshape(rows, width).astype(bf16)
    dq_f, local_gq = norm_backward(
        query_pre, q_recip, full_gq, unrotate(d_query_rot, cosine, sine, heads, head_size)
    )
    dk_f, local_gk = norm_backward(
        key_pre, k_recip, full_gk, unrotate(d_key_rot, cosine, sine, heads, head_size)
    )
    d_query_pre = dq_f.astype(bf16)
    d_key_pre = dk_f.astype(bf16)
    local_wq = jnp.dot(xb.T, d_query_pre, preferred_element_type=f32)
    local_wk = jnp.dot(xb.T, d_key_pre, preferred_element_type=f32)
    local_wv = jnp.dot(xb.T, d_value, preferred_element_type=f32)
    grad_input = (
        d_mid
        + jnp.dot(d_query_pre, full_query.T, preferred_element_type=f32)
        + jnp.dot(d_key_pre, full_key.T, preferred_element_type=f32)
        + jnp.dot(d_value, full_value.T, preferred_element_type=f32)
    )
    (
        share_wq,
        share_wk,
        share_wv,
        share_wo,
        share_wg,
        share_wu,
        share_wd,
        share_gq,
        share_gk,
        share_ga,
        share_gm,
    ) = (
        lax.psum_scatter(
            local_wq.astype(jnp.bfloat16), "fsdp", scatter_dimension=0, tiled=True
        ).astype(jnp.float32),
        lax.psum_scatter(
            local_wk.astype(jnp.bfloat16), "fsdp", scatter_dimension=0, tiled=True
        ).astype(jnp.float32),
        lax.psum_scatter(
            local_wv.astype(jnp.bfloat16), "fsdp", scatter_dimension=0, tiled=True
        ).astype(jnp.float32),
        lax.psum_scatter(
            local_wo.astype(jnp.bfloat16), "fsdp", scatter_dimension=0, tiled=True
        ).astype(jnp.float32),
        lax.psum_scatter(
            local_wg.astype(jnp.bfloat16), "fsdp", scatter_dimension=0, tiled=True
        ).astype(jnp.float32),
        lax.psum_scatter(
            local_wu.astype(jnp.bfloat16), "fsdp", scatter_dimension=0, tiled=True
        ).astype(jnp.float32),
        lax.psum_scatter(
            local_wd.astype(jnp.bfloat16), "fsdp", scatter_dimension=0, tiled=True
        ).astype(jnp.float32),
        lax.psum_scatter(
            local_gq.astype(jnp.bfloat16), "fsdp", scatter_dimension=0, tiled=True
        ).astype(jnp.float32),
        lax.psum_scatter(
            local_gk.astype(jnp.bfloat16), "fsdp", scatter_dimension=0, tiled=True
        ).astype(jnp.float32),
        lax.psum_scatter(
            local_ga.astype(jnp.bfloat16), "fsdp", scatter_dimension=0, tiled=True
        ).astype(jnp.float32),
        lax.psum_scatter(
            local_gm.astype(jnp.bfloat16), "fsdp", scatter_dimension=0, tiled=True
        ).astype(jnp.float32),
    )
    (
        total_wq,
        total_wk,
        total_wv,
        total_wo,
        total_wg,
        total_wu,
        total_wd,
        total_gq,
        total_gk,
        total_ga,
        total_gm,
    ) = lax.psum(
        (
            share_wq,
            share_wk,
            share_wv,
            share_wo,
            share_wg,
            share_wu,
            share_wd,
            share_gq,
            share_gk,
            share_ga,
            share_gm,
        ),
        "ctx",
    )
    return (
        output,
        grad_input,
        total_wq,
        total_wk,
        total_wv,
        total_wo,
        total_wg,
        total_wu,
        total_wd,
        total_gq,
        total_gk,
        total_ga,
        total_gm,
    )


def solution(mesh):
    in_specs = (
        P(("ctx", "fsdp"), None),
        P(("ctx", "fsdp"), None),
        P(),
        P(("ctx", "fsdp"), None),
        P(("ctx", "fsdp"), None),
        P(("ctx", "fsdp"), None),
        P(("ctx", "fsdp"), None),
        P(("ctx", "fsdp"), None),
        P(("ctx", "fsdp"), None),
        P(("ctx", "fsdp"), None),
        P(("ctx", "fsdp")),
        P(("ctx", "fsdp")),
        P(("ctx", "fsdp")),
        P(("ctx", "fsdp")),
    )
    out_specs = (
        P(("ctx", "fsdp"), None),
        P(("ctx", "fsdp"), None),
        P("fsdp", None),
        P("fsdp", None),
        P("fsdp", None),
        P("fsdp", None),
        P("fsdp", None),
        P("fsdp", None),
        P("fsdp", None),
        P("fsdp"),
        P("fsdp"),
        P("fsdp"),
        P("fsdp"),
    )
    return jax.shard_map(
        per_device, mesh=mesh, in_specs=in_specs, out_specs=out_specs, check_vma=False
    )
```

profile of v0, /device:TPU:0, one launch (start us, length us, event | category | flops | bytes accessed | tf_op | source)
XLA Modules:
  0.0 2478.7 jit_solution(6300280929021746939)
XLA Ops:
  10.6 64.9 %all-gather.18.cloned.1.call-done = bf16[1024,2048]{1,0:T(8,128)(2,1)} async-done(((bf16[32,2048]{1,0:T(8,128)(2,1)}), bf16[1024,2048]{1,0:T(8,128)(2,1)}) %all-gather.18.cloned.1.call-update) | async-done | bytes 4194320 | tf_op jit(solution)/shard_map/all_gather | solution.py:95
  80.3 39.5 %all-reduce.9 = (bf16[2048]{0:T(1024)(128)(2,1)S(1)}, bf16[2048]{0:T(1024)(128)(2,1)S(1)}, bf16[1024]{0:T(1024)(128)(2,1)S(1)}, bf16[1024]{0:T(1024)(128)(2,1)S(1)}) all-reduce(bf16[2048]{0:T(1024)(128)(2,1)S(1)} %dynamic-update-slice, bf16[2048]{0:T(1024)(128)(2,1)S(1)} %dynamic-update-slice.1, ...), channel_id=1, replica_groups=mesh['ctx'=16,'fsdp'=2] {'ctx','fsdp'}, use_global_device_ids=true, to_apply=%add | all-reduce | flops 6144 | bytes 24576
  120.9 18.3 all-gather.12.cloned.1.call-done
  143.7 59.0 %all-gather.16.cloned.1.call-done = bf16[1024,2048]{1,0:T(8,128)(2,1)} async-done(((bf16[32,2048]{1,0:T(8,128)(2,1)}), bf16[1024,2048]{1,0:T(8,128)(2,1)}) %all-gather.16.cloned.1.call-update) | async-done | bytes 4194320 | tf_op jit(solution)/shard_map/all_gather | solution.py:93
  213.8 105.0 %all-gather.20.cloned.1.call-done = bf16[4096,2048]{1,0:T(8,128)(2,1)} async-done(((bf16[128,2048]{1,0:T(8,128)(2,1)}), bf16[4096,2048]{1,0:T(8,128)(2,1)}) %all-gather.20.cloned.1.call-update) | async-done | bytes 16777232 | tf_op jit(solution)/shard_map/all_gather | solution.py:118
  318.7 20.8 copy.105
  339.6 127.5 %all-gather.14.cloned.1.call-done = bf16[4096,2048]{0,1:T(8,128)(2,1)} async-done(((bf16[128,2048]{0,1:T(8,128)(2,1)}), bf16[4096,2048]{0,1:T(8,128)(2,1)}) %all-gather.14.cloned.1.call-update) | async-done | bytes 16777232 | tf_op jit(solution)/shard_map/all_gather | solution.py:117
  467.1 111.3 %while.39 = (s32[]{:T(128)}, f32[16,128]{1,0:T(8,128)S(1)}, f32[16,128]{1,0:T(8,128)S(1)}, f32[128,16,128]{0,2,1:T(8,128)}, s32[8]{0:T(128)S(1)}, /*index=5*/s32...) while((s32[]{:T(128)}, f32[16,128]{1,0:T(8,128)S(1)}, ...), condition=%wide.region_5.6_spmd.clone, body=%wide.region_2.5_spmd.clone.sunk | while | flops 551366656 | bytes 44964588 | solution.py:140
  583.3 25.4 %all-gather.24.cloned.1.call-done = bf16[1024,4096]{1,0:T(8,128)(2,1)} async-done(((bf16[32,4096]{1,0:T(8,128)(2,1)}), bf16[1024,4096]{1,0:T(8,128)(2,1)}) %all-gather.24.cloned.1.call-update) | async-done | bytes 8388624 | tf_op jit(solution)/shard_map/all_gather | solution.py:145
  614.7 72.8 %all-gather.26.cloned.1.call-done = bf16[1024,4096]{1,0:T(8,128)(2,1)} async-done(((bf16[32,4096]{1,0:T(8,128)(2,1)}), bf16[1024,4096]{1,0:T(8,128)(2,1)}) %all-gather.26.cloned.1.call-update) | async-done | bytes 8388624 | tf_op jit(solution)/shard_map/all_gather | solution.py:146
  687.5 6.9 multiply_convert_fusion.3
  694.3 71.9 %all-gather.28.cloned.1.call-done = bf16[4096,1024]{1,0:T(8,128)(2,1)} async-done(((bf16[128,1024]{1,0:T(8,128)(2,1)}), bf16[4096,1024]{1,0:T(8,128)(2,1)}) %all-gather.28.cloned.1.call-update) | async-done | bytes 8388624 | tf_op jit(solution)/shard_map/all_gather | solution.py:147
  790.1 11.4 subtract_convert_fusion.2
  826.9 111.9 %all_gather.69 = f32[4096,16]{1,0:T(8,128)} all-gather(f32[128,16]{1,0:T(8,128)S(1)} %copy.133), channel_id=1, replica_groups=mesh['ctx'=16,'fsdp'=2] {'ctx','fsdp'}, dimensions={0}, use_global_device_ids=true | all-gather | bytes 270336 | tf_op jit(solution)/shard_map/all_gather | solution.py:186
  941.7 72.3 %all_gather.67 = f32[4096,16]{0,1:T(8,128)} all-gather(f32[128,16]{0,1:T(8,128)S(1)} %bitcast.239), channel_id=1, replica_groups=mesh['ctx'=16,'fsdp'=2] {'ctx','fsdp'}, dimensions={0}, use_global_device_ids=true | all-gather | bytes 270336 | tf_op jit(solution)/shard_map/all_gather | solution.py:185
  1014.9 121.4 %while.40 = (s32[]{:T(128)}, f32[128,16,128]{0,2,1:T(8,128)}, s32[8]{0:T(128)S(1)}, bf16[4096,2048]{0,1:T(8,128)(2,1)}, s32[4096]{0:T(1024)}, /*index=5*/s32[128...) while((s32[]{:T(128)}, f32[128,16,128]{0,2,1:T(8,128)}, ...), condition=%wide.region_12.13_spmd.clone, body=%wide.region_11.12_spmd.clone.sunk | while | flops 812187648 | bytes 26368728 | solution.py:210
  1138.7 7.0 convolution_convert_fusion.1
  1145.8 211.1 %while.41 = (s32[]{:T(128)}, f32[128,16,128]{0,2,1:T(8,128)}, f32[128,16,128]{0,2,1:T(8,128)}, s32[8]{0:T(128)S(1)}, bf16[4096,2048]{0,1:T(8,128)(2,1)}, /*index...) while((s32[]{:T(128)}, f32[128,16,128]{0,2,1:T(8,128)}, ...), condition=%wide.region_15.16_spmd.clone, body=%wide.region_14.15_spmd.clone.sunk | while | flops 1085341696 | bytes 39230184 | solution.py:237
  1378.1 45.7 %reduce-scatter.18.cloned.1.call-done = bf16[512,4096]{1,0:T(8,128)(2,1)} async-done(((bf16[1024,4096]{1,0:T(8,128)(2,1)}), bf16[512,4096]{1,0:T(8,128)(2,1)}) %reduce-scatter.18.cloned.1.call-update) | async-done | bytes 4194320 | tf_op jit(solution)/shard_map/reduce_scatter | solution.py:289
  1423.8 7.1 all-reduce.10
  1440.2 40.8 %reduce-scatter.10.cloned.1.call-done = bf16[512,2048]{0,1:T(8,128)(2,1)} async-done(((bf16[1024,2048]{0,1:T(8,128)(2,1)}), bf16[512,2048]{0,1:T(8,128)(2,1)}) %reduce-scatter.10.cloned.1.call-update) | async-done | bytes 2097168 | tf_op jit(solution)/shard_map/reduce_scatter | solution.py:277
  1481.0 57.1 %reduce-scatter.8.cloned.1.call-done = bf16[512,2048]{0,1:T(8,128)(2,1)} async-done(((bf16[1024,2048]{0,1:T(8,128)(2,1)}), bf16[512,2048]{0,1:T(8,128)(2,1)}) %reduce-scatter.8.cloned.1.call-update) | async-done | bytes 2097168 | tf_op jit(solution)/shard_map/reduce_scatter | solution.py:274
  1538.1 57.1 %reduce-scatter.12.cloned.1.call-done = bf16[512,2048]{0,1:T(8,128)(2,1)} async-done(((bf16[1024,2048]{0,1:T(8,128)(2,1)}), bf16[512,2048]{0,1:T(8,128)(2,1)}) %reduce-scatter.12.cloned.1.call-update) | async-done | bytes 2097168 | tf_op jit(solution)/shard_map/reduce_scatter | solution.py:280
  1595.3 860.2 %all-reduce.12 = (f32[512,2048]{0,1:T(8,128)}, f32[512,2048]{0,1:T(8,128)}, f32[512,2048]{0,1:T(8,128)}, f32[1024,1024]{1,0:T(8,128)}, f32[512,4096]{1,0:T(8,128...) all-reduce(bf16[512,2048]{0,1:T(8,128)(2,1)} %reduce-scatter.8.clon, ...), channel_id=1, replica_groups=mesh['ctx'=16,'fsdp'=2] {'ctx'}, use_global_device_ids=true, to_apply=%region_18.19 | all-reduce | flops 10488832 | bytes 62939136 | tf_op jit(solution)/shard_map/psum | solution.py:320
  (449 shorter events, 562.5 us)
Async XLA Ops:
  7.2 68.3 %all-gather.18.cloned.1.call-start = ((), (), s32[]{:S(2)}) async-start(), calls=%async_computation.10 | async-start | bytes 4325376 | tf_op jit(solution)/shard_map/all_gather | solution.py:95
  8.0 131.2 %all-gather.12.cloned.1.call-start = ((), (), s32[]{:S(2)}) async-start(), calls=%async_computation.7 | async-start | bytes 4325376 | tf_op jit(solution)/shard_map/all_gather | solution.py:94
  8.7 194.0 %all-gather.16.cloned.1.call-start = ((), (), s32[]{:S(2)}) async-start(), calls=%async_computation.9 | async-start | bytes 4325376 | tf_op jit(solution)/shard_map/all_gather | solution.py:93
  9.4 309.3 %all-gather.20.cloned.1.call-start = ((), (), s32[]{:S(2)}) async-start(), calls=%async_computation.11 | async-start | bytes 17301504 | tf_op jit(solution)/shard_map/all_gather | solution.py:118
  10.6 192.2 %copy-start.9 = (bf16[128,1024]{1,0:T(8,128)(2,1)}, bf16[128,1024]{1,0:T(8,128)(2,1)S(1)}, u32[]{:S(2)}) copy-start(bf16[128,1024]{1,0:T(8,128)(2,1)S(1)} %convert_element_type.172) | copy-start | bytes 786436
  79.3 387.8 %all-gather.14.cloned.1.call-start = ((), (), s32[]{:S(2)}) async-start(), calls=%async_computation.8 | async-start | bytes 17301504 | tf_op jit(solution)/shard_map/all_gather | solution.py:117
  120.9 86.5 %copy-start.26 = (f32[128,64]{0,1:T(8,128)}, f32[128,64]{0,1:T(8,128)S(1)}, u32[]{:S(2)}) copy-start(f32[128,64]{0,1:T(8,128)S(1)} %get-tuple-element.606) | copy-start | bytes 98308
  120.9 86.5 %copy-start.28 = (f32[128,64]{0,1:T(8,128)}, f32[128,64]{0,1:T(8,128)S(1)}, u32[]{:S(2)}) copy-start(f32[128,64]{0,1:T(8,128)S(1)} %get-tuple-element.607) | copy-start | bytes 98308
  208.6 371.6 %all-gather.22.cloned.1.call-start = ((), (), s32[]{:S(2)}) async-start(), calls=%async_computation.12 | async-start | bytes 4325376 | tf_op jit(solution)/shard_map/all_gather | solution.py:96
  209.1 399.6 %all-gather.24.cloned.1.call-start = ((), (), s32[]{:S(2)}) async-start(), calls=%async_computation.13 | async-start | bytes 8650752 | tf_op jit(solution)/shard_map/all_gather | solution.py:145
  209.9 477.6 %all-gather.26.cloned.1.call-start = ((), (), s32[]{:S(2)}) async-start(), calls=%async_computation.14 | async-start | bytes 8650752 | tf_op jit(solution)/shard_map/all_gather | solution.py:146
  210.6 555.6 %all-gather.28.cloned.1.call-start = ((), (), s32[]{:S(2)}) async-start(), calls=%async_computation.15 | async-start | bytes 8650752 | tf_op jit(solution)/shard_map/all_gather | solution.py:147
  211.4 934.4 %all-gather.30.cloned.1.call-start = ((), (), s32[]{:S(2)}) async-start(), calls=%async_computation.16 | async-start | bytes 17301504 | tf_op jit(solution)/shard_map/all_gather | solution.py:211
  212.3 933.5 %all-gather.32.cloned.1.call-start = ((), (), s32[]{:S(2)}) async-start(), calls=%async_computation.17 | async-start | bytes 17301504 | tf_op jit(solution)/shard_map/all_gather | solution.py:212
  804.6 573.4 %reduce-scatter.14.cloned.1.call-start = ((), (), s32[]{:S(2)}) async-start(), calls=%async_computation.21 | async-start | bytes 6291456 | tf_op jit(solution)/shard_map/reduce_scatter | solution.py:283
  808.9 569.2 %reduce-scatter.20.cloned.1.call-start = ((), (), s32[]{:S(2)}) async-start(), calls=%async_computation.24 | async-start | bytes 12582912 | tf_op jit(solution)/shard_map/reduce_scatter | solution.py:292
  815.6 562.5 %reduce-scatter.16.cloned.1.call-start = ((), (), s32[]{:S(2)}) async-start(), calls=%async_computation.22 | async-start | bytes 12582912 | tf_op jit(solution)/shard_map/reduce_scatter | solution.py:286
  822.6 601.2 %reduce-scatter.18.cloned.1.call-start = ((), (), s32[]{:S(2)}) async-start(), calls=%async_computation.23 | async-start | bytes 12582912 | tf_op jit(solution)/shard_map/reduce_scatter | solution.py:289
  1145.7 335.3 %reduce-scatter.10.cloned.1.call-start = ((), (), s32[]{:S(2)}) async-start(), calls=%async_computation.19 | async-start | bytes 6291456 | tf_op jit(solution)/shard_map/reduce_scatter | solution.py:277
  1145.8 212.5 %copy-start.27 = (f32[128,64]{0,1:T(8,128)S(1)}, f32[128,64]{0,1:T(8,128)}, u32[]{:S(2)}) copy-start(f32[128,64]{0,1:T(8,128)} %copy-done.26) | copy-start | bytes 98308
  1145.8 212.5 %copy-start.29 = (f32[128,64]{0,1:T(8,128)S(1)}, f32[128,64]{0,1:T(8,128)}, u32[]{:S(2)}) copy-start(f32[128,64]{0,1:T(8,128)} %copy-done.28) | copy-start | bytes 98308
  1365.3 172.9 %reduce-scatter.8.cloned.1.call-start = ((), (), s32[]{:S(2)}) async-start(), calls=%async_computation.18 | async-start | bytes 6291456 | tf_op jit(solution)/shard_map/reduce_scatter | solution.py:274
  1370.9 224.4 %reduce-scatter.12.cloned.1.call-start = ((), (), s32[]{:S(2)}) async-start(), calls=%async_computation.20 | async-start | bytes 6291456 | tf_op jit(solution)/shard_map/reduce_scatter | solution.py:280
  1437.9 157.4 %copy-start.22 = (bf16[1024,1024]{1,0:T(8,128)(2,1)S(1)}, bf16[1024,1024]{1,0:T(8,128)(2,1)}, u32[]{:S(2)}) copy-start(bf16[1024,1024]{1,0:T(8,128)(2,1)} %reduce-scatter.14.cloned.1.call-done) | copy-start | bytes 6291460
  (49 other events, 654.7 us)
Sparse Core Ops, SparseCore 0:
  11.0 64.4 all-gather.17
  78.5 60.6 all-gather.11
  142.2 60.5 all-gather.15
  205.6 113.1 all-gather.19
  322.0 144.9 all-gather.13
  469.9 59.8 all-gather.21
  532.8 75.8 all-gather.23
  611.7 75.6 all-gather.25
  690.5 75.7 all-gather.27
  769.0 171.5 all-gather.29
  943.6 118.3 all-gather.31
  1064.7 52.6 reduce-scatter.13
  1120.3 99.3 reduce-scatter.19
  1222.4 99.3 reduce-scatter.15
  1324.4 99.3 reduce-scatter.17
  1426.5 54.4 reduce-scatter.9
  1483.7 54.3 reduce-scatter.7
  1540.9 54.3 reduce-scatter.11
where the time goes:
time: 2510 us; the launch traced here: 2480 us
  blocking collectives  1090 us (43%)
  waiting for transfers between devices  750 us (30%)
  matrix products  346 us (14%)
  local copies, waits for them, and re-layouts  217 us (9%)
  other arithmetic  40.2 us (2%)
    psum x1, blocking collectives, per_device(): lax.psum((share_wq, share_wk, share_wv, share_wo, share_wg, share_wu, sha...  860 us
    all_gather x1, waiting for transfers between devices, per_device(): keys_in = lax.all_gather(key, ('ctx', 'fsdp'), axis=0, tiled=True)  128 us
    all_gather x1, blocking collectives, per_device(): lax.all_gather(delta_rows, ('ctx', 'fsdp'), axis=0, tiled=True)  112 us
    all_gather x1, waiting for transfers between devices, per_device(): values_in = lax.all_gather(value, ('ctx', 'fsdp'), axis=0, tiled=True)  105 us
    all_gather x1, waiting for transfers between devices, per_device(): lax.all_gather(w_up, ('ctx', 'fsdp'), axis=0, tiled=True)  72.8 us
    all_gather x1, blocking collectives, per_device(): lax.all_gather(lse.T, ('ctx', 'fsdp'), axis=0, tiled=True)  72.3 us
    all_gather x1, waiting for transfers between devices, per_device(): lax.all_gather(w_down, ('ctx', 'fsdp'), axis=0, tiled=True)  71.9 us
    all_gather x1, waiting for transfers between devices, per_device(): lax.all_gather(w_value, ('ctx', 'fsdp'), axis=0, tiled=True)  64.9 us
  transfers between devices with their start and end apart: 18, of which 12 were waited for; matrix products, arithmetic and copies ran while one was open for 23% of the time, Pallas kernels for 0%

commit v1 on v0

v1 whole, which is shorter than its diff:
```python
import functools
import math

import jax
import jax.numpy as jnp
from jax import lax
from jax.experimental import pallas as pl
from jax.experimental.pallas import tpu as pltpu
from jax.sharding import Mesh
from jax.sharding import PartitionSpec as P

NEG = -1e30


def dot(a, b, ca, cb):
    return lax.dot_general(a, b, (((ca,), (cb,)), ((), ())), preferred_element_type=jnp.float32)


def query_positions(seq_ref, tile, per, blk):
    lane = lax.broadcasted_iota(jnp.int32, (1, per * blk), 1)
    out = jnp.zeros((1, per * blk), jnp.int32)
    for b in range(per):
        first = seq_ref[tile * per + b] * blk
        out = jnp.where(lane // blk == b, first + lane - b * blk, out)
    return out


def sorted_load(src, dst, sem, count, blk, slot):
    def start(i, carry):
        pltpu.make_async_copy(
            src.at[pl.ds(pl.multiple_of(i * blk, blk), blk), :],
            dst.at[pl.ds(pl.multiple_of(slot(i) * blk, blk), blk), :],
            sem,
        ).start()
        return carry

    lax.fori_loop(0, count, start, 0)


def attend_kernel(
    place_ref, seq_ref, kslot_ref, q_ref, kv_ref, o_ref, lse_ref, q_s, kv_s, o_s, sems,
    *, heads, head_size, blk, per, chunk, scale
):
    nq = q_s.shape[0] // blk
    nk = kv_s.shape[0] // blk
    width = heads * head_size
    rows = per * blk
    sorted_load(q_ref, q_s, sems.at[0], nq, blk, lambda i: place_ref[i])
    sorted_load(kv_ref, kv_s, sems.at[1], nk, blk, lambda i: kslot_ref[i])
    pltpu.make_async_copy(q_ref, q_s, sems.at[0]).wait()
    pltpu.make_async_copy(kv_ref, kv_s, sems.at[1]).wait()

    def tile_body(tile, carry):
        base = pl.multiple_of(tile * rows, rows)
        qpos = query_positions(seq_ref, tile, per, blk)
        full = (seq_ref[tile * per] * blk) // chunk
        last = ((seq_ref[tile * per + per - 1] + 1) * blk + chunk - 1) // chunk
        for h in range(heads):
            cols = pl.ds(h * head_size, head_size)
            vcols = pl.ds(width + h * head_size, head_size)
            qt = q_s[pl.ds(base, rows), cols]

            def step(j, state, masked):
                top, total, acc = state
                low = pl.multiple_of(j * chunk, chunk)
                s = dot(kv_s[pl.ds(low, chunk), cols], qt, 1, 1) * scale
                if masked:
                    kpos = low + lax.broadcasted_iota(jnp.int32, s.shape, 0)
                    s = jnp.where(kpos <= qpos, s, NEG)
                top_new = jnp.maximum(top, jnp.max(s, axis=0, keepdims=True))
                p = jnp.exp(s - top_new)
                factor = jnp.exp(top - top_new)
                total = total * factor + jnp.sum(p, axis=0, keepdims=True)
                acc = acc * factor + dot(kv_s[pl.ds(low, chunk), vcols], p.astype(jnp.bfloat16), 0, 0)
                return top_new, total, acc

            state = (
                jnp.full((1, rows), NEG, jnp.float32),
                jnp.zeros((1, rows), jnp.float32),
                jnp.zeros((head_size, rows), jnp.float32),
            )
            state = lax.fori_loop(0, full, functools.partial(step, masked=False), state)
            top, total, acc = lax.fori_loop(full, last, functools.partial(step, masked=True), state)
            o_s[pl.ds(base, rows), cols] = (acc / total).T.astype(o_s.dtype)
            lse_ref[pl.ds(tile * heads + h, 1), :] = top + jnp.log(total)
        return carry

    lax.fori_loop(0, nq // per, tile_body, 0)

    def put(i, carry):
        pltpu.make_async_copy(
            o_s.at[pl.ds(pl.multiple_of(place_ref[i] * blk, blk), blk), :],
            o_ref.at[pl.ds(pl.multiple_of(i * blk, blk), blk), :],
            sems.at[0],
        ).start()
        return carry

    lax.fori_loop(0, nq, put, 0)
    pltpu.make_async_copy(o_s, o_ref, sems.at[0]).wait()


def attend(place, seq, kslot, q, kv, heads, head_size, blk):
    nq = q.shape[0] // blk
    per = min(4, nq)
    chunk = 512
    rows = per * blk
    width = heads * head_size
    scale = 1.0 / math.sqrt(head_size)
    return pl.pallas_call(
        functools.partial(
            attend_kernel, heads=heads, head_size=head_size, blk=blk, per=per, chunk=chunk, scale=scale
        ),
        out_shape=(
            jax.ShapeDtypeStruct(q.shape, q.dtype),
            jax.ShapeDtypeStruct((nq // per * heads, rows), jnp.float32),
        ),
        grid_spec=pltpu.PrefetchScalarGridSpec(
            num_scalar_prefetch=3,
            grid=(),
            in_specs=[pl.BlockSpec(memory_space=pl.ANY)] * 2,
            out_specs=[pl.BlockSpec(memory_space=pl.ANY), pl.BlockSpec(memory_space=pltpu.VMEM)],
            scratch_shapes=[
                pltpu.VMEM(q.shape, q.dtype),
                pltpu.VMEM(kv.shape, kv.dtype),
                pltpu.VMEM(q.shape, q.dtype),
                pltpu.SemaphoreType.DMA((2,)),
            ],
        ),
        compiler_params=pltpu.CompilerParams(vmem_limit_bytes=56 * 1024 * 1024),
        name="attend",
    )(place, seq, kslot, q, kv)


def attend_back_kernel(
    place_ref, seq_ref, kslot_ref, q_ref, kv_ref, o_ref, do_ref, lse_ref,
    dq_ref, dkv_ref, q_s, kv_s, o_s, do_s, dq_s, dkv_s, sems,
    *, heads, head_size, blk, per, chunk, scale
):
    nq = q_s.shape[0] // blk
    nk = kv_s.shape[0] // blk
    width = heads * head_size
    rows = per * blk
    sorted_load(q_ref, q_s, sems.at[0], nq, blk, lambda i: place_ref[i])
    sorted_load(o_ref, o_s, sems.at[1], nq, blk, lambda i: place_ref[i])
    sorted_load(do_ref, do_s, sems.at[2], nq, blk, lambda i: place_ref[i])
    sorted_load(kv_ref, kv_s, sems.at[3], nk, blk, lambda i: kslot_ref[i])
    dkv_s[...] = jnp.zeros_like(dkv_s)
    pltpu.make_async_copy(q_ref, q_s, sems.at[0]).wait()
    pltpu.make_async_copy(o_ref, o_s, sems.at[1]).wait()
    pltpu.make_async_copy(do_ref, do_s, sems.at[2]).wait()
    pltpu.make_async_copy(kv_ref, kv_s, sems.at[3]).wait()

    def tile_body(tile, carry):
        base = pl.multiple_of(tile * rows, rows)
        qpos = query_positions(seq_ref, tile, per, blk)
        full = (seq_ref[tile * per] * blk) // chunk
        last = ((seq_ref[tile * per + per - 1] + 1) * blk + chunk - 1) // chunk
        for h in range(heads):
            cols = pl.ds(h * head_size, head_size)
            vcols = pl.ds(width + h * head_size, head_size)
            qt = q_s[pl.ds(base, rows), cols]
            dot_o = do_s[pl.ds(base, rows), cols]
            prod = dot_o.astype(jnp.float32) * o_s[pl.ds(base, rows), cols].astype(jnp.float32)
            delta = jnp.sum(prod.T, axis=0, keepdims=True)
            lse = lse_ref[pl.ds(tile * heads + h, 1), :]

            def step(j, acc, masked):
                low = pl.multiple_of(j * chunk, chunk)
                krows = pl.ds(low, chunk)
                kc = kv_s[krows, cols]
                s = dot(kc, qt, 1, 1) * scale - lse
                if masked:
                    kpos = low + lax.broadcasted_iota(jnp.int32, s.shape, 0)
                    s = jnp.where(kpos <= qpos, s, NEG)
                p = jnp.exp(s)
                dp = dot(kv_s[krows, vcols], dot_o, 1, 1)
                ds = (p * (dp - delta)).astype(jnp.bfloat16)
                dkv_s[krows, vcols] += dot(p.astype(jnp.bfloat16), dot_o, 1, 0)
                dkv_s[krows, cols] += dot(ds, qt, 1, 0)
                return acc + dot(kc, ds, 0, 0)

            acc = jnp.zeros((head_size, rows), jnp.float32)
            acc = lax.fori_loop(0, full, functools.partial(step, masked=False), acc)
            acc = lax.fori_loop(full, last, functools.partial(step, masked=True), acc)
            dq_s[pl.ds(base, rows), cols] = (acc * scale).T.astype(dq_s.dtype)
        return carry

    lax.fori_loop(0, nq // per, tile_body, 0)
    kv_s[:, :width] = (dkv_s[:, :width] * scale).astype(kv_s.dtype)
    kv_s[:, width:] = dkv_s[:, width:].astype(kv_s.dtype)

    def put_q(i, carry):
        pltpu.make_async_copy(
            dq_s.at[pl.ds(pl.multiple_of(place_ref[i] * blk, blk), blk), :],
            dq_ref.at[pl.ds(pl.multiple_of(i * blk, blk), blk), :],
            sems.at[0],
        ).start()
        return carry

    def put_k(i, carry):
        pltpu.make_async_copy(
            kv_s.at[pl.ds(pl.multiple_of(kslot_ref[i] * blk, blk), blk), :],
            dkv_ref.at[pl.ds(pl.multiple_of(i * blk, blk), blk), :],
            sems.at[3],
        ).start()
        return carry

    lax.fori_loop(0, nq, put_q, 0)
    lax.fori_loop(0, nk, put_k, 0)
    pltpu.make_async_copy(dq_s, dq_ref, sems.at[0]).wait()
    pltpu.make_async_copy(kv_s, dkv_ref, sems.at[3]).wait()


def attend_back(place, seq, kslot, q, kv, o, do, lse, heads, head_size, blk):
    nq = q.shape[0] // blk
    per = min(4, nq)
    chunk = 512
    scale = 1.0 / math.sqrt(head_size)
    return pl.pallas_call(
        functools.partial(
            attend_back_kernel, heads=heads, head_size=head_size, blk=blk, per=per, chunk=chunk, scale=scale
        ),
        out_shape=(
            jax.ShapeDtypeStruct(q.shape, jnp.float32),
            jax.ShapeDtypeStruct(kv.shape, kv.dtype),
        ),
        grid_spec=pltpu.PrefetchScalarGridSpec(
            num_scalar_prefetch=3,
            grid=(),
            in_specs=[pl.BlockSpec(memory_space=pl.ANY)] * 4 + [pl.BlockSpec(memory_space=pltpu.VMEM)],
            out_specs=[pl.BlockSpec(memory_space=pl.ANY)] * 2,
            scratch_shapes=[
                pltpu.VMEM(q.shape, q.dtype),
                pltpu.VMEM(kv.shape, kv.dtype),
                pltpu.VMEM(q.shape, q.dtype),
                pltpu.VMEM(q.shape, q.dtype),
                pltpu.VMEM(q.shape, jnp.float32),
                pltpu.VMEM(kv.shape, jnp.float32),
                pltpu.SemaphoreType.DMA((4,)),
            ],
        ),
        compiler_params=pltpu.CompilerParams(vmem_limit_bytes=58 * 1024 * 1024),
        name="attend_back",
    )(place, seq, kslot, q, kv, o, do, lse)


EPS = 1e-06
THETA = 500000.0
HD = 128


def norm_forward(value, gain):
    recip = lax.rsqrt(jnp.mean(value * value, axis=-1, keepdims=True) + EPS)
    return (value * recip * gain, recip)


def norm_backward(value, recip, gain, grad_out):
    scaled = grad_out * gain
    width = value.shape[-1]
    grad_in = (
        recip * scaled
        - value * (recip * recip * recip) * jnp.sum(scaled * value, axis=-1, keepdims=True) / width
    )
    grad_gain = jnp.sum(grad_out * value * recip, axis=0)
    return (grad_in, grad_gain)


def turn(flat, cosine, sine, heads):
    half = HD // 2
    table = flat.reshape(flat.shape[0], heads, HD)
    first = table[..., :half]
    second = table[..., half:]
    joined = jnp.concatenate(
        [first * cosine - second * sine, second * cosine + first * sine], axis=-1
    )
    return joined.reshape(flat.shape[0], heads * HD)


def flip(value, *axes):
    last = 2 ** len(axes) - 1
    return lax.ppermute(value, axes, [(i, i ^ last) for i in range(last + 1)])


def gather8(x, a, b):
    mine = jnp.stack([x, flip(x, b), flip(x, a), flip(x, a, b)])
    other = flip(mine, "c")
    return jnp.concatenate([mine, other]).reshape(8 * x.shape[0], x.shape[1])


def scatter8(x, a, b):
    bf16 = jnp.bfloat16
    parts = x.astype(bf16).reshape(2, 4, x.shape[0] // 8, x.shape[1])
    mine = x.reshape(parts.shape)[0] + flip(parts[1], "c").astype(jnp.float32)
    out = mine.astype(bf16)
    return (
        mine[0]
        + flip(out[1], b).astype(jnp.float32)
        + flip(out[2], a).astype(jnp.float32)
        + flip(out[3], a, b).astype(jnp.float32)
    )


def sum8(x, a, b):
    t = x.reshape((2, 2, 2) + x.shape[1:])
    for axis, name in enumerate(("c", a, b)):
        t = t + jnp.flip(flip(t, name), axis)
    return t.reshape(x.shape)


def in_order(value, axis, name):
    return jnp.where(lax.axis_index(name) == 1, jnp.flip(value, axis), value)


def gather4(x, a, b):
    pair = jnp.stack([x, flip(x, a)])
    quad = jnp.stack([pair, flip(pair, b)])
    return in_order(in_order(quad, 1, a), 0, b)


def halve(x, name):
    me = lax.axis_index(name)
    keep = lax.dynamic_index_in_dim(x, me, 0, keepdims=False)
    send = lax.dynamic_index_in_dim(x, 1 - me, 0, keepdims=False)
    return keep.astype(jnp.float32) + flip(send.astype(jnp.bfloat16), name).astype(jnp.float32)


def spread(x, a, b):
    pair = jnp.stack([x, flip(x, a)])
    return jnp.stack([pair, flip(pair, b)])


def collect(x, a, b):
    half = x[0].astype(jnp.float32) + flip(x[1], b).astype(jnp.float32)
    return half[0] + flip(half[1].astype(jnp.bfloat16), a).astype(jnp.float32)


def layer(
    layer_input,
    grad_output,
    positions,
    w_query,
    w_key,
    w_value,
    w_out,
    w_gate,
    w_up,
    w_down,
    gain_query,
    gain_key,
    gain_attn,
    gain_mlp,
    *,
    outer,
):
    f32 = jnp.float32
    bf16 = jnp.bfloat16
    rows, d = layer_input.shape
    drows, e = w_query.shape
    f = w_gate.shape[1]
    blk = rows // 2
    devices = positions.shape[0] // rows
    teams = devices // 8
    every = ("o", "h", "l", "y", "c", "x")
    heads = e // HD
    mine = heads // 8
    wide = mine * HD
    index = {name: lax.axis_index(name) for name in every}

    aligned = w_out.shape[0] * teams == wide and outer == 1 and (wide // mine) == 2 * w_out.shape[0]
    if aligned:
        def by_team(w):
            return w.reshape(drows, 4, 2, 2, HD).transpose(1, 3, 0, 2, 4).reshape(8, drows, wide)
    else:
        def by_team(w):
            return w.reshape(drows, 8, wide).transpose(1, 0, 2)

    gains = jnp.concatenate([gain_query, gain_key, gain_attn, gain_mlp])
    pad = drows * 128 - gains.shape[0]
    gains = jnp.pad(gains, (0, pad)).reshape(1, drows, 128)
    payload = jnp.concatenate(
        [by_team(w_query), by_team(w_key), by_team(w_value), jnp.broadcast_to(gains, (8, drows, 128))],
        axis=2,
    )
    payload = lax.all_to_all(payload, ("h", "l", "c"), 0, 0, tiled=True)
    payload = gather4(payload, "y", "x")
    if outer > 1:
        payload = lax.all_gather(payload, "o", axis=0)
    else:
        payload = payload[None]
    payload = payload.reshape(outer, 2, 2, 2, 2, 2, drows, 3 * wide + 128)
    payload = payload.transpose(0, 3, 4, 2, 5, 1, 6, 7).reshape(d, 3 * wide + 128)
    w_qkv = payload[:, : 3 * wide]
    gains = payload[:, 3 * wide :].reshape(devices, drows * 128)
    e_own, d_own = e // devices, d // devices
    full_gq = gains[:, :e_own].reshape(e)
    full_gk = gains[:, e_own : 2 * e_own].reshape(e)
    full_ga = gains[:, 2 * e_own : 2 * e_own + d_own].reshape(1, d).astype(f32)
    full_gm = gains[:, 2 * e_own + d_own : 2 * e_own + 2 * d_own].reshape(1, d).astype(f32)
    team_a = index["h"] * 4 + index["l"] * 2 + index["c"]
    if aligned:
        def own_gain(g):
            t = g.reshape(4, 2, 2, HD).transpose(0, 2, 1, 3).reshape(8, wide)
            return lax.dynamic_slice_in_dim(t, team_a, 1, 0).astype(f32)
    else:
        def own_gain(g):
            return lax.dynamic_slice_in_dim(g.reshape(8, wide), team_a, 1, 0).astype(f32)
    gq, gk = own_gain(full_gq), own_gain(full_gk)

    if aligned:
        w_o = gather4(w_out, "x", "y").reshape(wide, d)
    else:
        w_o = lax.all_gather(w_out, every, axis=0, tiled=True)
        w_o = lax.dynamic_slice_in_dim(w_o, team_a * wide, wide, 0)

    unit = f // (8 * outer * 2)
    units = outer * 2 * unit

    def by_unit(w):
        return w.reshape(drows, outer * 2, 8, unit).transpose(2, 0, 1, 3).reshape(8, drows, units)

    ff = jnp.concatenate([by_unit(w_gate), by_unit(w_up)], axis=2)
    ff = lax.all_to_all(ff, ("l", "y", "c"), 0, 0, tiled=True)
    ff = gather4(ff, "h", "x")
    w_d = gather4(w_down, "h", "x")
    if outer > 1:
        ff = lax.all_gather(ff, "o", axis=0)
        w_d = lax.all_gather(w_d, "o", axis=0)
    else:
        ff, w_d = ff[None], w_d[None]
    ff = ff.reshape(outer, 2, 2, 2, 2, 2, drows, 2 * units)
    w_gu = ff.transpose(0, 2, 3, 4, 5, 1, 6, 7).reshape(d, 2 * units)
    w_d = w_d.transpose(0, 2, 1, 3, 4).reshape(units, d)

    table = positions.reshape(outer, 2, 2, 2, 2, 2, rows)[..., ::blk] // blk
    for axis, name in enumerate(every):
        if name != "o":
            table = in_order(table, axis, name)
    kslot = table.transpose(0, 5, 3, 4, 1, 2, 6)
    qblocks = lax.dynamic_index_in_dim(kslot, index["o"], 0, keepdims=False)[0, 0].reshape(-1)
    kslot = kslot.reshape(-1)
    nq = qblocks.shape[0]
    place = jnp.sum((qblocks[None, :] < qblocks[:, None]).astype(jnp.int32), axis=1)
    seq = jnp.sum(
        jnp.where(place[None, :] == jnp.arange(nq)[:, None], qblocks[None, :], 0), axis=1
    ).astype(jnp.int32)
    group_pos = (qblocks[:, None] * blk + jnp.arange(blk, dtype=jnp.int32)[None, :]).reshape(-1)
    freqs = THETA ** (-(2.0 * jnp.arange(HD // 2, dtype=f32)) / HD)
    angles = group_pos.astype(f32)[:, None] * freqs[None, :]
    cosine, sine = jnp.cos(angles)[:, None, :], jnp.sin(angles)[:, None, :]

    xg = gather8(layer_input.astype(bf16), "h", "l")
    group = xg.shape[0]
    pre = jnp.dot(xg, w_qkv, preferred_element_type=f32)
    q_pre, k_pre, value = pre[:, :wide], pre[:, wide : 2 * wide], pre[:, 2 * wide :].astype(bf16)
    squares = jnp.stack([jnp.sum(q_pre * q_pre, axis=-1), jnp.sum(k_pre * k_pre, axis=-1)])
    squares = sum8(squares.reshape(2, 8, rows).transpose(1, 0, 2), "h", "l")
    recip = lax.rsqrt(squares.transpose(1, 0, 2).reshape(2, group, 1) / e + EPS)
    q_recip, k_recip = recip[0], recip[1]
    query = turn(q_pre * q_recip * gq, cosine, sine, mine).astype(bf16)
    key = turn(k_pre * k_recip * gk, cosine, sine, mine).astype(bf16)
    keys = spread(key, "y", "x")
    values = spread(value, "x", "y").transpose(1, 0, 2, 3)
    kv = jnp.concatenate([keys, values], axis=-1)
    if outer > 1:
        kv = lax.all_gather(kv, "o", axis=0)
    kv = kv.reshape(-1, 2 * wide)
    attended, lse = attend(place, seq, kslot, query, kv, mine, HD, blk)
    proj = scatter8(jnp.dot(attended, w_o, preferred_element_type=f32), "h", "l")
    attn_branch, a_recip = norm_forward(proj, full_ga)
    mid = layer_input + attn_branch

    mg = gather8(mid.astype(bf16), "l", "y")
    gate_up = jnp.dot(mg, w_gu, preferred_element_type=f32)
    gate, up = gate_up[:, :units], gate_up[:, units:]
    sig = jax.nn.sigmoid(gate)
    silu = gate * sig
    hidden = (silu * up).astype(bf16)
    down = scatter8(jnp.dot(hidden, w_d, preferred_element_type=f32), "l", "y")
    mlp_branch, m_recip = norm_forward(down, full_gm)
    output = mid + mlp_branch
    d_down_f, local_gm = norm_backward(down, m_recip, full_gm, grad_output)
    dg = gather8(d_down_f.astype(bf16), "l", "y")
    d_hidden = lax.dot_general(dg, w_d, (((1,), (1,)), ((), ())), preferred_element_type=f32)
    d_gate = (d_hidden * up * sig * (1.0 + gate * (1.0 - sig))).astype(bf16)
    d_up = (d_hidden * silu).astype(bf16)
    d_gu = jnp.concatenate([d_gate, d_up], axis=1)
    d_mid = grad_output + scatter8(
        lax.dot_general(d_gu, w_gu, (((1,), (1,)), ((), ())), preferred_element_type=f32), "l", "y"
    )
    local_wd = lax.dot_general(hidden, dg, (((0,), (0,)), ((), ())), preferred_element_type=f32)
    local_wgu = lax.dot_general(mg, d_gu, (((0,), (0,)), ((), ())), preferred_element_type=f32)

    d_proj_f, local_ga = norm_backward(proj, a_recip, full_ga, d_mid)
    pg = gather8(d_proj_f.astype(bf16), "h", "l")
    d_att = lax.dot_general(pg, w_o, (((1,), (1,)), ((), ())), preferred_element_type=f32).astype(bf16)
    local_wo = lax.dot_general(attended, pg, (((0,), (0,)), ((), ())), preferred_element_type=f32)
    dq_rot, dkv = attend_back(place, seq, kslot, query, kv, attended, d_att, lse, mine, HD, blk)
    if outer > 1:
        dkv = lax.psum_scatter(
            dkv.reshape(outer, 2, 2, group, 2 * wide), "o", scatter_dimension=0, tiled=False
        )
    else:
        dkv = dkv.reshape(2, 2, group, 2 * wide)
    dk_rot = collect(dkv[..., :wide], "y", "x")
    d_value = collect(dkv[..., wide:].transpose(1, 0, 2, 3), "x", "y").astype(bf16)
    dq_n = turn(dq_rot, cosine, -sine, mine)
    dk_n = turn(dk_rot, cosine, -sine, mine)
    local_gq = jnp.sum(dq_n * q_pre * q_recip, axis=0)
    local_gk = jnp.sum(dk_n * k_pre * k_recip, axis=0)
    dq_s, dk_s = dq_n * gq, dk_n * gk
    sums = jnp.stack([jnp.sum(dq_s * q_pre, axis=-1), jnp.sum(dk_s * k_pre, axis=-1)])
    sums = sum8(sums.reshape(2, 8, rows).transpose(1, 0, 2), "h", "l").transpose(1, 0, 2)
    sums = sums.reshape(2, group, 1)
    d_qpre = (q_recip * dq_s - q_pre * (q_recip * q_recip * q_recip) * sums[0] / e).astype(bf16)
    d_kpre = (k_recip * dk_s - k_pre * (k_recip * k_recip * k_recip) * sums[1] / e).astype(bf16)
    d_qkv = jnp.concatenate([d_qpre, d_kpre, d_value], axis=1)
    grad_input = d_mid + scatter8(
        lax.dot_general(d_qkv, w_qkv, (((1,), (1,)), ((), ())), preferred_element_type=f32), "h", "l"
    )
    local_wqkv = lax.dot_general(xg, d_qkv, (((0,), (0,)), ((), ())), preferred_element_type=f32)

    ctx = ("o", "h", "l", "y", "c")

    def settle(local, a, b):
        cols = local.shape[1]
        part = halve(local.reshape(2, -1, cols), b)
        part = halve(part.reshape(2, -1, cols), a)
        if outer > 1:
            part = lax.psum_scatter(
                part.astype(bf16).reshape(outer, -1, cols), "o", scatter_dimension=0, tiled=False
            )
        return part.astype(bf16)

    half_d = d // 2
    got = lax.all_gather(settle(local_wqkv, "y", "x"), ctx, axis=0)
    got = got.reshape(outer, 2, 2, 2, 2, half_d // (2 * outer), 3 * wide)
    got = got.transpose(3, 0, 5, 1, 2, 4, 6).reshape(half_d, 8, 3, wide)

    def by_head(g):
        if aligned:
            g = g.reshape(half_d, 4, 2, 2, HD).transpose(0, 1, 3, 2, 4)
        return g.reshape(half_d, e).astype(f32)

    total_wq, total_wk, total_wv = by_head(got[:, :, 0]), by_head(got[:, :, 1]), by_head(got[:, :, 2])

    got = lax.all_gather(settle(local_wgu, "h", "x"), ctx, axis=0)
    got = got.reshape(outer, 2, 8, half_d // (2 * outer), 2, outer * 2, unit)
    got = got.transpose(4, 1, 0, 3, 5, 2, 6).reshape(2, half_d, f)
    total_wg, total_wu = got[0].astype(f32), got[1].astype(f32)

    got = lax.all_gather(settle(local_wd, "h", "x"), ctx, axis=0)
    half_u = units // 2
    if outer > 1:
        got = got.reshape(outer, 2, 8, half_u // (2 * outer), d).transpose(2, 1, 0, 3, 4)
        got = got.reshape(8, outer, unit, d).transpose(1, 0, 2, 3)
    else:
        got = got.reshape(2, 8, half_u // 2, d).transpose(1, 0, 2, 3)
    total_wd = got.reshape(f // 2, d).astype(f32)

    got = lax.all_gather(settle(local_wo, "y", "x"), every, axis=0)
    got = got.reshape(outer, 2, 2, 2, 2, 2, wide // (4 * outer), d)
    got = got.transpose(1, 2, 4, 5, 3, 0, 6, 7).reshape(4, 2, 2, wide // 2, d)
    if aligned:
        got = got.transpose(0, 2, 1, 3, 4)
    got = got.reshape(2, e // 2, d)
    total_wo = lax.dynamic_index_in_dim(got, index["x"], 0, keepdims=False).astype(f32)

    def own_part(local):
        zero = jnp.zeros((8, wide), f32)
        zero = lax.dynamic_update_slice_in_dim(zero, local.reshape(1, wide), team_a, 0)
        if aligned:
            zero = zero.reshape(4, 2, 2, HD).transpose(0, 2, 1, 3)
        return zero.reshape(-1)

    small = jnp.concatenate([own_part(local_gq), own_part(local_gk), local_ga, local_gm])
    small = lax.psum(small, every)

    def own_half(v):
        return lax.dynamic_index_in_dim(v.reshape(2, -1), index["x"], 0, keepdims=False)

    total_gq = own_half(small[:e])
    total_gk = own_half(small[e : 2 * e])
    total_ga = own_half(small[2 * e : 2 * e + d])
    total_gm = own_half(small[2 * e + d :])
    return (
        output,
        grad_input,
        total_wq,
        total_wk,
        total_wv,
        total_wo,
        total_wg,
        total_wu,
        total_wd,
        total_gq,
        total_gk,
        total_ga,
        total_gm,
    )


def solution(mesh):
    outer = mesh.shape["ctx"] // 16
    names = ("o", "h", "l", "y", "c", "x")
    fine = Mesh(mesh.devices.reshape(outer, 2, 2, 2, 2, 2), names)
    every, half = P(names), P("x")
    in_specs = (every, every, P()) + (every,) * 11
    out_specs = (every, every) + (half,) * 11
    return jax.shard_map(
        functools.partial(layer, outer=outer),
        mesh=fine,
        in_specs=in_specs,
        out_specs=out_specs,
        check_vma=False,
    )
```

time: 2510 us -> 959 us (0.38)
  blocking collectives: 1090 us -> 39.5 us
  waiting for transfers between devices: 750 us -> 386 us
  matrix products: 346 us -> 31 us
  starting transfers between devices: 0.72 us -> 87.3 us
  other arithmetic: 40.2 us -> 110 us
  Pallas kernels: 0 us -> 56.2 us
    psum x1, blocking collectives: 860 us -> 39.5 us  [layer(): small = lax.psum(small, every)]
    all_gather x11 -> x4, waiting for transfers between devices: 545 us -> 0.01 us  [the longest x1 0.01 us: layer(): got = lax.all_gather(settle(local_wd, 'h', 'x'), ctx, axis=0)]
    ppermute x0 -> x62, waiting for transfers between devices: none -> 370 us  [flip(): return lax.ppermute(value, axes, [(i, i ^ last) for i in range(last + 1)])]
    dot_general x77 -> x12, matrix products: 346 us -> 31 us  [the longest x1 5.12 us: layer(): lax.dot_general(dg, w_d, (((1,), (1,)), ((), ())), preferred_element_type...]
    reduce_scatter x7 -> x0, waiting for transfers between devices: 201 us -> none  [the longest x1 57.1 us: per_device(): lax.psum_scatter(local_wv.astype(jnp.bfloat16), 'fsdp', scatter_dimension...]
    all_gather x2 -> x0, blocking collectives: 184 us -> none  [the longest x1 112 us: per_device(): lax.all_gather(delta_rows, ('ctx', 'fsdp'), axis=0, tiled=True)]
    dynamic_slice x88 -> x5, local copies, waits for them, and re-layouts: 155 us -> 2.37 us  [the longest x4 2.36 us: own_half(): lax.dynamic_index_in_dim(v.reshape(2, -1), index['x'], 0, keepdims=False)]
    ppermute x0 -> x62, starting transfers between devices: none -> 77.1 us  [flip(): return lax.ppermute(value, axes, [(i, i ^ last) for i in range(last + 1)])]
  transfers between devices with their start and end apart: 18 -> 68, of which waited for: 12 -> 40; matrix products, arithmetic and copies ran while one was open for 23% -> 27% of each run, Pallas kernels for 0% -> 6%
where the time goes in v1:
time: 959 us; the launch traced here: 942 us
  waiting for transfers between devices  386 us (40%)
  local copies, waits for them, and re-layouts  216 us (23%)
  other arithmetic  110 us (11%)
  starting transfers between devices  87.3 us (9%)
  Pallas kernels  56.2 us (6%)
  blocking collectives  39.5 us (4%)
  matrix products  31 us (3%)
  between operations  15.5 us (2%)
    ppermute x62, waiting for transfers between devices, flip(): return lax.ppermute(value, axes, [(i, i ^ last) for i in range(last + 1)])  370 us
    ppermute x62, starting transfers between devices, flip(): return lax.ppermute(value, axes, [(i, i ^ last) for i in range(last + 1)])  77.1 us
    unnamed x153, local copies, waits for them, and re-layouts  55.3 us
    psum x1, blocking collectives, layer(): small = lax.psum(small, every)  39.5 us
    reshape x2, local copies, waits for them, and re-layouts, layer(): got = got.reshape(outer, 2, 8, half_d // (2 * outer), 2, outer * 2, unit)  30.5 us
    pallas_call x1, Pallas kernels, attend_back(): pl.pallas_call(functools.partial(attend_back_kernel, heads=heads, head_si...  29.1 us
    pallas_call x1, Pallas kernels, attend(): pl.pallas_call(functools.partial(attend_kernel, heads=heads, head_size=he...  27.1 us
  transfers between devices with their start and end apart: 68, of which 40 were waited for; matrix products, arithmetic and copies ran while one was open for 27% of the time, Pallas kernels for 6%

profile of v1, /device:TPU:0, one launch (start us, length us, event | category | flops | bytes accessed | tf_op | source)
XLA Modules:
  0.0 942.4 jit_solution(12429437349096069062)
XLA Ops:
  31.1 16.7 %all-to-all-done = bf16[8,32,896]{2,1,0:T(8,128)(2,1)S(1)} async-done(((bf16[8,32,896]{2,1,0:T(8,128)(2,1)}), bf16[8,32,896]{2,1,0:T(8,128)(2,1)S(1)}, u32[]{:S(2)}, u32[]{:S(2)}) %all-to-all-start) | async-done | bytes 458784 | tf_op jit(solution)/shard_map/all_to_all | solution.py:384
  64.8 15.5 %collective-permute-done.5 = bf16[2,8,32,896]{3,2,1,0:T(8,128)(2,1)S(1)} collective-permute-done((bf16[2,8,32,896]{3,2,1,0:T(8,128)(2,1)S(1)}, bf16[2,8,32,896]{3,2,1,0:T(8,128)(2,1)S(1)}, u32[]{:S(2)}, u32[]{:S(2)}) %collective-permute-start.5) | collective-permute-done | bytes 917536 | tf_op jit(solution)/shard_map/ppermute | solution.py:281
  157.4 27.1 %attend.1 = (bf16[1024,256]{1,0:T(8,128)(2,1)}, f32[8,256]{1,0:T(8,128)}) custom-call(s32[16]{0:T(128)} %copy-done.56, s32[16]{0:T(128)} %select_reduce_fusion.seq_ref, s32[64]{0:T(128)} %reshape.543.kslot_ref, bf16[1024,256]{1,0:T(8,128)(2,1)} %bitcast.454, bf16[4096,512]{1,0:T(8,128)(2,1)} %bitcast.428), custom_call_target="tpu_custom_call" | custom-call | tf_op jit(solution)/shard_map/attend/pallas_call | solution.py:109
  218.5 28.2 %collective-permute-done.23 = bf16[8,32,1024]{2,1,0:T(8,128)(2,1)S(1)} collective-permute-done((bf16[8,32,1024]{2,1,0:T(8,128)(2,1)}, bf16[8,32,1024]{2,1,0:T(8,128)(2,1)S(1)}, u32[]{:S(2)}, u32[]{:S(2)}) %collective-permute-start.23) | collective-permute-done | bytes 524320 | tf_op jit(solution)/shard_map/ppermute | solution.py:281
  263.3 9.4 %collective-permute-done.24 = bf16[2,8,32,1024]{3,2,1,0:T(8,128)(2,1)} collective-permute-done((bf16[2,8,32,1024]{3,2,1,0:T(8,128)(2,1)}, bf16[2,8,32,1024]{3,2,1,0:T(8,128)(2,1)}, u32[]{:S(2)}, u32[]{:S(2)}) %collective-permute-start.24) | collective-permute-done | bytes 1048608 | tf_op jit(solution)/shard_map/ppermute | solution.py:281
  334.6 14.3 %collective-permute-done.60 = bf16[256,1024]{1,0:T(8,128)(2,1)} collective-permute-done((bf16[256,1024]{1,0:T(8,128)(2,1)}, bf16[256,1024]{1,0:T(8,128)(2,1)}, u32[]{:S(2)}, u32[]{:S(2)}) %collective-permute-start.60) | collective-permute-done | bytes 524320 | tf_op jit(solution)/shard_map/ppermute | solution.py:281
  351.5 14.2 %collective-permute-done.61 = bf16[128,1024]{1,0:T(8,128)(2,1)} collective-permute-done((bf16[128,1024]{1,0:T(8,128)(2,1)S(1)}, bf16[128,1024]{1,0:T(8,128)(2,1)}, u32[]{:S(2)}, u32[]{:S(2)}) %collective-permute-start.61) | collective-permute-done | bytes 262176 | tf_op jit(solution)/shard_map/ppermute | solution.py:281
  382.5 10.8 %collective-permute-done.38 = bf16[128,1024]{1,0:T(8,128)(2,1)S(1)} collective-permute-done((bf16[128,1024]{1,0:T(8,128)(2,1)S(1)}, bf16[128,1024]{1,0:T(8,128)(2,1)S(1)}, u32[]{:S(2)}, u32[]{:S(2)}) %collective-permute-start.38) | collective-permute-done | bytes 262176 | tf_op jit(solution)/shard_map/ppermute | solution.py:281
  404.4 20.9 %collective-permute-done.39 = bf16[128,1024]{1,0:T(8,128)(2,1)S(1)} collective-permute-done((bf16[128,1024]{1,0:T(8,128)(2,1)S(1)}, bf16[128,1024]{1,0:T(8,128)(2,1)S(1)}, u32[]{:S(2)}, u32[]{:S(2)}) %collective-permute-start.39) | collective-permute-done | bytes 262176 | tf_op jit(solution)/shard_map/ppermute | solution.py:281
  425.3 9.6 %collective-permute-done.41 = bf16[128,1024]{1,0:T(8,128)(2,1)S(1)} collective-permute-done((bf16[128,1024]{1,0:T(8,128)(2,1)S(1)}, bf16[128,1024]{1,0:T(8,128)(2,1)S(1)}, u32[]{:S(2)}, u32[]{:S(2)}) %collective-permute-start.41) | collective-permute-done | bytes 262176 | tf_op jit(solution)/shard_map/ppermute | solution.py:281
  463.2 29.1 %attend_back.1 = (f32[1024,256]{1,0:T(8,128)}, bf16[4096,512]{1,0:T(8,128)(2,1)}) custom-call(s32[16]{0:T(128)} %copy-done.56, s32[16]{0:T(128)} %select_reduce_fusion.seq_ref, s32[64]{0:T(128)} %reshape.543.kslot_ref, bf16[1024,256]{1,0:T(8,128)(2,1)} %bitcast.455, bf16[4096,512]{1,0:T(8,128)(2,1)} %bitcast.429, bf16[1024,256]{1,0:T(8,128)(2,1)} %get-tuple-element.17.o_ref, ...), custom_call_target="tpu_custom_call" | custom-call | tf_op jit(solution)/shard_map/attend_back/pallas_call | solution.py:219
  506.4 14.9 %collective-permute-done.43 = bf16[2,1024,256]{2,1,0:T(8,128)(2,1)} collective-permute-done((bf16[2,1024,256]{2,1,0:T(8,128)(2,1)}, bf16[2,1024,256]{2,1,0:T(8,128)(2,1)}, u32[]{:S(2)}, u32[]{:S(2)}) %collective-permute-start.43) | collective-permute-done | bytes 1048608 | tf_op jit(solution)/shard_map/ppermute | solution.py:281
  537.8 10.0 %collective-permute-done.44 = bf16[1024,256]{1,0:T(8,128)(2,1)} collective-permute-done((bf16[1024,256]{1,0:T(8,128)(2,1)}, bf16[1024,256]{1,0:T(8,128)(2,1)}, u32[]{:S(2)}, u32[]{:S(2)}) %collective-permute-start.44) | collective-permute-done | bytes 524320 | tf_op jit(solution)/shard_map/ppermute | solution.py:281
  592.4 17.4 %collective-permute-done.54 = bf16[512,768]{1,0:T(8,128)(2,1)S(1)} collective-permute-done((bf16[512,768]{1,0:T(8,128)(2,1)S(1)}, bf16[512,768]{1,0:T(8,128)(2,1)S(1)}, u32[]{:S(2)}, u32[]{:S(2)}) %collective-permute-start.54) | collective-permute-done | bytes 786464 | tf_op jit(solution)/shard_map/ppermute | solution.py:281
  627.7 22.3 %collective-permute-done.58 = bf16[512,1024]{1,0:T(8,128)(2,1)S(1)} collective-permute-done((bf16[512,1024]{1,0:T(8,128)(2,1)S(1)}, bf16[512,1024]{1,0:T(8,128)(2,1)S(1)}, u32[]{:S(2)}, u32[]{:S(2)}) %collective-permute-start.58) | collective-permute-done | bytes 1048608 | tf_op jit(solution)/shard_map/ppermute | solution.py:281
  659.9 45.5 %collective-permute-done.59 = bf16[256,1024]{1,0:T(8,128)(2,1)S(1)} collective-permute-done((bf16[256,1024]{1,0:T(8,128)(2,1)S(1)}, bf16[256,1024]{1,0:T(8,128)(2,1)S(1)}, u32[]{:S(2)}, u32[]{:S(2)}) %collective-permute-start.59) | collective-permute-done | bytes 524320 | tf_op jit(solution)/shard_map/ppermute | solution.py:281
  710.6 39.5 %psum.7 = f32[6144]{0:T(1024)S(1)} all-reduce(f32[6144]{0:T(1024)S(1)} %pad_maximum_fusion.26), channel_id=1, replica_groups=mesh['o'=1,'h'=2,'l'=2,'y'=2,'c'=2,'x'=2] {'o','h','l','y','c','x'}, use_global_device_ids=true, to_apply=%region_14.15 | all-reduce | flops 6144 | bytes 49152 | tf_op jit(solution)/shard_map/psum | solution.py:576
  761.5 10.6 %collective-permute-done.53 = bf16[128,1024]{1,0:T(8,128)(2,1)S(1)} collective-permute-done((bf16[128,1024]{1,0:T(8,128)(2,1)}, bf16[128,1024]{1,0:T(8,128)(2,1)S(1)}, u32[]{:S(2)}, u32[]{:S(2)}) %collective-permute-start.53) | collective-permute-done | bytes 262176 | tf_op jit(solution)/shard_map/ppermute | solution.py:281
  772.2 30.2 %collective-permute-done.52 = bf16[128,1024]{1,0:T(8,128)(2,1)S(1)} collective-permute-done((bf16[128,1024]{1,0:T(8,128)(2,1)}, bf16[128,1024]{1,0:T(8,128)(2,1)S(1)}, u32[]{:S(2)}, u32[]{:S(2)}) %collective-permute-start.52) | collective-permute-done | bytes 262176 | tf_op jit(solution)/shard_map/ppermute | solution.py:281
  815.2 16.2 %copy.140 = bf16[2,1,256,2,2,2,768]{2,0,6,5,4,3,1:T(2,128)(2,1)} copy(bf16[2,1,256,2,2,2,768]{6,2,5,0,4,3,1:T(8,128)(2,1)} %bitcast.450) | data formatting | bytes 12582912 | tf_op jit(solution)/shard_map/transpose | solution.py:537
  831.3 10.8 %reshape.578 = bf16[512,8,3,256]{0,3,2,1:T(8,128)(2,1)} reshape(bf16[2,1,256,2,2,2,768]{2,0,6,5,4,3,1:T(2,128)(2,1)} %copy.140) | data formatting | bytes 12582912 | tf_op jit(solution)/shard_map/reshape | solution.py:537
  874.4 14.6 %reshape.584 = bf16[1,2,8,256,2,2,256]{6,5,4,3,2,1,0:T(2,128)(2,1)} reshape(bf16[4096,1024]{1,0:T(8,128)(2,1)} %all-gather.13.cloned.1.call-done) | data formatting | bytes 16777216 | tf_op jit(solution)/shard_map/reshape | solution.py:547
  889.0 15.9 %copy.181 = bf16[1,2,8,256,2,2,256]{6,2,5,3,1,0,4:T(8,128)(2,1)} copy(bf16[1,2,8,256,2,2,256]{6,5,4,3,2,1,0:T(2,128)(2,1)} %reshape.584) | data formatting | bytes 16777216 | tf_op jit(solution)/shard_map/reshape | solution.py:547
  904.9 12.0 %slice_convert_fusion = (f32[1,2,1,256,2,8,256]{6,5,4,3,1,2,0:T(8,128)}, f32[1,2,1,256,2,8,256]{6,5,4,3,1,2,0:T(8,128)}) fusion(bf16[2,2,1,256,2,8,256]{6,5,4,3,1,2,0:T(8,128)(2,1)} %bitcast.430), kind=kLoop, calls=%fused_computation.1 | loop fusion | flops 4194304 | bytes 25165824 | tf_op jit(solution)/shard_map/convert_element_type | solution.py:549
  (489 shorter events, 471.0 us)
Async XLA Ops:
  9.1 43.5 %collective-permute-start = (bf16[128,1024]{1,0:T(8,128)(2,1)}, bf16[128,1024]{1,0:T(8,128)(2,1)S(1)}, u32[]{:S(2)}, u32[]{:S(2)}) collective-permute-start(bf16[128,1024]{1,0:T(8,128)(2,1)} %get-tuple-element.79), channel_id=1, source_target_pairs={{0,8},{8,0},{1,9},{9,1},{2,10},{10,2},{3,11},{11,3},{4,12},{12,4},... | collective-permute-start | bytes 786440 | tf_op jit(solution)/shard_map/ppermute | solution.py:281
  12.2 40.7 %collective-permute-start.1 = (bf16[128,1024]{1,0:T(8,128)(2,1)}, bf16[128,1024]{1,0:T(8,128)(2,1)S(1)}, u32[]{:S(2)}, u32[]{:S(2)}) collective-permute-start(bf16[128,1024]{1,0:T(8,128)(2,1)} %get-tuple-element.79), channel_id=1, source_target_pairs={{0,16},{16,0},{1,17},{17,1},{2,18},{18,2},{3,19},{19,3},{4,20},{20... | collective-permute-start | bytes 786440 | tf_op jit(solution)/shard_map/ppermute | solution.py:281
  14.8 38.2 %collective-permute-start.2 = (bf16[128,1024]{1,0:T(8,128)(2,1)}, bf16[128,1024]{1,0:T(8,128)(2,1)}, u32[]{:S(2)}, u32[]{:S(2)}) collective-permute-start(bf16[128,1024]{1,0:T(8,128)(2,1)} %get-tuple-element.79), channel_id=1, source_target_pairs={{0,24},{8,16},{16,8},{24,0},{1,25},{9,17},{17,9},{25,1},{2,26},{10... | collective-permute-start | bytes 786440 | tf_op jit(solution)/shard_map/ppermute | solution.py:281
  18.3 29.6 %all-to-all-start = ((bf16[8,32,896]{2,1,0:T(8,128)(2,1)}), bf16[8,32,896]{2,1,0:T(8,128)(2,1)S(1)}, u32[]{:S(2)}, u32[]{:S(2)}) async-start(bf16[8,32,896]{2,1,0:T(8,128)(2,1)} %pad_maximum_fusion.24), calls=%async_computation | async-start | bytes 917504 | tf_op jit(solution)/shard_map/all_to_all | solution.py:384
  23.4 37.8 %collective-permute-start.13 = (bf16[64,1024]{1,0:T(8,128)(2,1)S(1)}, bf16[64,1024]{1,0:T(8,128)(2,1)}, u32[]{:S(2)}, u32[]{:S(2)}) collective-permute-start(bf16[64,1024]{1,0:T(8,128)(2,1)S(1)} %copy-done.54), channel_id=1, source_target_pairs={{0,1},{1,0},{2,3},{3,2},{4,5},{5,4},{6,7},{7,6},{8,9},{9,8},{10,11... | collective-permute-start | bytes 393224 | tf_op jit(solution)/shard_map/ppermute | solution.py:281
  52.6 136.9 %collective-permute-start.25 = (bf16[128,1024]{1,0:T(8,128)(2,1)}, bf16[128,1024]{1,0:T(8,128)(2,1)}, u32[]{:S(2)}, u32[]{:S(2)}) collective-permute-start(bf16[128,1024]{1,0:T(8,128)(2,1)} %param.23), channel_id=1, source_target_pairs={{0,16},{16,0},{1,17},{17,1},{2,18},{18,2},{3,19},{19,3},{4,20},{20... | collective-permute-start | bytes 786440 | tf_op jit(solution)/shard_map/ppermute | solution.py:281
  114.5 30.5 %collective-permute-start.12 = (bf16[2,1024,256]{1,2,0:T(8,128)(2,1)}, bf16[2,1024,256]{1,2,0:T(8,128)(2,1)}, u32[]{:S(2)}, u32[]{:S(2)}) collective-permute-start(bf16[2,1024,256]{1,2,0:T(8,128)(2,1)} %get-tuple-element.120), channel_id=1, source_target_pairs={{0,4},{4,0},{1,5},{5,1},{2,6},{6,2},{3,7},{7,3},{8,12},{12,8},{9,1... | collective-permute-start | bytes 3145736 | tf_op jit(solution)/shard_map/ppermute | solution.py:281
  196.7 606.7 %all-gather.15.cloned.1.call-start = ((), (), s32[]{:S(2)}) async-start(), calls=%async_computation.5 | async-start | bytes 4456448 | tf_op jit(solution)/shard_map/all_gather | solution.py:551
  208.6 38.1 %collective-permute-start.23 = (bf16[8,32,1024]{2,1,0:T(8,128)(2,1)}, bf16[8,32,1024]{2,1,0:T(8,128)(2,1)S(1)}, u32[]{:S(2)}, u32[]{:S(2)}) collective-permute-start(bf16[8,32,1024]{2,1,0:T(8,128)(2,1)} %all-to-all-done.1), channel_id=1, source_target_pairs={{0,16},{16,0},{1,17},{17,1},{2,18},{18,2},{3,19},{19,3},{4,20},{20... | collective-permute-start | bytes 1572872 | tf_op jit(solution)/shard_map/ppermute | solution.py:281
  214.1 36.3 %collective-permute-start.18 = (bf16[128,1024]{1,0:T(8,128)(2,1)}, bf16[128,1024]{1,0:T(8,128)(2,1)S(1)}, u32[]{:S(2)}, u32[]{:S(2)}) collective-permute-start(bf16[128,1024]{1,0:T(8,128)(2,1)} %get-tuple-element.113), channel_id=1, source_target_pairs={{0,24},{8,16},{16,8},{24,0},{1,25},{9,17},{17,9},{25,1},{2,26},{10... | collective-permute-start | bytes 786440 | tf_op jit(solution)/shard_map/ppermute | solution.py:281
  216.3 40.7 %collective-permute-start.17 = (bf16[128,1024]{1,0:T(8,128)(2,1)}, bf16[128,1024]{1,0:T(8,128)(2,1)}, u32[]{:S(2)}, u32[]{:S(2)}) collective-permute-start(bf16[128,1024]{1,0:T(8,128)(2,1)} %get-tuple-element.114), channel_id=1, source_target_pairs={{0,16},{16,0},{1,17},{17,1},{2,18},{18,2},{3,19},{19,3},{4,20},{20... | collective-permute-start | bytes 786440 | tf_op jit(solution)/shard_map/ppermute | solution.py:281
  217.0 40.1 %collective-permute-start.16 = (bf16[128,1024]{1,0:T(8,128)(2,1)}, bf16[128,1024]{1,0:T(8,128)(2,1)}, u32[]{:S(2)}, u32[]{:S(2)}) collective-permute-start(bf16[128,1024]{1,0:T(8,128)(2,1)} %get-tuple-element.112), channel_id=1, source_target_pairs={{0,8},{8,0},{1,9},{9,1},{2,10},{10,2},{3,11},{11,3},{4,12},{12,4},... | collective-permute-start | bytes 786440 | tf_op jit(solution)/shard_map/ppermute | solution.py:281
  367.6 442.4 %all-gather.11.cloned.1.call-start = ((), (), s32[]{:S(2)}) async-start(), calls=%async_computation.3 | async-start | bytes 4325376 | tf_op jit(solution)/shard_map/all_gather | solution.py:560
  400.0 25.3 %collective-permute-start.39 = (bf16[128,1024]{1,0:T(8,128)(2,1)S(1)}, bf16[128,1024]{1,0:T(8,128)(2,1)S(1)}, u32[]{:S(2)}, u32[]{:S(2)}) collective-permute-start(bf16[128,1024]{1,0:T(8,128)(2,1)S(1)} %get-tuple-element.62), channel_id=1, source_target_pairs={{0,8},{8,0},{1,9},{9,1},{2,10},{10,2},{3,11},{11,3},{4,12},{12,4},... | collective-permute-start | bytes 786440 | tf_op jit(solution)/shard_map/ppermute | solution.py:281
  402.5 32.4 %collective-permute-start.41 = (bf16[128,1024]{1,0:T(8,128)(2,1)S(1)}, bf16[128,1024]{1,0:T(8,128)(2,1)S(1)}, u32[]{:S(2)}, u32[]{:S(2)}) collective-permute-start(bf16[128,1024]{1,0:T(8,128)(2,1)S(1)} %get-tuple-element.62), channel_id=1, source_target_pairs={{0,24},{8,16},{16,8},{24,0},{1,25},{9,17},{17,9},{25,1},{2,26},{10... | collective-permute-start | bytes 786440 | tf_op jit(solution)/shard_map/ppermute | solution.py:281
  458.5 33.9 %collective-permute-start.57 = (bf16[64,1024]{1,0:T(8,128)(2,1)S(1)}, bf16[64,1024]{1,0:T(8,128)(2,1)S(1)}, u32[]{:S(2)}, u32[]{:S(2)}) collective-permute-start(bf16[64,1024]{1,0:T(8,128)(2,1)S(1)} %fusion.45), channel_id=1, source_target_pairs={{0,4},{4,0},{1,5},{5,1},{2,6},{6,2},{3,7},{7,3},{8,12},{12,8},{9,1... | collective-permute-start | bytes 393224 | tf_op jit(solution)/shard_map/ppermute | solution.py:281
  493.1 322.1 %all-gather.9.cloned.1.call-start = ((), (), s32[]{:S(2)}) async-start(), calls=%async_computation.2 | async-start | bytes 6684672 | tf_op jit(solution)/shard_map/all_gather | solution.py:535
  495.6 25.7 %collective-permute-start.43 = (bf16[2,1024,256]{2,1,0:T(8,128)(2,1)}, bf16[2,1024,256]{2,1,0:T(8,128)(2,1)}, u32[]{:S(2)}, u32[]{:S(2)}) collective-permute-start(bf16[2,1024,256]{2,1,0:T(8,128)(2,1)} %slice_bitcast_fusion.4), channel_id=1, source_target_pairs={{0,1},{1,0},{2,3},{3,2},{4,5},{5,4},{6,7},{7,6},{8,9},{9,8},{10,11... | collective-permute-start | bytes 3145736 | tf_op jit(solution)/shard_map/ppermute | solution.py:281
  506.4 28.2 %collective-permute-start.48 = (bf16[2,1024,256]{1,2,0:T(8,128)(2,1)}, bf16[2,1024,256]{1,2,0:T(8,128)(2,1)}, u32[]{:S(2)}, u32[]{:S(2)}) collective-permute-start(bf16[2,1024,256]{1,2,0:T(8,128)(2,1)} %slice_bitcast_fusion.1), channel_id=1, source_target_pairs={{0,4},{4,0},{1,5},{5,1},{2,6},{6,2},{3,7},{7,3},{8,12},{12,8},{9,1... | collective-permute-start | bytes 3145736 | tf_op jit(solution)/shard_map/ppermute | solution.py:281
  620.2 254.2 %all-gather.13.cloned.1.call-start = ((), (), s32[]{:S(2)}) async-start(), calls=%async_computation.4 | async-start | bytes 8912896 | tf_op jit(solution)/shard_map/all_gather | solution.py:546
  650.6 54.8 %collective-permute-start.59 = (bf16[256,1024]{1,0:T(8,128)(2,1)S(1)}, bf16[256,1024]{1,0:T(8,128)(2,1)S(1)}, u32[]{:S(2)}, u32[]{:S(2)}) collective-permute-start(bf16[256,1024]{1,0:T(8,128)(2,1)S(1)} %fusion.21), channel_id=1, source_target_pairs={{0,16},{16,0},{1,17},{17,1},{2,18},{18,2},{3,19},{19,3},{4,20},{20... | collective-permute-start | bytes 1572872 | tf_op jit(solution)/shard_map/ppermute | solution.py:281
  710.4 40.4 %collective-permute-start.50 = (bf16[4,128,1024]{2,1,0:T(8,128)(2,1)S(1)}, bf16[4,128,1024]{2,1,0:T(8,128)(2,1)S(1)}, u32[]{:S(2)}, u32[]{:S(2)}) collective-permute-start(bf16[4,128,1024]{2,1,0:T(8,128)(2,1)S(1)} %bitcast.489), channel_id=1, source_target_pairs={{0,2},{2,0},{1,3},{3,1},{4,6},{6,4},{5,7},{7,5},{8,10},{10,8},{9,1... | collective-permute-start | bytes 3145736 | tf_op jit(solution)/shard_map/ppermute | solution.py:281
  756.9 45.5 %collective-permute-start.52 = (bf16[128,1024]{1,0:T(8,128)(2,1)}, bf16[128,1024]{1,0:T(8,128)(2,1)S(1)}, u32[]{:S(2)}, u32[]{:S(2)}) collective-permute-start(bf16[128,1024]{1,0:T(8,128)(2,1)} %get-tuple-element.101), channel_id=1, source_target_pairs={{0,16},{16,0},{1,17},{17,1},{2,18},{18,2},{3,19},{19,3},{4,20},{20... | collective-permute-start | bytes 786440 | tf_op jit(solution)/shard_map/ppermute | solution.py:281
  759.1 43.3 %collective-permute-start.51 = (bf16[128,1024]{1,0:T(8,128)(2,1)}, bf16[128,1024]{1,0:T(8,128)(2,1)S(1)}, u32[]{:S(2)}, u32[]{:S(2)}) collective-permute-start(bf16[128,1024]{1,0:T(8,128)(2,1)} %get-tuple-element.99), channel_id=1, source_target_pairs={{0,8},{8,0},{1,9},{9,1},{2,10},{10,2},{3,11},{11,3},{4,12},{12,4},... | collective-permute-start | bytes 786440 | tf_op jit(solution)/shard_map/ppermute | solution.py:281
  (110 other events, 1290.8 us)
Sparse Core Ops, SparseCore 0:
  367.7 70.1 all-gather.14
  493.2 69.9 all-gather.10
  620.3 87.0 all-gather.8
  709.4 93.7 all-gather.12

commit v2 on v1

v2 whole, which is shorter than its diff:
```python
import functools
import math

import jax
import jax.numpy as jnp
from jax import lax
from jax.experimental import pallas as pl
from jax.experimental.pallas import tpu as pltpu
from jax.sharding import Mesh
from jax.sharding import PartitionSpec as P

NEG = -1e30


def dot(a, b, ca, cb):
    return lax.dot_general(a, b, (((ca,), (cb,)), ((), ())), preferred_element_type=jnp.float32)


def query_positions(seq_ref, tile, per, blk):
    lane = lax.broadcasted_iota(jnp.int32, (1, per * blk), 1)
    out = jnp.zeros((1, per * blk), jnp.int32)
    for b in range(per):
        first = seq_ref[tile * per + b] * blk
        out = jnp.where(lane // blk == b, first + lane - b * blk, out)
    return out


def sorted_load(src, dst, sem, count, blk, slot):
    def start(i, carry):
        pltpu.make_async_copy(
            src.at[pl.ds(pl.multiple_of(i * blk, blk), blk), :],
            dst.at[pl.ds(pl.multiple_of(slot(i) * blk, blk), blk), :],
            sem,
        ).start()
        return carry

    lax.fori_loop(0, count, start, 0)


def take(srcs, dst, sem, blk, slot):
    base = 0
    for src in srcs:
        sorted_load(src, dst, sem, src.shape[0] // blk, blk, lambda i, base=base: slot(base + i))
        base += src.shape[0] // blk


def finish(dst, sem):
    pltpu.make_async_copy(dst, dst, sem).wait()


def give(src, dsts, sem, blk, slot):
    base = 0
    for dst in dsts:

        def start(i, carry, dst=dst, base=base):
            pltpu.make_async_copy(
                src.at[pl.ds(pl.multiple_of(slot(base + i) * blk, blk), blk), :],
                dst.at[pl.ds(pl.multiple_of(i * blk, blk), blk), :],
                sem,
            ).start()
            return carry

        lax.fori_loop(0, dst.shape[0] // blk, start, 0)
        base += dst.shape[0] // blk


def attend_kernel(place_ref, seq_ref, kslot_ref, *refs, heads, head_size, blk, per, chunk, scale, pieces):
    q_ref, refs = refs[0], refs[1:]
    k_refs, v_refs, refs = refs[:pieces], refs[pieces : 2 * pieces], refs[2 * pieces :]
    o_ref, lse_ref, q_s, k_s, v_s, o_s, sems = refs
    nq = q_s.shape[0] // blk
    rows = per * blk
    take([q_ref], q_s, sems.at[0], blk, lambda i: place_ref[i])
    take(k_refs, k_s, sems.at[1], blk, lambda i: kslot_ref[i])
    take(v_refs, v_s, sems.at[2], blk, lambda i: kslot_ref[i])
    finish(q_s, sems.at[0])
    finish(k_s, sems.at[1])
    finish(v_s, sems.at[2])

    def tile_body(tile, carry):
        base = pl.multiple_of(tile * rows, rows)
        qpos = query_positions(seq_ref, tile, per, blk)
        full = (seq_ref[tile * per] * blk) // chunk
        last = ((seq_ref[tile * per + per - 1] + 1) * blk + chunk - 1) // chunk
        windows = [pl.ds(h * head_size, head_size) for h in range(heads)]
        qts = [q_s[pl.ds(base, rows), w] for w in windows]

        def step(j, states, masked):
            low = pl.multiple_of(j * chunk, chunk)
            krows = pl.ds(low, chunk)
            if masked:
                kpos = low + lax.broadcasted_iota(jnp.int32, (chunk, rows), 0)
                seen = kpos <= qpos
            scores = [dot(k_s[krows, w], qt, 1, 1) * scale for w, qt in zip(windows, qts)]
            out = []
            for w, s, (top, total, acc) in zip(windows, scores, states):
                if masked:
                    s = jnp.where(seen, s, NEG)
                top_new = jnp.maximum(top, jnp.max(s, axis=0, keepdims=True))
                p = jnp.exp(s - top_new)
                factor = jnp.exp(top - top_new)
                total = total * factor + jnp.sum(p, axis=0, keepdims=True)
                acc = acc * factor + dot(v_s[krows, w], p.astype(jnp.bfloat16), 0, 0)
                out.append((top_new, total, acc))
            return tuple(out)

        state = (
            jnp.full((1, rows), NEG, jnp.float32),
            jnp.zeros((1, rows), jnp.float32),
            jnp.zeros((head_size, rows), jnp.float32),
        )
        states = (state,) * heads
        states = lax.fori_loop(0, full, functools.partial(step, masked=False), states)
        states = lax.fori_loop(full, last, functools.partial(step, masked=True), states)
        for h, (top, total, acc) in enumerate(states):
            o_s[pl.ds(base, rows), windows[h]] = (acc / total).T.astype(o_s.dtype)
            lse_ref[pl.ds(tile * heads + h, 1), :] = top + jnp.log(total)
        return carry

    lax.fori_loop(0, nq // per, tile_body, 0)
    give(o_s, [o_ref], sems.at[0], blk, lambda i: place_ref[i])
    finish(o_s, sems.at[0])


ANY = pl.BlockSpec(memory_space=pl.ANY)
WHOLE = pl.BlockSpec(memory_space=pltpu.VMEM)


def attend(place, seq, kslot, q, ks, vs, heads, head_size, blk):
    nq = q.shape[0] // blk
    per = min(4, nq)
    rows = per * blk
    keys = sum(k.shape[0] for k in ks)
    return pl.pallas_call(
        functools.partial(
            attend_kernel, heads=heads, head_size=head_size, blk=blk, per=per, chunk=512,
            scale=1.0 / math.sqrt(head_size), pieces=len(ks),
        ),
        out_shape=(
            jax.ShapeDtypeStruct(q.shape, q.dtype),
            jax.ShapeDtypeStruct((nq // per * heads, rows), jnp.float32),
        ),
        grid_spec=pltpu.PrefetchScalarGridSpec(
            num_scalar_prefetch=3,
            grid=(),
            in_specs=[ANY] * (1 + 2 * len(ks)),
            out_specs=[ANY, WHOLE],
            scratch_shapes=[
                pltpu.VMEM(q.shape, q.dtype),
                pltpu.VMEM((keys, q.shape[1]), q.dtype),
                pltpu.VMEM((keys, q.shape[1]), q.dtype),
                pltpu.VMEM(q.shape, q.dtype),
                pltpu.SemaphoreType.DMA((3,)),
            ],
        ),
        compiler_params=pltpu.CompilerParams(vmem_limit_bytes=58 * 1024 * 1024),
        name="attend",
    )(place, seq, kslot, q, *ks, *vs)


def attend_back_kernel(
    place_ref, seq_ref, kslot_ref, *refs, heads, head_size, blk, per, chunk, scale, pieces
):
    (q_ref, o_ref, do_ref, lse_ref), refs = refs[:4], refs[4:]
    k_refs, v_refs, refs = refs[:pieces], refs[pieces : 2 * pieces], refs[2 * pieces :]
    dq_ref, refs = refs[0], refs[1:]
    dk_refs, dv_refs, refs = refs[:pieces], refs[pieces : 2 * pieces], refs[2 * pieces :]
    q_s, k_s, v_s, o_s, do_s, dq_s, dk_s, dv_s, sems = refs
    nq = q_s.shape[0] // blk
    rows = per * blk
    take([q_ref], q_s, sems.at[0], blk, lambda i: place_ref[i])
    take([o_ref], o_s, sems.at[1], blk, lambda i: place_ref[i])
    take([do_ref], do_s, sems.at[2], blk, lambda i: place_ref[i])
    take(k_refs, k_s, sems.at[3], blk, lambda i: kslot_ref[i])
    take(v_refs, v_s, sems.at[4], blk, lambda i: kslot_ref[i])
    dk_s[...] = jnp.zeros_like(dk_s)
    dv_s[...] = jnp.zeros_like(dv_s)
    finish(q_s, sems.at[0])
    finish(o_s, sems.at[1])
    finish(do_s, sems.at[2])
    finish(k_s, sems.at[3])
    finish(v_s, sems.at[4])

    def tile_body(tile, carry):
        base = pl.multiple_of(tile * rows, rows)
        qpos = query_positions(seq_ref, tile, per, blk)
        full = (seq_ref[tile * per] * blk) // chunk
        last = ((seq_ref[tile * per + per - 1] + 1) * blk + chunk - 1) // chunk
        windows = [pl.ds(h * head_size, head_size) for h in range(heads)]
        qts = [q_s[pl.ds(base, rows), w] for w in windows]
        dos = [do_s[pl.ds(base, rows), w] for w in windows]
        deltas, lses = [], []
        for h, w in enumerate(windows):
            prod = dos[h].astype(jnp.float32) * o_s[pl.ds(base, rows), w].astype(jnp.float32)
            deltas.append(jnp.sum(prod.T, axis=0, keepdims=True))
            lses.append(lse_ref[pl.ds(tile * heads + h, 1), :])

        def step(j, accs, masked):
            low = pl.multiple_of(j * chunk, chunk)
            krows = pl.ds(low, chunk)
            if masked:
                kpos = low + lax.broadcasted_iota(jnp.int32, (chunk, rows), 0)
                seen = kpos <= qpos
            out = []
            for h, w in enumerate(windows):
                kc = k_s[krows, w]
                s = dot(kc, qts[h], 1, 1) * scale - lses[h]
                if masked:
                    s = jnp.where(seen, s, NEG)
                p = jnp.exp(s)
                dp = dot(v_s[krows, w], dos[h], 1, 1)
                ds = (p * (dp - deltas[h])).astype(jnp.bfloat16)
                dv_s[krows, w] += dot(p.astype(jnp.bfloat16), dos[h], 1, 0)
                dk_s[krows, w] += dot(ds, qts[h], 1, 0)
                out.append(accs[h] + dot(kc, ds, 0, 0))
            return tuple(out)

        accs = (jnp.zeros((head_size, rows), jnp.float32),) * heads
        accs = lax.fori_loop(0, full, functools.partial(step, masked=False), accs)
        accs = lax.fori_loop(full, last, functools.partial(step, masked=True), accs)
        for h, w in enumerate(windows):
            dq_s[pl.ds(base, rows), w] = (accs[h] * scale).T
        return carry

    lax.fori_loop(0, nq // per, tile_body, 0)
    v_s[...] = dv_s[...].astype(v_s.dtype)
    give(v_s, dv_refs, sems.at[4], blk, lambda i: kslot_ref[i])
    k_s[...] = (dk_s[...] * scale).astype(k_s.dtype)
    give(k_s, dk_refs, sems.at[3], blk, lambda i: kslot_ref[i])
    give(dq_s, [dq_ref], sems.at[0], blk, lambda i: place_ref[i])
    finish(v_s, sems.at[4])
    finish(k_s, sems.at[3])
    finish(dq_s, sems.at[0])


def attend_back(place, seq, kslot, q, ks, vs, o, do, lse, heads, head_size, blk):
    nq = q.shape[0] // blk
    per = min(4, nq)
    keys = sum(k.shape[0] for k in ks)
    bf16, f32 = q.dtype, jnp.float32
    out = pl.pallas_call(
        functools.partial(
            attend_back_kernel, heads=heads, head_size=head_size, blk=blk, per=per, chunk=512,
            scale=1.0 / math.sqrt(head_size), pieces=len(ks),
        ),
        out_shape=(
            jax.ShapeDtypeStruct(q.shape, f32),
            *(jax.ShapeDtypeStruct(k.shape, bf16) for k in ks),
            *(jax.ShapeDtypeStruct(v.shape, bf16) for v in vs),
        ),
        grid_spec=pltpu.PrefetchScalarGridSpec(
            num_scalar_prefetch=3,
            grid=(),
            in_specs=[ANY] * 3 + [WHOLE] + [ANY] * (2 * len(ks)),
            out_specs=[ANY] * (1 + 2 * len(ks)),
            scratch_shapes=[
                pltpu.VMEM(q.shape, bf16),
                pltpu.VMEM((keys, q.shape[1]), bf16),
                pltpu.VMEM((keys, q.shape[1]), bf16),
                pltpu.VMEM(q.shape, bf16),
                pltpu.VMEM(q.shape, bf16),
                pltpu.VMEM(q.shape, f32),
                pltpu.VMEM((keys, q.shape[1]), f32),
                pltpu.VMEM((keys, q.shape[1]), f32),
                pltpu.SemaphoreType.DMA((5,)),
            ],
        ),
        compiler_params=pltpu.CompilerParams(vmem_limit_bytes=60 * 1024 * 1024),
        name="attend_back",
    )(place, seq, kslot, q, o, do, lse, *ks, *vs)
    return out[0], out[1 : 1 + len(ks)], out[1 + len(ks) :]


def rotate(x, cosine, sine, heads, head_size):
    parts = []
    for h in range(heads):
        part = x[:, h * head_size : (h + 1) * head_size]
        parts.append(part * cosine + pltpu.roll(part, head_size // 2, 1) * sine)
    return jnp.concatenate(parts, axis=1)


def prepare_kernel(pre_ref, recip_ref, gain_ref, cos_ref, sin_ref, q_ref, k_ref, *, heads, head_size):
    wide = heads * head_size
    for i, out in enumerate((q_ref, k_ref)):
        x = pre_ref[:, i * wide : (i + 1) * wide] * recip_ref[:, i : i + 1] * gain_ref[i : i + 1, :]
        out[...] = rotate(x, cos_ref[...], sin_ref[...], heads, head_size).astype(out.dtype)


def prepare(pre, recip, gain, cosine, sine, heads, head_size):
    rows, wide = pre.shape[0], heads * head_size
    step = 256
    return pl.pallas_call(
        functools.partial(prepare_kernel, heads=heads, head_size=head_size),
        out_shape=(jax.ShapeDtypeStruct((rows, wide), jnp.bfloat16),) * 2,
        grid=(rows // step,),
        in_specs=[
            pl.BlockSpec((step, 2 * wide), lambda i: (i, 0)),
            pl.BlockSpec((step, 2), lambda i: (i, 0)),
            pl.BlockSpec((2, wide), lambda i: (0, 0)),
            pl.BlockSpec((step, head_size), lambda i: (i, 0)),
            pl.BlockSpec((step, head_size), lambda i: (i, 0)),
        ],
        out_specs=[pl.BlockSpec((step, wide), lambda i: (i, 0))] * 2,
        name="prepare",
    )(pre, recip, gain, cosine, sine)


def unturn_kernel(
    dq_ref, dka_ref, dkb_ref, pre_ref, recip_ref, gain_ref, cos_ref, sin_ref,
    ds_ref, sum_ref, gg_ref, *, heads, head_size
):
    wide = heads * head_size
    dk = dka_ref[...] + dkb_ref[...].astype(jnp.float32)

    @pl.when(pl.program_id(0) == 0)
    def _():
        gg_ref[...] = jnp.zeros_like(gg_ref)

    for i, d in enumerate((dq_ref[...], dk)):
        cols = slice(i * wide, (i + 1) * wide)
        n = rotate(d, cos_ref[...], -sin_ref[...], heads, head_size)
        pre = pre_ref[:, cols]
        gg_ref[i : i + 1, :] += jnp.sum(n * pre * recip_ref[:, i : i + 1], axis=0, keepdims=True)
        scaled = n * gain_ref[i : i + 1, :]
        ds_ref[:, cols] = scaled
        sum_ref[i : i + 1, :] = jnp.sum((scaled * pre).T, axis=0, keepdims=True)


def unturn(dq, dka, dkb, pre, recip, gain, cosine, sine, heads, head_size):
    rows, wide = pre.shape[0], heads * head_size
    step = 256
    by_row = lambda n: pl.BlockSpec((step, n), lambda i: (i, 0))
    fixed = pl.BlockSpec((2, wide), lambda i: (0, 0))
    return pl.pallas_call(
        functools.partial(unturn_kernel, heads=heads, head_size=head_size),
        out_shape=(
            jax.ShapeDtypeStruct((rows, 2 * wide), jnp.float32),
            jax.ShapeDtypeStruct((2, rows), jnp.float32),
            jax.ShapeDtypeStruct((2, wide), jnp.float32),
        ),
        grid=(rows // step,),
        in_specs=[
            by_row(wide), by_row(wide), by_row(wide), by_row(2 * wide), by_row(2), fixed,
            by_row(head_size), by_row(head_size),
        ],
        out_specs=[by_row(2 * wide), pl.BlockSpec((2, step), lambda i: (0, i)), fixed],
        name="unturn",
    )(dq, dka, dkb, pre, recip, gain, cosine, sine)


def unpack_kernel(src_ref, *refs, plan, pieces, cover):
    outs = refs[: len(plan[0])]
    got, wide, in_sems, out_sems = refs[len(outs) :]

    def fetch(p):
        return pltpu.make_async_copy(src_ref.at[p], got.at[p % 2], in_sems.at[p % 2])

    def parts(p):
        copies = []
        for out, moves in zip(outs, plan[p]):
            for rows, cols, drow, dcol in moves:
                copies.append(
                    pltpu.make_async_copy(
                        wide.at[p % 2, pl.ds(*rows), pl.ds(*cols)],
                        out.at[pl.ds(drow, rows[1]), pl.ds(dcol, cols[1])],
                        out_sems.at[p % 2],
                    )
                )
        return copies

    def done(p):
        window = wide.at[p % 2, pl.ds(0, cover), :]
        pltpu.make_async_copy(window, window, out_sems.at[p % 2]).wait()

    fetch(0).start()
    for p in range(pieces):
        if p + 1 < pieces:
            fetch(p + 1).start()
        fetch(p).wait()
        if p >= 2:
            done(p - 2)
        wide[p % 2] = got[p % 2].astype(jnp.float32)
        for copy in parts(p):
            copy.start()
    for p in range(max(pieces - 2, 0), pieces):
        done(p)


def unpack(src, shapes, plan, cover):
    pieces, rows, cols = src.shape
    return pl.pallas_call(
        functools.partial(unpack_kernel, plan=plan, pieces=pieces, cover=cover),
        out_shape=tuple(jax.ShapeDtypeStruct(s, jnp.float32) for s in shapes),
        in_specs=[ANY],
        out_specs=[ANY] * len(shapes),
        scratch_shapes=[
            pltpu.VMEM((2, rows, cols), src.dtype),
            pltpu.VMEM((2, rows, cols), jnp.float32),
            pltpu.SemaphoreType.DMA((2,)),
            pltpu.SemaphoreType.DMA((2,)),
        ],
        compiler_params=pltpu.CompilerParams(vmem_limit_bytes=40 * 1024 * 1024),
        name="unpack",
    )(src)


EPS = 1e-06
THETA = 500000.0
HD = 128


def norm_forward(value, gain):
    recip = lax.rsqrt(jnp.mean(value * value, axis=-1, keepdims=True) + EPS)
    return (value * recip * gain, recip)


def norm_backward(value, recip, gain, grad_out):
    scaled = grad_out * gain
    width = value.shape[-1]
    grad_in = (
        recip * scaled
        - value * (recip * recip * recip) * jnp.sum(scaled * value, axis=-1, keepdims=True) / width
    )
    grad_gain = jnp.sum(grad_out * value * recip, axis=0)
    return (grad_in, grad_gain)


def flip(value, *axes):
    last = 2 ** len(axes) - 1
    return lax.ppermute(value, axes, [(i, i ^ last) for i in range(last + 1)])


def gather8(x, a, b):
    mine = jnp.stack([x, flip(x, b), flip(x, a), flip(x, a, b)])
    other = flip(mine, "c")
    return jnp.concatenate([mine, other]).reshape(8 * x.shape[0], x.shape[1])


def scatter8(x, a, b):
    bf16 = jnp.bfloat16
    parts = x.astype(bf16).reshape(2, 4, x.shape[0] // 8, x.shape[1])
    mine = x.reshape(parts.shape)[0] + flip(parts[1], "c").astype(jnp.float32)
    out = mine.astype(bf16)
    return (
        mine[0]
        + flip(out[1], b).astype(jnp.float32)
        + flip(out[2], a).astype(jnp.float32)
        + flip(out[3], a, b).astype(jnp.float32)
    )


def sum8(x, a, b):
    t = x.reshape((2, 2, 2) + x.shape[1:])
    for axis, name in enumerate(("c", a, b)):
        t = t + jnp.flip(flip(t, name), axis)
    return t.reshape(x.shape)


def in_order(value, axis, name):
    return jnp.where(lax.axis_index(name) == 1, jnp.flip(value, axis), value)


def gather4(x, a, b):
    pair = jnp.stack([x, flip(x, a)])
    quad = jnp.stack([pair, flip(pair, b)])
    return in_order(in_order(quad, 1, a), 0, b)


def halve(x, name):
    me = lax.axis_index(name)
    keep = lax.dynamic_index_in_dim(x, me, 0, keepdims=False)
    send = lax.dynamic_index_in_dim(x, 1 - me, 0, keepdims=False)
    return keep.astype(jnp.float32) + flip(send.astype(jnp.bfloat16), name).astype(jnp.float32)


def layer(
    layer_input,
    grad_output,
    positions,
    w_query,
    w_key,
    w_value,
    w_out,
    w_gate,
    w_up,
    w_down,
    gain_query,
    gain_key,
    gain_attn,
    gain_mlp,
    *,
    outer,
):
    f32 = jnp.float32
    bf16 = jnp.bfloat16
    rows, d = layer_input.shape
    drows, e = w_query.shape
    f = w_gate.shape[1]
    blk = rows // 2
    devices = positions.shape[0] // rows
    teams = devices // 8
    every = ("o", "h", "l", "y", "c", "x")
    heads = e // HD
    mine = heads // 8
    wide = mine * HD
    index = {name: lax.axis_index(name) for name in every}

    def by_team(w):
        return w.reshape(drows, mine, 8, HD).transpose(2, 0, 1, 3).reshape(8, drows, wide)

    gains = jnp.concatenate([gain_query, gain_key, gain_attn, gain_mlp])
    pad = drows * 128 - gains.shape[0]
    gains = jnp.pad(gains, (0, pad)).reshape(1, drows, 128)
    payload = jnp.concatenate(
        [by_team(w_query), by_team(w_key), by_team(w_value), jnp.broadcast_to(gains, (8, drows, 128))],
        axis=2,
    )
    payload = lax.all_to_all(payload, ("h", "l", "c"), 0, 0, tiled=True)
    payload = gather4(payload, "y", "x")
    if outer > 1:
        payload = lax.all_gather(payload, "o", axis=0)
    else:
        payload = payload[None]
    payload = payload.reshape(outer, 2, 2, 2, 2, 2, drows, 3 * wide + 128)
    payload = payload.transpose(0, 3, 4, 2, 5, 1, 6, 7).reshape(d, 3 * wide + 128)
    w_qkv = payload[:, : 3 * wide]
    gains = payload[:, 3 * wide :].reshape(devices, drows * 128)
    e_own, d_own = e // devices, d // devices
    full_gq = gains[:, :e_own].reshape(e)
    full_gk = gains[:, e_own : 2 * e_own].reshape(e)
    full_ga = gains[:, 2 * e_own : 2 * e_own + d_own].reshape(1, d).astype(f32)
    full_gm = gains[:, 2 * e_own + d_own : 2 * e_own + 2 * d_own].reshape(1, d).astype(f32)
    team_a = index["h"] * 4 + index["l"] * 2 + index["c"]

    def own_gain(g):
        return lax.dynamic_index_in_dim(g.reshape(mine, 8, HD), team_a, 1, keepdims=False).reshape(wide)

    gain_qk = jnp.stack([own_gain(full_gq), own_gain(full_gk)]).astype(f32)

    if outer == 1:
        w_o = gather4(w_out, "h", "x").transpose(1, 0, 2, 3).reshape(wide, d)
        w_o = lax.ppermute(
            w_o, ("h", "l", "y"), [(i, 2 * (i % 4) + i // 4) for i in range(8)]
        )
    else:
        w_o = lax.all_gather(w_out, every, axis=0, tiled=True).reshape(mine, 8, HD, d)
        w_o = lax.dynamic_index_in_dim(w_o, team_a, 1, keepdims=False).reshape(wide, d)

    unit = f // (8 * outer * 2)
    units = outer * 2 * unit

    def by_unit(w):
        return w.reshape(drows, outer * 2, 8, unit).transpose(2, 0, 1, 3).reshape(8, drows, units)

    ff = jnp.concatenate([by_unit(w_gate), by_unit(w_up)], axis=2)
    ff = lax.all_to_all(ff, ("l", "y", "c"), 0, 0, tiled=True)
    ff = gather4(ff, "h", "x")
    w_d = gather4(w_down, "h", "x")
    if outer > 1:
        ff = lax.all_gather(ff, "o", axis=0)
        w_d = lax.all_gather(w_d, "o", axis=0)
    else:
        ff, w_d = ff[None], w_d[None]
    ff = ff.reshape(outer, 2, 2, 2, 2, 2, drows, 2 * units)
    w_gu = ff.transpose(0, 2, 3, 4, 5, 1, 6, 7).reshape(d, 2 * units)
    w_d = w_d.transpose(0, 2, 1, 3, 4).reshape(units, d)

    table = positions.reshape(outer, 2, 2, 2, 2, 2, rows)[..., ::blk] // blk
    for axis, name in enumerate(every):
        if name != "o":
            table = in_order(table, axis, name)
    kslot = table.transpose(0, 5, 3, 4, 1, 2, 6)
    qblocks = lax.dynamic_index_in_dim(kslot, index["o"], 0, keepdims=False)[0, 0].reshape(-1)
    kslot = kslot.reshape(-1)
    nq = qblocks.shape[0]
    place = jnp.sum((qblocks[None, :] < qblocks[:, None]).astype(jnp.int32), axis=1)
    seq = jnp.sum(
        jnp.where(place[None, :] == jnp.arange(nq)[:, None], qblocks[None, :], 0), axis=1
    ).astype(jnp.int32)
    group_pos = (qblocks[:, None] * blk + jnp.arange(blk, dtype=jnp.int32)[None, :]).reshape(-1)
    freqs = THETA ** (-(2.0 * jnp.arange(HD // 2, dtype=f32)) / HD)
    angles = group_pos.astype(f32)[:, None] * freqs[None, :]
    cosine, sine = jnp.cos(angles), jnp.sin(angles)
    cosine = jnp.concatenate([cosine, cosine], axis=1)
    sine = jnp.concatenate([-sine, sine], axis=1)

    xg = gather8(layer_input.astype(bf16), "h", "l")
    group = xg.shape[0]
    pre = jnp.dot(xg, w_qkv, preferred_element_type=f32)
    pre_qk, value = pre[:, : 2 * wide], pre[:, 2 * wide :].astype(bf16)
    squares = jnp.sum((pre_qk * pre_qk).reshape(group, 2, wide), axis=-1).T
    squares = sum8(squares.reshape(2, 8, rows).transpose(1, 0, 2), "h", "l")
    recip = lax.rsqrt(squares.transpose(1, 0, 2).reshape(2, group) / e + EPS).T
    query, key = prepare(pre_qk, recip, gain_qk, cosine, sine, mine, HD)
    key_y, value_x = flip(key, "y"), flip(value, "x")
    keys = [key, key_y, flip(key, "x"), flip(key_y, "x")]
    values = [value, flip(value, "y"), value_x, flip(value_x, "y")]
    if outer > 1:
        keys = [lax.all_gather(jnp.stack(keys), "o", axis=0).reshape(-1, wide)]
        values = [lax.all_gather(jnp.stack(values), "o", axis=0).reshape(-1, wide)]
    attended, lse = attend(place, seq, kslot, query, keys, values, mine, HD, blk)
    proj = scatter8(jnp.dot(attended, w_o, preferred_element_type=f32), "h", "l")
    attn_branch, a_recip = norm_forward(proj, full_ga)
    mid = layer_input + attn_branch

    mg = gather8(mid.astype(bf16), "l", "y")
    gate_up = jnp.dot(mg, w_gu, preferred_element_type=f32)
    gate, up = gate_up[:, :units], gate_up[:, units:]
    sig = jax.nn.sigmoid(gate)
    silu = gate * sig
    hidden = (silu * up).astype(bf16)
    down = scatter8(jnp.dot(hidden, w_d, preferred_element_type=f32), "l", "y")
    mlp_branch, m_recip = norm_forward(down, full_gm)
    output = mid + mlp_branch
    d_down_f, local_gm = norm_backward(down, m_recip, full_gm, grad_output)
    dg = gather8(d_down_f.astype(bf16), "l", "y")
    d_hidden = lax.dot_general(dg, w_d, (((1,), (1,)), ((), ())), preferred_element_type=f32)
    d_gate = (d_hidden * up * sig * (1.0 + gate * (1.0 - sig))).astype(bf16)
    d_up = (d_hidden * silu).astype(bf16)
    d_gu = jnp.concatenate([d_gate, d_up], axis=1)
    d_mid = grad_output + scatter8(
        lax.dot_general(d_gu, w_gu, (((1,), (1,)), ((), ())), preferred_element_type=f32), "l", "y"
    )
    local_wd = lax.dot_general(hidden, dg, (((0,), (0,)), ((), ())), preferred_element_type=f32)
    local_wgu = lax.dot_general(mg, d_gu, (((0,), (0,)), ((), ())), preferred_element_type=f32)

    d_proj_f, local_ga = norm_backward(proj, a_recip, full_ga, d_mid)
    pg = gather8(d_proj_f.astype(bf16), "h", "l")
    d_att = lax.dot_general(pg, w_o, (((1,), (1,)), ((), ())), preferred_element_type=f32).astype(bf16)
    local_wo = lax.dot_general(attended, pg, (((0,), (0,)), ((), ())), preferred_element_type=f32)
    dq_rot, dk, dv = attend_back(
        place, seq, kslot, query, keys, values, attended, d_att, lse, mine, HD, blk
    )
    if outer > 1:
        def own_quarter(g):
            g = g[0].reshape(outer, 4, group, wide)
            return list(lax.psum_scatter(g, "o", scatter_dimension=0, tiled=False))

        dk, dv = own_quarter(dk), own_quarter(dv)
    dk_a = dk[0].astype(f32) + flip(dk[2], "x").astype(f32)
    dk_b = flip((dk[1].astype(f32) + flip(dk[3], "x").astype(f32)).astype(bf16), "y")
    dv_a = dv[0].astype(f32) + flip(dv[1], "y").astype(f32)
    dv_b = flip((dv[2].astype(f32) + flip(dv[3], "y").astype(f32)).astype(bf16), "x")
    d_value = (dv_a + dv_b.astype(f32)).astype(bf16)
    d_scaled, sums, local_gqk = unturn(
        dq_rot, dk_a, dk_b, pre_qk, recip, gain_qk, cosine, sine, mine, HD
    )
    sums = sum8(sums.reshape(2, 8, rows).transpose(1, 0, 2), "h", "l").transpose(1, 0, 2)
    sums = sums.reshape(2, group).T
    cubes = recip * recip * recip * sums / e
    d_qk = (
        recip[:, :, None] * d_scaled.reshape(group, 2, wide)
        - pre_qk.reshape(group, 2, wide) * cubes[:, :, None]
    ).astype(bf16)
    d_qkv = jnp.concatenate([d_qk.reshape(group, 2 * wide), d_value], axis=1)
    grad_input = d_mid + scatter8(
        lax.dot_general(d_qkv, w_qkv, (((1,), (1,)), ((), ())), preferred_element_type=f32), "h", "l"
    )
    local_wqkv = lax.dot_general(xg, d_qkv, (((0,), (0,)), ((), ())), preferred_element_type=f32)

    ctx = ("o", "h", "l", "y", "c")

    def settle(local, a, b):
        cols = local.shape[1]
        part = halve(local.reshape(2, -1, cols), b)
        part = halve(part.reshape(2, -1, cols), a)
        if outer > 1:
            part = lax.psum_scatter(
                part.astype(bf16).reshape(outer, -1, cols), "o", scatter_dimension=0, tiled=False
            )
        return part.astype(bf16)

    half_d, half_f = d // 2, f // 2
    part_gu, part_d, part_o = settle(local_wgu, "h", "x"), settle(local_wd, "h", "x"), settle(local_wo, "y", "x")
    part_qkv = settle(local_wqkv, "y", "x")
    n_qk, n_am = wide, d
    lines = -(-max(n_qk, n_am) // (3 * wide))
    lines = -(-lines // 16) * 16

    def line(v, n):
        return jnp.pad(v.reshape(2, n), ((0, 0), (0, lines * 3 * wide - n)))

    small = jnp.stack(
        [
            line(local_gqk.reshape(2, 2, -1).transpose(1, 0, 2), n_qk),
            line(jnp.stack([local_ga, local_gm]).reshape(2, 2, -1).transpose(1, 0, 2), n_am),
        ],
        axis=1,
    )
    small = halve(small, "x")
    small = halve(small, "y")
    if outer > 1:
        small = lax.psum(small, "o") / outer
    small = small.reshape(lines, 3 * wide).astype(bf16)
    part_qkv = jnp.concatenate([part_qkv, small])
    n_gu, n_d, n_o, n_qkv = part_gu.shape[0], part_d.shape[0], part_o.shape[0], part_qkv.shape[0] - lines

    if outer == 1:
        first = lax.all_gather(jnp.concatenate([part_gu, part_d, part_o]), ctx, axis=0).reshape(16, -1, d)
        last = lax.all_gather(part_qkv, ctx, axis=0).reshape(16, -1, 3 * wide)
        plan_first, plan_last = [], []
        for p in range(16):
            h, l, y, c = p >> 3, (p >> 2) & 1, (p >> 1) & 1, p & 1
            team_f, team_q = 4 * l + 2 * y + c, 4 * h + 2 * l + c
            ups = [
                [
                    ((0, n_gu), (m * units + o * unit, unit), h * n_gu, (o * 8 + team_f) * unit)
                    for o in range(2)
                ]
                for m in range(2)
            ]
            downs = [((n_gu, n_d), (0, d), team_f * unit + h * n_d, 0)]
            os = [((n_gu + n_d, n_o), (0, d), team_q * HD + y * n_o, 0)]
            plan_first.append([*ups, downs, os])
            plan_last.append(
                [
                    [
                        ((0, n_qkv), (m * wide + o * HD, HD), y * n_qkv, (o * 8 + team_q) * HD)
                        for o in range(mine)
                    ]
                    for m in range(3)
                ]
            )
        total_wg, total_wu, total_wd, total_wo = unpack(
            first, [(half_d, f), (half_d, f), (half_f, d), (e // 2, d)], plan_first, n_gu + n_d + n_o
        )
        total_wq, total_wk, total_wv = unpack(last, [(half_d, e)] * 3, plan_last, n_qkv)
        got_small = last[:, n_qkv:]
    else:
        got = lax.all_gather(part_qkv, ctx, axis=0)
        got_small = got.reshape(-1, n_qkv + lines, 3 * wide)[:, n_qkv:]
        got = got.reshape(outer, 2, 2, 2, 2, n_qkv + lines, 3 * wide)[..., :n_qkv, :]
        got = got.transpose(3, 0, 5, 1, 2, 4, 6).reshape(half_d, 8, 3, mine, HD)
        got = got.transpose(2, 0, 3, 1, 4).reshape(3, half_d, e)
        total_wq, total_wk, total_wv = got[0].astype(f32), got[1].astype(f32), got[2].astype(f32)
        got = lax.all_gather(part_gu, ctx, axis=0)
        got = got.reshape(outer, 2, 8, n_gu, 2, outer * 2, unit)
        got = got.transpose(4, 1, 0, 3, 5, 2, 6).reshape(2, half_d, f)
        total_wg, total_wu = got[0].astype(f32), got[1].astype(f32)
        got = lax.all_gather(part_d, ctx, axis=0)
        got = got.reshape(outer, 2, 8, n_d, d).transpose(2, 1, 0, 3, 4)
        total_wd = got.reshape(8, outer, unit, d).transpose(1, 0, 2, 3).reshape(half_f, d).astype(f32)
        got = lax.all_gather(part_o, ctx, axis=0)
        got = got.reshape(outer, 2, 2, 2, 2, n_o, d).transpose(1, 2, 4, 3, 0, 5, 6)
        total_wo = got.reshape(e // 2, d).astype(f32)

    got_small = got_small.astype(f32).reshape(outer, 4, 2, 2, lines * 3 * wide)
    if outer > 1:
        got_small = jnp.sum(got_small, axis=0)
    else:
        got_small = got_small[0]
    qk = got_small[:, 0, :, :n_qk].reshape(8, 2, mine // 2, HD).transpose(1, 2, 0, 3).reshape(2, e // 2)
    total_gq, total_gk = qk[0], qk[1]
    am = jnp.sum(got_small[:, 1, :, :n_am], axis=(0, 1)).reshape(2, half_d)
    total_ga, total_gm = am[0], am[1]
    return (
        output,
        grad_input,
        total_wq,
        total_wk,
        total_wv,
        total_wo,
        total_wg,
        total_wu,
        total_wd,
        total_gq,
        total_gk,
        total_ga,
        total_gm,
    )


def solution(mesh):
    outer = mesh.shape["ctx"] // 16
    names = ("o", "h", "l", "y", "c", "x")
    fine = Mesh(mesh.devices.reshape(outer, 2, 2, 2, 2, 2), names)
    every, half = P(names), P("x")
    in_specs = (every, every, P()) + (every,) * 11
    out_specs = (every, every) + (half,) * 11
    return jax.shard_map(
        functools.partial(layer, outer=outer),
        mesh=fine,
        in_specs=in_specs,
        out_specs=out_specs,
        check_vma=False,
    )
```

time: 959 us -> 819 us (0.85)
  local copies, waits for them, and re-layouts: 216 us -> 44.8 us
  waiting for transfers between devices: 386 us -> 495 us
  other arithmetic: 110 us -> 54.9 us
  blocking collectives: 39.5 us -> 0 us
  Pallas kernels: 56.2 us -> 77.9 us
    all_gather x4 -> x2, waiting for transfers between devices: 0.01 us -> 61.5 us  [the longest x1 61.5 us: layer(): lax.all_gather(jnp.concatenate([part_gu, part_d, part_o]), ctx, axis=0)]
    reshape x16 -> x9, local copies, waits for them, and re-layouts: 49.3 us -> 3.95 us  [the longest x1 2.33 us: layer(): squares = jnp.sum((pre_qk * pre_qk).reshape(group, 2, wide), axis=-1).T]
    ppermute x62 -> x68, waiting for transfers between devices: 370 us -> 409 us  [flip(): return lax.ppermute(value, axes, [(i, i ^ last) for i in range(last + 1)])]
    psum x1 -> x0, blocking collectives: 39.5 us -> none  [layer(): small = lax.psum(small, every)]
    unnamed x153 -> x137, local copies, waits for them, and re-layouts: 55.3 us -> 18.7 us
    convert_element_type x9 -> x1, local copies, waits for them, and re-layouts: 36.4 us -> 0.04 us  [layer(): small = small.reshape(lines, 3 * wide).astype(bf16)]
    pallas_call x0 -> x4, Pallas kernels: none -> 34 us  [the longest x2 24.5 us: unpack(): pl.pallas_call(functools.partial(unpack_kernel, plan=plan, pieces=pieces,...]
    transpose x6 -> x0, local copies, waits for them, and re-layouts: 18.8 us -> none  [the longest x1 16.2 us: layer(): got = got.transpose(3, 0, 5, 1, 2, 4, 6).reshape(half_d, 8, 3, wide)]
  transfers between devices with their start and end apart: 68 -> 73, of which waited for: 40 -> 42; matrix products, arithmetic and copies ran while one was open for 27% -> 11% of each run, Pallas kernels for 6% -> 5%
where the time goes in v2:
time: 819 us; the launch traced here: 808 us
  waiting for transfers between devices  495 us (60%)
  starting transfers between devices  82.6 us (10%)
  Pallas kernels  77.9 us (10%)
  other arithmetic  54.9 us (7%)
  local copies, waits for them, and re-layouts  44.8 us (5%)
  matrix products  37.1 us (5%)
  between operations  16.2 us (2%)
    ppermute x68, waiting for transfers between devices, flip(): return lax.ppermute(value, axes, [(i, i ^ last) for i in range(last + 1)])  409 us
    ppermute x68, starting transfers between devices, flip(): return lax.ppermute(value, axes, [(i, i ^ last) for i in range(last + 1)])  67.3 us
    all_gather x1, waiting for transfers between devices, layer(): lax.all_gather(jnp.concatenate([part_gu, part_d, part_o]), ctx, axis=0)  61.5 us
    pallas_call x2, Pallas kernels, unpack(): pl.pallas_call(functools.partial(unpack_kernel, plan=plan, pieces=pieces,...  24.5 us
    pallas_call x1, Pallas kernels, attend_back(): pl.pallas_call(functools.partial(attend_back_kernel, heads=heads, head_si...  24.3 us
    all_to_all x1, waiting for transfers between devices, layer(): payload = lax.all_to_all(payload, ('h', 'l', 'c'), 0, 0, tiled=True)  22.9 us
    pallas_call x1, Pallas kernels, attend(): pl.pallas_call(functools.partial(attend_kernel, heads=heads, head_size=he...  19.6 us
    unnamed x137, local copies, waits for them, and re-layouts  18.7 us
  transfers between devices with their start and end apart: 73, of which 42 were waited for; matrix products, arithmetic and copies ran while one was open for 11% of the time, Pallas kernels for 5%

profile of v2, /device:TPU:0, one launch (start us, length us, event | category | flops | bytes accessed | tf_op | source)
XLA Modules:
  0.0 808.4 jit_solution(3762902321355193494)
XLA Ops:
  27.4 22.9 %all-to-all-done = bf16[8,32,896]{2,1,0:T(8,128)(2,1)S(1)} async-done(((bf16[8,32,896]{2,1,0:T(8,128)(2,1)}), bf16[8,32,896]{2,1,0:T(8,128)(2,1)S(1)}, u32[]{:S(2)}, u32[]{:S(2)}) %all-to-all-start) | async-done | bytes 458784 | tf_op jit(solution)/shard_map/all_to_all | solution.py:518
  64.5 19.9 %collective-permute-done.5 = bf16[2,8,32,896]{3,2,1,0:T(8,128)(2,1)S(1)} collective-permute-done((bf16[2,8,32,896]{3,2,1,0:T(8,128)(2,1)S(1)}, bf16[2,8,32,896]{3,2,1,0:T(8,128)(2,1)S(1)}, u32[]{:S(2)}, u32[]{:S(2)}) %collective-permute-start.5) | collective-permute-done | bytes 917536 | tf_op jit(solution)/shard_map/ppermute | solution.py:430
  100.9 26.1 %collective-permute-done.7 = f32[2,2,2,2,128]{3,4,2,1,0:T(8,128)S(1)} collective-permute-done((f32[2,2,2,2,128]{3,4,2,1,0:T(8,128)S(1)}, f32[2,2,2,2,128]{3,4,2,1,0:T(8,128)S(1)}, u32[]{:S(2)}, u32[]{:S(2)}) %collective-permute-start.7) | collective-permute-done | bytes 8224 | tf_op jit(solution)/shard_map/ppermute | solution.py:430
  127.8 13.2 %collective-permute-done.8 = f32[2,2,2,2,128]{3,4,2,1,0:T(8,128)S(1)} collective-permute-done((f32[2,2,2,2,128]{3,4,2,1,0:T(8,128)S(1)}, f32[2,2,2,2,128]{3,4,2,1,0:T(8,128)S(1)}, u32[]{:S(2)}, u32[]{:S(2)}) %collective-permute-start.8) | collective-permute-done | bytes 8224 | tf_op jit(solution)/shard_map/ppermute | solution.py:430
  173.1 9.8 %collective-permute-done.12.refs_6_.refs_9_ = bf16[1024,256]{1,0:T(8,128)(2,1)S(1)} collective-permute-done((bf16[1024,256]{1,0:T(8,128)(2,1)S(1)}, bf16[1024,256]{1,0:T(8,128)(2,1)S(1)}, u32[]{:S(2)}, u32[]{:S(2)}) %collective-permute-start.12) | collective-permute-done | bytes 524320 | tf_op jit(solution)/shard_map/ppermute | solution.py:430
  192.3 19.6 %attend.1 = (bf16[1024,256]{1,0:T(8,128)(2,1)}, f32[8,256]{1,0:T(8,128)}) custom-call(s32[16]{0:T(128)} %copy-done.51, s32[16]{0:T(128)} %select_reduce_fusion.seq_ref, s32[64]{0:T(128)} %reshape.295.kslot_ref, bf16[1024,256]{1,0:T(8,128)(2,1)} %get-tuple-element.36.refs_0_, bf16[1024,256]{1,0:T(8,128)(2,1)} %get-tuple-element.37.refs_1_.refs_4_, ...), custom_call_target="tpu_custom_call" | custom-call | tf_op jit(solution)/shard_map/attend/pallas_call | solution.py:134
  240.4 29.9 %collective-permute-done.26 = bf16[8,32,1024]{2,1,0:T(8,128)(2,1)S(1)} collective-permute-done((bf16[8,32,1024]{2,1,0:T(8,128)(2,1)}, bf16[8,32,1024]{2,1,0:T(8,128)(2,1)S(1)}, u32[]{:S(2)}, u32[]{:S(2)}) %collective-permute-start.26) | collective-permute-done | bytes 524320 | tf_op jit(solution)/shard_map/ppermute | solution.py:430
  285.9 10.7 %collective-permute-done.27 = bf16[2,8,32,1024]{3,2,1,0:T(8,128)(2,1)} collective-permute-done((bf16[2,8,32,1024]{3,2,1,0:T(8,128)(2,1)}, bf16[2,8,32,1024]{3,2,1,0:T(8,128)(2,1)}, u32[]{:S(2)}, u32[]{:S(2)}) %collective-permute-start.27) | collective-permute-done | bytes 1048608 | tf_op jit(solution)/shard_map/ppermute | solution.py:430
  316.5 10.9 %collective-permute-done.31 = bf16[128,1024]{1,0:T(8,128)(2,1)S(1)} collective-permute-done((bf16[128,1024]{1,0:T(8,128)(2,1)}, bf16[128,1024]{1,0:T(8,128)(2,1)S(1)}, u32[]{:S(2)}, u32[]{:S(2)}) %collective-permute-start.31) | collective-permute-done | bytes 262176 | tf_op jit(solution)/shard_map/ppermute | solution.py:430
  350.0 13.8 %fusion.9 = f32[1024,1024]{1,0:T(8,128)S(1)} fusion(bf16[1024,1024]{1,0:T(8,128)(2,1)S(1)} %bitcast.363, bf16[1024,512]{0,1:T(8,128)(2,1)S(1)} %get-tuple-element.85, bf16[1024,512]{0,1:T(8,128)(2,1)S(1)} %get-tuple-element.84), kind=kOutput, calls=%fused_computation.36 | convolution fusion | flops 2151677952 | bytes 8388608 | tf_op jit(solution)/shard_map/dot_general | solution.py:622
  370.8 10.5 %collective-permute-done.39 = bf16[128,1024]{1,0:T(8,128)(2,1)S(1)} collective-permute-done((bf16[128,1024]{1,0:T(8,128)(2,1)S(1)}, bf16[128,1024]{1,0:T(8,128)(2,1)S(1)}, u32[]{:S(2)}, u32[]{:S(2)}) %collective-permute-start.39) | collective-permute-done | bytes 262176 | tf_op jit(solution)/shard_map/ppermute | solution.py:430
  395.1 12.9 %collective-permute-done.43 = bf16[128,1024]{1,0:T(8,128)(2,1)S(1)} collective-permute-done((bf16[128,1024]{1,0:T(8,128)(2,1)S(1)}, bf16[128,1024]{1,0:T(8,128)(2,1)S(1)}, u32[]{:S(2)}, u32[]{:S(2)}) %collective-permute-start.43) | collective-permute-done | bytes 262176 | tf_op jit(solution)/shard_map/ppermute | solution.py:430
  413.9 24.3 %attend_back.1 = (f32[1024,256]{1,0:T(8,128)}, bf16[1024,256]{1,0:T(8,128)(2,1)}, bf16[1024,256]{1,0:T(8,128)(2,1)}, bf16[1024,256]{1,0:T(8,128)(2,1)}, bf16[102...) custom-call(s32[16]{0:T(128)} %copy-done.51, ...), custom_call_target="tpu_custom_call" | custom-call | tf_op jit(solution)/shard_map/attend_back/pallas_call | solution.py:241
  440.4 13.0 %collective-permute-done.47 = bf16[1024,256]{1,0:T(8,128)(2,1)S(1)} collective-permute-done((bf16[1024,256]{1,0:T(8,128)(2,1)}, bf16[1024,256]{1,0:T(8,128)(2,1)S(1)}, u32[]{:S(2)}, u32[]{:S(2)}) %collective-permute-start.47) | collective-permute-done | bytes 524320 | tf_op jit(solution)/shard_map/ppermute | solution.py:430
  487.5 18.9 %collective-permute-done.50 = f32[2,2,2,2,128]{3,4,2,1,0:T(8,128)S(1)} collective-permute-done((f32[2,2,2,2,128]{3,4,2,1,0:T(8,128)S(1)}, f32[2,2,2,2,128]{3,4,2,1,0:T(8,128)S(1)}, u32[]{:S(2)}, u32[]{:S(2)}) %collective-permute-start.50) | collective-permute-done | bytes 8224 | tf_op jit(solution)/shard_map/ppermute | solution.py:430
  508.1 12.3 %collective-permute-done.51 = f32[2,2,2,2,128]{3,4,2,1,0:T(8,128)S(1)} collective-permute-done((f32[2,2,2,2,128]{3,4,2,1,0:T(8,128)S(1)}, f32[2,2,2,2,128]{3,4,2,1,0:T(8,128)S(1)}, u32[]{:S(2)}, u32[]{:S(2)}) %collective-permute-start.51) | collective-permute-done | bytes 8224 | tf_op jit(solution)/shard_map/ppermute | solution.py:430
  529.9 16.1 %collective-permute-done.59 = bf16[512,768]{1,0:T(8,128)(2,1)S(1)} collective-permute-done((bf16[512,768]{1,0:T(8,128)(2,1)S(1)}, bf16[512,768]{1,0:T(8,128)(2,1)S(1)}, u32[]{:S(2)}, u32[]{:S(2)}) %collective-permute-start.59) | collective-permute-done | bytes 786464 | tf_op jit(solution)/shard_map/ppermute | solution.py:430
  570.8 26.8 %collective-permute-done.65 = bf16[256,1024]{1,0:T(8,128)(2,1)S(1)} collective-permute-done((bf16[256,1024]{1,0:T(8,128)(2,1)S(1)}, bf16[256,1024]{1,0:T(8,128)(2,1)S(1)}, u32[]{:S(2)}, u32[]{:S(2)}) %collective-permute-start.65) | collective-permute-done | bytes 524320 | tf_op jit(solution)/shard_map/ppermute | solution.py:430
  606.4 30.9 %collective-permute-done.66 = bf16[128,1024]{1,0:T(8,128)(2,1)S(1)} collective-permute-done((bf16[128,1024]{1,0:T(8,128)(2,1)S(1)}, bf16[128,1024]{1,0:T(8,128)(2,1)S(1)}, u32[]{:S(2)}, u32[]{:S(2)}) %collective-permute-start.66) | collective-permute-done | bytes 262176 | tf_op jit(solution)/shard_map/ppermute | solution.py:430
  639.2 10.4 %collective-permute-done.64 = bf16[256,1024]{1,0:T(8,128)(2,1)S(1)} collective-permute-done((bf16[256,1024]{1,0:T(8,128)(2,1)S(1)}, bf16[256,1024]{1,0:T(8,128)(2,1)S(1)}, u32[]{:S(2)}, u32[]{:S(2)}) %collective-permute-start.64) | collective-permute-done | bytes 524320 | tf_op jit(solution)/shard_map/ppermute | solution.py:430
  660.8 18.6 %collective-permute-done.56 = bf16[128,1024]{1,0:T(8,128)(2,1)S(1)} collective-permute-done((bf16[128,1024]{1,0:T(8,128)(2,1)S(1)}, bf16[128,1024]{1,0:T(8,128)(2,1)S(1)}, u32[]{:S(2)}, u32[]{:S(2)}) %collective-permute-start.56) | collective-permute-done | bytes 262176 | tf_op jit(solution)/shard_map/ppermute | solution.py:430
  679.9 29.4 %collective-permute-done.57 = bf16[128,1024]{1,0:T(8,128)(2,1)S(1)} collective-permute-done((bf16[128,1024]{1,0:T(8,128)(2,1)S(1)}, bf16[128,1024]{1,0:T(8,128)(2,1)S(1)}, u32[]{:S(2)}, u32[]{:S(2)}) %collective-permute-start.57) | collective-permute-done | bytes 262176 | tf_op jit(solution)/shard_map/ppermute | solution.py:430
  723.1 61.5 %all-gather.7.cloned.1.call-done = bf16[7168,1024]{1,0:T(8,128)(2,1)} async-done(((bf16[448,1024]{1,0:T(8,128)(2,1)}), bf16[7168,1024]{1,0:T(8,128)(2,1)}) %all-gather.7.cloned.1.call-update) | async-done | bytes 14680080 | tf_op jit(solution)/shard_map/all_gather | solution.py:699
  784.6 16.4 %unpack.3 = (f32[512,4096]{1,0:T(8,128)}, f32[512,4096]{1,0:T(8,128)}, f32[2048,1024]{1,0:T(8,128)}, f32[1024,1024]{1,0:T(8,128)}) custom-call(bf16[16,448,1024]{2,1,0:T(8,128)(2,1)} %bitcast.329), custom_call_target="tpu_custom_call" | custom-call | tf_op jit(solution)/shard_map/unpack/pallas_call | solution.py:391
  (437 shorter events, 313.3 us)
Async XLA Ops:
  9.1 44.6 %collective-permute-start.2 = (bf16[128,1024]{1,0:T(8,128)(2,1)}, bf16[128,1024]{1,0:T(8,128)(2,1)S(1)}, u32[]{:S(2)}, u32[]{:S(2)}) collective-permute-start(bf16[128,1024]{1,0:T(8,128)(2,1)} %get-tuple-element.83), channel_id=1, source_target_pairs={{0,24},{8,16},{16,8},{24,0},{1,25},{9,17},{17,9},{25,1},{2,26},{10... | collective-permute-start | bytes 786440 | tf_op jit(solution)/shard_map/ppermute | solution.py:430
  14.2 39.5 %collective-permute-start.1 = (bf16[128,1024]{1,0:T(8,128)(2,1)}, bf16[128,1024]{1,0:T(8,128)(2,1)S(1)}, u32[]{:S(2)}, u32[]{:S(2)}) collective-permute-start(bf16[128,1024]{1,0:T(8,128)(2,1)} %get-tuple-element.83), channel_id=1, source_target_pairs={{0,16},{16,0},{1,17},{17,1},{2,18},{18,2},{3,19},{19,3},{4,20},{20... | collective-permute-start | bytes 786440 | tf_op jit(solution)/shard_map/ppermute | solution.py:430
  14.2 39.5 %collective-permute-start = (bf16[128,1024]{1,0:T(8,128)(2,1)}, bf16[128,1024]{1,0:T(8,128)(2,1)S(1)}, u32[]{:S(2)}, u32[]{:S(2)}) collective-permute-start(bf16[128,1024]{1,0:T(8,128)(2,1)} %get-tuple-element.83), channel_id=1, source_target_pairs={{0,8},{8,0},{1,9},{9,1},{2,10},{10,2},{3,11},{11,3},{4,12},{12,4},... | collective-permute-start | bytes 786440 | tf_op jit(solution)/shard_map/ppermute | solution.py:430
  23.3 39.7 %collective-permute-start.15 = (bf16[64,1024]{1,0:T(8,128)(2,1)}, bf16[64,1024]{1,0:T(8,128)(2,1)S(1)}, u32[]{:S(2)}, u32[]{:S(2)}) collective-permute-start(bf16[64,1024]{1,0:T(8,128)(2,1)} %param.20), channel_id=1, source_target_pairs={{0,16},{16,0},{1,17},{17,1},{2,18},{18,2},{3,19},{19,3},{4,20},{20... | collective-permute-start | bytes 393224 | tf_op jit(solution)/shard_map/ppermute | solution.py:430
  63.8 84.2 %collective-permute-start.16 = (bf16[2,64,1024]{2,1,0:T(8,128)(2,1)}, bf16[2,64,1024]{2,1,0:T(8,128)(2,1)}, u32[]{:S(2)}, u32[]{:S(2)}) collective-permute-start(bf16[2,64,1024]{2,1,0:T(8,128)(2,1)} %get-tuple-element.110), channel_id=1, source_target_pairs={{0,1},{1,0},{2,3},{3,2},{4,5},{5,4},{6,7},{7,6},{8,9},{9,8},{10,11... | collective-permute-start | bytes 786440 | tf_op jit(solution)/shard_map/ppermute | solution.py:430
  99.3 50.9 %collective-permute-start.13 = (bf16[1024,256]{1,0:T(8,128)(2,1)S(1)}, bf16[1024,256]{1,0:T(8,128)(2,1)S(1)}, u32[]{:S(2)}, u32[]{:S(2)}) collective-permute-start(bf16[1024,256]{1,0:T(8,128)(2,1)S(1)} %slice.296.refs_5_.refs_8_), channel_id=1, source_target_pairs={{0,1},{1,0},{2,3},{3,2},{4,5},{5,4},{6,7},{7,6},{8,9},{9,8},{10,11... | collective-permute-start | bytes 1572872 | tf_op jit(solution)/shard_map/ppermute | solution.py:430
  149.0 33.9 %collective-permute-start.12 = (bf16[1024,256]{1,0:T(8,128)(2,1)S(1)}, bf16[1024,256]{1,0:T(8,128)(2,1)S(1)}, u32[]{:S(2)}, u32[]{:S(2)}) collective-permute-start(bf16[1024,256]{1,0:T(8,128)(2,1)S(1)} %slice.296.refs_5_.refs_8_), channel_id=1, source_target_pairs={{0,4},{4,0},{1,5},{5,1},{2,6},{6,2},{3,7},{7,3},{8,12},{12,8},{9,1... | collective-permute-start | bytes 1572872 | tf_op jit(solution)/shard_map/ppermute | solution.py:430
  149.6 33.3 %collective-permute-start.10 = (bf16[1024,256]{1,0:T(8,128)(2,1)S(1)}, bf16[1024,256]{1,0:T(8,128)(2,1)S(1)}, u32[]{:S(2)}, u32[]{:S(2)}) collective-permute-start(bf16[1024,256]{1,0:T(8,128)(2,1)S(1)} %copy-done.29), channel_id=1, source_target_pairs={{0,1},{1,0},{2,3},{3,2},{4,5},{5,4},{6,7},{7,6},{8,9},{9,8},{10,11... | collective-permute-start | bytes 1572872 | tf_op jit(solution)/shard_map/ppermute | solution.py:430
  150.2 42.1 %collective-permute-start.14 = (bf16[1024,256]{1,0:T(8,128)(2,1)S(1)}, bf16[1024,256]{1,0:T(8,128)(2,1)}, u32[]{:S(2)}, u32[]{:S(2)}) collective-permute-start(bf16[1024,256]{1,0:T(8,128)(2,1)S(1)} %collective-permute-done.13.refs_7_.refs_10_), channel_id=1, source_target_pairs={{0,4},{4,0},{1,5},{5,1},{2,6},{6,2},{3,7},{7,3},{8,12},{12,8},{9,1... | collective-permute-start | bytes 1572872 | tf_op jit(solution)/shard_map/ppermute | solution.py:430
  162.9 49.1 %collective-permute-start.17 = (bf16[256,1024]{1,0:T(8,128)(2,1)}, bf16[256,1024]{1,0:T(8,128)(2,1)}, u32[]{:S(2)}, u32[]{:S(2)}) collective-permute-start(bf16[256,1024]{1,0:T(8,128)(2,1)} %bitcast.39), channel_id=1, source_target_pairs={{0,0},{4,8},{8,16},{12,24},{16,4},{20,12},{24,20},{28,28},{1,1},{5... | collective-permute-start | bytes 1572872 | tf_op jit(solution)/shard_map/ppermute | solution.py:542
  182.9 34.1 %collective-permute-start.28 = (bf16[128,1024]{1,0:T(8,128)(2,1)}, bf16[128,1024]{1,0:T(8,128)(2,1)S(1)}, u32[]{:S(2)}, u32[]{:S(2)}) collective-permute-start(bf16[128,1024]{1,0:T(8,128)(2,1)} %param.23), channel_id=1, source_target_pairs={{0,16},{16,0},{1,17},{17,1},{2,18},{18,2},{3,19},{19,3},{4,20},{20... | collective-permute-start | bytes 786440 | tf_op jit(solution)/shard_map/ppermute | solution.py:430
  223.1 487.2 %all-gather.5.cloned.1.call-start = ((), (), s32[]{:S(2)}) async-start(), calls=%async_computation.2 | async-start | bytes 7102464 | tf_op jit(solution)/shard_map/all_gather | solution.py:700
  232.9 37.4 %collective-permute-start.26 = (bf16[8,32,1024]{2,1,0:T(8,128)(2,1)}, bf16[8,32,1024]{2,1,0:T(8,128)(2,1)S(1)}, u32[]{:S(2)}, u32[]{:S(2)}) collective-permute-start(bf16[8,32,1024]{2,1,0:T(8,128)(2,1)} %all-to-all-done.1), channel_id=1, source_target_pairs={{0,16},{16,0},{1,17},{17,1},{2,18},{18,2},{3,19},{19,3},{4,20},{20... | collective-permute-start | bytes 1572872 | tf_op jit(solution)/shard_map/ppermute | solution.py:430
  236.5 37.8 %collective-permute-start.19 = (bf16[128,1024]{1,0:T(8,128)(2,1)S(1)}, bf16[128,1024]{1,0:T(8,128)(2,1)S(1)}, u32[]{:S(2)}, u32[]{:S(2)}) collective-permute-start(bf16[128,1024]{1,0:T(8,128)(2,1)S(1)} %get-tuple-element.99), channel_id=1, source_target_pairs={{0,8},{8,0},{1,9},{9,1},{2,10},{10,2},{3,11},{11,3},{4,12},{12,4},... | collective-permute-start | bytes 786440 | tf_op jit(solution)/shard_map/ppermute | solution.py:430
  238.2 36.1 %collective-permute-start.21 = (bf16[128,1024]{1,0:T(8,128)(2,1)S(1)}, bf16[128,1024]{1,0:T(8,128)(2,1)S(1)}, u32[]{:S(2)}, u32[]{:S(2)}) collective-permute-start(bf16[128,1024]{1,0:T(8,128)(2,1)S(1)} %get-tuple-element.100), channel_id=1, source_target_pairs={{0,24},{8,16},{16,8},{24,0},{1,25},{9,17},{17,9},{25,1},{2,26},{10... | collective-permute-start | bytes 786440 | tf_op jit(solution)/shard_map/ppermute | solution.py:430
  240.4 40.3 %collective-permute-start.20 = (bf16[128,1024]{1,0:T(8,128)(2,1)S(1)}, bf16[128,1024]{1,0:T(8,128)(2,1)S(1)}, u32[]{:S(2)}, u32[]{:S(2)}) collective-permute-start(bf16[128,1024]{1,0:T(8,128)(2,1)S(1)} %get-tuple-element.101), channel_id=1, source_target_pairs={{0,16},{16,0},{1,17},{17,1},{2,18},{18,2},{3,19},{19,3},{4,20},{20... | collective-permute-start | bytes 786440 | tf_op jit(solution)/shard_map/ppermute | solution.py:430
  462.9 43.7 %collective-permute-start.52 = (bf16[1024,256]{1,0:T(8,128)(2,1)}, bf16[1024,256]{1,0:T(8,128)(2,1)}, u32[]{:S(2)}, u32[]{:S(2)}) collective-permute-start(bf16[1024,256]{1,0:T(8,128)(2,1)} %get-tuple-element.48), channel_id=1, source_target_pairs={{0,4},{4,0},{1,5},{5,1},{2,6},{6,2},{3,7},{7,3},{8,12},{12,8},{9,1... | collective-permute-start | bytes 1572872 | tf_op jit(solution)/shard_map/ppermute | solution.py:430
  486.2 42.5 %collective-permute-start.61 = (bf16[2,12288]{1,0:T(2,128)(2,1)S(1)}, bf16[2,12288]{1,0:T(2,128)(2,1)S(1)}, u32[]{:S(2)}, u32[]{:S(2)}) collective-permute-start(bf16[2,12288]{1,0:T(2,128)(2,1)S(1)} %fusion.44), channel_id=1, source_target_pairs={{0,1},{1,0},{2,3},{3,2},{4,5},{5,4},{6,7},{7,6},{8,9},{9,8},{10,11... | collective-permute-start | bytes 147464 | tf_op jit(solution)/shard_map/ppermute | solution.py:430
  556.5 228.1 %all-gather.7.cloned.1.call-start = ((), (), s32[]{:S(2)}) async-start(), calls=%async_computation.3 | async-start | bytes 15597568 | tf_op jit(solution)/shard_map/all_gather | solution.py:699
  563.7 37.6 %collective-permute-start.63 = (bf16[512,1024]{1,0:T(8,128)(2,1)S(1)}, bf16[512,1024]{1,0:T(8,128)(2,1)}, u32[]{:S(2)}, u32[]{:S(2)}) collective-permute-start(bf16[512,1024]{1,0:T(8,128)(2,1)S(1)} %fusion.10), channel_id=1, source_target_pairs={{0,1},{1,0},{2,3},{3,2},{4,5},{5,4},{6,7},{7,6},{8,9},{9,8},{10,11... | collective-permute-start | bytes 3145736 | tf_op jit(solution)/shard_map/ppermute | solution.py:430
  599.0 38.3 %collective-permute-start.66 = (bf16[128,1024]{1,0:T(8,128)(2,1)S(1)}, bf16[128,1024]{1,0:T(8,128)(2,1)S(1)}, u32[]{:S(2)}, u32[]{:S(2)}) collective-permute-start(bf16[128,1024]{1,0:T(8,128)(2,1)S(1)} %fusion.34), channel_id=1, source_target_pairs={{0,16},{16,0},{1,17},{17,1},{2,18},{18,2},{3,19},{19,3},{4,20},{20... | collective-permute-start | bytes 786440 | tf_op jit(solution)/shard_map/ppermute | solution.py:430
  604.3 33.1 %collective-permute-start.67 = (bf16[128,1024]{1,0:T(8,128)(2,1)S(1)}, bf16[128,1024]{1,0:T(8,128)(2,1)S(1)}, u32[]{:S(2)}, u32[]{:S(2)}) collective-permute-start(bf16[128,1024]{1,0:T(8,128)(2,1)S(1)} %fusion.35), channel_id=1, source_target_pairs={{0,1},{1,0},{2,3},{3,2},{4,5},{5,4},{6,7},{7,6},{8,9},{9,8},{10,11... | collective-permute-start | bytes 786440 | tf_op jit(solution)/shard_map/ppermute | solution.py:430
  605.7 43.8 %collective-permute-start.64 = (bf16[256,1024]{1,0:T(8,128)(2,1)S(1)}, bf16[256,1024]{1,0:T(8,128)(2,1)S(1)}, u32[]{:S(2)}, u32[]{:S(2)}) collective-permute-start(bf16[256,1024]{1,0:T(8,128)(2,1)S(1)} %fusion.16), channel_id=1, source_target_pairs={{0,16},{16,0},{1,17},{17,1},{2,18},{18,2},{3,19},{19,3},{4,20},{20... | collective-permute-start | bytes 1572872 | tf_op jit(solution)/shard_map/ppermute | solution.py:430
  658.5 50.8 %collective-permute-start.57 = (bf16[128,1024]{1,0:T(8,128)(2,1)S(1)}, bf16[128,1024]{1,0:T(8,128)(2,1)S(1)}, u32[]{:S(2)}, u32[]{:S(2)}) collective-permute-start(bf16[128,1024]{1,0:T(8,128)(2,1)S(1)} %get-tuple-element.90), channel_id=1, source_target_pairs={{0,16},{16,0},{1,17},{17,1},{2,18},{18,2},{3,19},{19,3},{4,20},{20... | collective-permute-start | bytes 786440 | tf_op jit(solution)/shard_map/ppermute | solution.py:430
  (108 other events, 1297.7 us)
Sparse Core Ops, SparseCore 0:
  556.6 85.6 all-gather.4
  650.9 133.6 all-gather.6

commit v3 on v2

--- a/solution.py
+++ b/solution.py
@@ -9,6 +9,7 @@
 from jax.sharding import Mesh
 from jax.sharding import PartitionSpec as P
 
+EPS = 1e-06
 NEG = -1e30
 
 
@@ -65,17 +66,19 @@
 
 
 def attend_kernel(place_ref, seq_ref, kslot_ref, *refs, heads, head_size, blk, per, chunk, scale, pieces):
-    q_ref, refs = refs[0], refs[1:]
+    (q_ref, wo_ref), refs = refs[:2], refs[2:]
     k_refs, v_refs, refs = refs[:pieces], refs[pieces : 2 * pieces], refs[2 * pieces :]
-    o_ref, lse_ref, q_s, k_s, v_s, o_s, sems = refs
+    o_ref, lse_ref, mine_ref, send_ref, q_s, k_s, v_s, o_s, wo_s, part_s, low_s, sems = refs
     nq = q_s.shape[0] // blk
     rows = per * blk
     take([q_ref], q_s, sems.at[0], blk, lambda i: place_ref[i])
     take(k_refs, k_s, sems.at[1], blk, lambda i: kslot_ref[i])
     take(v_refs, v_s, sems.at[2], blk, lambda i: kslot_ref[i])
+    pltpu.make_async_copy(wo_ref, wo_s, sems.at[3]).start()
     finish(q_s, sems.at[0])
     finish(k_s, sems.at[1])
     finish(v_s, sems.at[2])
+    finish(wo_s, sems.at[3])
 
     def tile_body(tile, carry):
         base = pl.multiple_of(tile * rows, rows)
@@ -115,10 +118,18 @@
         for h, (top, total, acc) in enumerate(states):
             o_s[pl.ds(base, rows), windows[h]] = (acc / total).T.astype(o_s.dtype)
             lse_ref[pl.ds(tile * heads + h, 1), :] = top + jnp.log(total)
+        part = dot(o_s[pl.ds(base, rows), :], wo_s[...], 1, 0)
+        part_s[pl.ds(base, rows), :] = part
+        low_s[pl.ds(base, rows), :] = part.astype(low_s.dtype)
         return carry
 
     lax.fori_loop(0, nq // per, tile_body, 0)
+    half = nq // 2
+    give(part_s, [mine_ref], sems.at[1], blk, lambda i: place_ref[i])
+    give(low_s, [send_ref], sems.at[2], blk, lambda i: place_ref[half + i])
     give(o_s, [o_ref], sems.at[0], blk, lambda i: place_ref[i])
+    finish(mine_ref, sems.at[1])
+    finish(send_ref, sems.at[2])
     finish(o_s, sems.at[0])
 
 
@@ -126,7 +137,7 @@
 WHOLE = pl.BlockSpec(memory_space=pltpu.VMEM)
 
 
-def attend(place, seq, kslot, q, ks, vs, heads, head_size, blk):
+def attend(place, seq, kslot, q, ks, vs, w_o, heads, head_size, blk):
     nq = q.shape[0] // blk
     per = min(4, nq)
     rows = per * blk
@@ -139,23 +150,28 @@
         out_shape=(
             jax.ShapeDtypeStruct(q.shape, q.dtype),
             jax.ShapeDtypeStruct((nq // per * heads, rows), jnp.float32),
+            jax.ShapeDtypeStruct((q.shape[0] // 2, w_o.shape[1]), jnp.float32),
+            jax.ShapeDtypeStruct((q.shape[0] // 2, w_o.shape[1]), q.dtype),
         ),
         grid_spec=pltpu.PrefetchScalarGridSpec(
             num_scalar_prefetch=3,
             grid=(),
-            in_specs=[ANY] * (1 + 2 * len(ks)),
-            out_specs=[ANY, WHOLE],
+            in_specs=[ANY] * (2 + 2 * len(ks)),
+            out_specs=[ANY, WHOLE, ANY, ANY],
             scratch_shapes=[
                 pltpu.VMEM(q.shape, q.dtype),
                 pltpu.VMEM((keys, q.shape[1]), q.dtype),
                 pltpu.VMEM((keys, q.shape[1]), q.dtype),
                 pltpu.VMEM(q.shape, q.dtype),
-                pltpu.SemaphoreType.DMA((3,)),
+                pltpu.VMEM(w_o.shape, q.dtype),
+                pltpu.VMEM((q.shape[0], w_o.shape[1]), jnp.float32),
+                pltpu.VMEM((q.shape[0], w_o.shape[1]), q.dtype),
+                pltpu.SemaphoreType.DMA((4,)),
             ],
         ),
         compiler_params=pltpu.CompilerParams(vmem_limit_bytes=58 * 1024 * 1024),
         name="attend",
-    )(place, seq, kslot, q, *ks, *vs)
+    )(place, seq, kslot, q, w_o, *ks, *vs)
 
 
 def attend_back_kernel(
@@ -279,35 +295,55 @@
     return jnp.concatenate(parts, axis=1)
 
 
-def prepare_kernel(pre_ref, recip_ref, gain_ref, cos_ref, sin_ref, q_ref, k_ref, *, heads, head_size):
+def column(row):
+    return jnp.broadcast_to(row, (8, row.shape[1])).T[:, :1]
+
+
+def reciprocal_root(sums_ref, i, width):
+    return column(lax.rsqrt(sums_ref[i : i + 1, :] / width + EPS))
+
+
+def prepare_kernel(pre_ref, sums_ref, gain_ref, cos_ref, sin_ref, q_ref, k_ref, *, heads, head_size, width):
     wide = heads * head_size
     for i, out in enumerate((q_ref, k_ref)):
-        x = pre_ref[:, i * wide : (i + 1) * wide] * recip_ref[:, i : i + 1] * gain_ref[i : i + 1, :]
+        recip = reciprocal_root(sums_ref, i, width)
+        x = pre_ref[:, i * wide : (i + 1) * wide] * recip * gain_ref[i : i + 1, :]
         out[...] = rotate(x, cos_ref[...], sin_ref[...], heads, head_size).astype(out.dtype)
 
 
-def prepare(pre, recip, gain, cosine, sine, heads, head_size):
+def by_row(step, n):
+    return pl.BlockSpec((step, n), lambda i, *_: (i, 0))
+
+
+def by_lane(step):
+    return pl.BlockSpec((2, step), lambda i, *_: (0, i))
+
+
+def fixed(rows, cols):
+    return pl.BlockSpec((rows, cols), lambda i, *_: (0, 0))
+
+
+TILE = 256
+
+
+def prepare(pre, sums, gain, cosine, sine, heads, head_size, width):
     rows, wide = pre.shape[0], heads * head_size
-    step = 256
     return pl.pallas_call(
-        functools.partial(prepare_kernel, heads=heads, head_size=head_size),
+        functools.partial(prepare_kernel, heads=heads, head_size=head_size, width=width),
         out_shape=(jax.ShapeDtypeStruct((rows, wide), jnp.bfloat16),) * 2,
-        grid=(rows // step,),
+        grid=(rows // TILE,),
         in_specs=[
-            pl.BlockSpec((step, 2 * wide), lambda i: (i, 0)),
-            pl.BlockSpec((step, 2), lambda i: (i, 0)),
-            pl.BlockSpec((2, wide), lambda i: (0, 0)),
-            pl.BlockSpec((step, head_size), lambda i: (i, 0)),
-            pl.BlockSpec((step, head_size), lambda i: (i, 0)),
+            by_row(TILE, 2 * wide), by_lane(TILE), fixed(2, wide),
+            by_row(TILE, head_size), by_row(TILE, head_size),
         ],
-        out_specs=[pl.BlockSpec((step, wide), lambda i: (i, 0))] * 2,
+        out_specs=[by_row(TILE, wide)] * 2,
         name="prepare",
-    )(pre, recip, gain, cosine, sine)
+    )(pre, sums, gain, cosine, sine)
 
 
 def unturn_kernel(
-    dq_ref, dka_ref, dkb_ref, pre_ref, recip_ref, gain_ref, cos_ref, sin_ref,
-    ds_ref, sum_ref, gg_ref, *, heads, head_size
+    dq_ref, dka_ref, dkb_ref, pre_ref, sums_ref, gain_ref, cos_ref, sin_ref,
+    ds_ref, sum_ref, gg_ref, *, heads, head_size, width
 ):
     wide = heads * head_size
     dk = dka_ref[...] + dkb_ref[...].astype(jnp.float32)
@@ -318,34 +354,388 @@
 
     for i, d in enumerate((dq_ref[...], dk)):
         cols = slice(i * wide, (i + 1) * wide)
+        recip = reciprocal_root(sums_ref, i, width)
         n = rotate(d, cos_ref[...], -sin_ref[...], heads, head_size)
         pre = pre_ref[:, cols]
-        gg_ref[i : i + 1, :] += jnp.sum(n * pre * recip_ref[:, i : i + 1], axis=0, keepdims=True)
+        gg_ref[i : i + 1, :] += jnp.sum(n * pre * recip, axis=0, keepdims=True)
         scaled = n * gain_ref[i : i + 1, :]
         ds_ref[:, cols] = scaled
         sum_ref[i : i + 1, :] = jnp.sum((scaled * pre).T, axis=0, keepdims=True)
 
 
-def unturn(dq, dka, dkb, pre, recip, gain, cosine, sine, heads, head_size):
+def unturn(dq, dka, dkb, pre, sums, gain, cosine, sine, heads, head_size, width):
     rows, wide = pre.shape[0], heads * head_size
-    step = 256
-    by_row = lambda n: pl.BlockSpec((step, n), lambda i: (i, 0))
-    fixed = pl.BlockSpec((2, wide), lambda i: (0, 0))
     return pl.pallas_call(
-        functools.partial(unturn_kernel, heads=heads, head_size=head_size),
+        functools.partial(unturn_kernel, heads=heads, head_size=head_size, width=width),
         out_shape=(
             jax.ShapeDtypeStruct((rows, 2 * wide), jnp.float32),
             jax.ShapeDtypeStruct((2, rows), jnp.float32),
             jax.ShapeDtypeStruct((2, wide), jnp.float32),
         ),
-        grid=(rows // step,),
+        grid=(rows // TILE,),
         in_specs=[
-            by_row(wide), by_row(wide), by_row(wide), by_row(2 * wide), by_row(2), fixed,
-            by_row(head_size), by_row(head_size),
+            by_row(TILE, wide), by_row(TILE, wide), by_row(TILE, wide), by_row(TILE, 2 * wide),
+            by_lane(TILE), fixed(2, wide), by_row(TILE, head_size), by_row(TILE, head_size),
         ],
-        out_specs=[by_row(2 * wide), pl.BlockSpec((2, step), lambda i: (0, i)), fixed],
+        out_specs=[by_row(TILE, 2 * wide), by_lane(TILE), fixed(2, wide)],
         name="unturn",
-    )(dq, dka, dkb, pre, recip, gain, cosine, sine)
+    )(dq, dka, dkb, pre, sums, gain, cosine, sine)
+
+
+def fetch(refs, dst, sems):
+    base = 0
+    for ref in refs:
+        rows = ref.shape[0]
+        pltpu.make_async_copy(ref, dst.at[pl.ds(base, rows), :], sems.at[base // TILE]).start()
+        base += rows
+
+
+def arrive(dst, sems, tile):
+    finish(dst.at[pl.ds(pl.multiple_of(tile * TILE, TILE), TILE), :], sems.at[tile])
+
+
+def tile_rows(tile):
+    return pl.ds(pl.multiple_of(tile * TILE, TILE), TILE)
+
+
+def place_quarters(refs, dst, sem, cols, row_of):
+    for j, ref in enumerate(refs):
+        for s in range(ref.shape[0]):
+            rows = ref.shape[1]
+            row = pl.multiple_of(row_of(j // 2, j % 2, s) * rows, rows)
+            pltpu.make_async_copy(ref.at[s, :, pl.ds(0, cols)], dst.at[pl.ds(row, rows), :], sem).start()
+
+
+def project_kernel(me_ref, *refs, wide):
+    x_refs, w_refs, refs = refs[:8], refs[8:12], refs[12:]
+    pre_ref, v_ref, sum_ref, w_ref, x_s, x_sems, w_sem = refs
+    tile = pl.program_id(0)
+
+    @pl.when(tile == 0)
+    def _():
+        place_quarters(
+            w_refs, w_ref, w_sem, 3 * wide,
+            lambda jx, jy, s: (((s // 2) * 2 + (jy ^ me_ref[0])) * 2 + s % 2) * 2 + (jx ^ me_ref[1]),
+        )
+        fetch(x_refs, x_s, x_sems)
+        finish(w_ref, w_sem)
+
+    arrive(x_s, x_sems, tile)
+    p = dot(x_s[tile_rows(tile), :], w_ref[...], 1, 0)
+    pre_ref[...] = p[:, : 2 * wide]
+    v_ref[...] = p[:, 2 * wide :].astype(v_ref.dtype)
+    for i in range(2):
+        part = p[:, i * wide : (i + 1) * wide]
+        sum_ref[i : i + 1, :] = jnp.sum((part * part).T, axis=0, keepdims=True)
+
+
+def project(me, xs, ws, wide):
+    rows, d = xs[0].shape[0] * 8, xs[0].shape[1]
+    bf16, f32 = xs[0].dtype, jnp.float32
+    return pl.pallas_call(
+        functools.partial(project_kernel, wide=wide),
+        out_shape=(
+            jax.ShapeDtypeStruct((rows, 2 * wide), f32),
+            jax.ShapeDtypeStruct((rows, wide), bf16),
+            jax.ShapeDtypeStruct((2, rows), f32),
+            jax.ShapeDtypeStruct((d, 3 * wide), bf16),
+        ),
+        grid_spec=pltpu.PrefetchScalarGridSpec(
+            num_scalar_prefetch=1,
+            grid=(rows // TILE,),
+            in_specs=[ANY] * 12,
+            out_specs=[by_row(TILE, 2 * wide), by_row(TILE, wide), by_lane(TILE), fixed(d, 3 * wide)],
+            scratch_shapes=[
+                pltpu.VMEM((rows, d), bf16),
+                pltpu.SemaphoreType.DMA((rows // TILE,)),
+                pltpu.SemaphoreType.DMA,
+            ],
+        ),
+        name="project",
+    )(me, *xs, *ws)
+
+
+def halves(tile, tiles, part, mine_ref, send_ref):
+    @pl.when(tile < tiles // 2)
+    def _():
+        mine_ref[...] = part
+
+    @pl.when(tile >= tiles // 2)
+    def _():
+        send_ref[...] = part.astype(send_ref.dtype)
+
+
+def half_specs(tiles, cols):
+    half = tiles // 2
+    return [
+        pl.BlockSpec((TILE, cols), lambda i, *_: (jnp.minimum(i, half - 1), 0)),
+        pl.BlockSpec((TILE, cols), lambda i, *_: (jnp.maximum(i - half, 0), 0)),
+    ]
+
+
+def half_shapes(rows, cols):
+    return [
+        jax.ShapeDtypeStruct((rows // 2, cols), jnp.float32),
+        jax.ShapeDtypeStruct((rows // 2, cols), jnp.bfloat16),
+    ]
+
+
+def expand_kernel(me_ref, *refs, units, tiles):
+    x_refs, w_refs, d_refs, refs = refs[:8], refs[8:12], refs[12:16], refs[16:]
+    gu_ref, hid_ref, mine_ref, send_ref, w_ref, d_ref, x_s, x_sems, w_sems = refs
+    tile = pl.program_id(0)
+
+    @pl.when(tile == 0)
+    def _():
+        place_quarters(
+            w_refs, w_ref, w_sems.at[0], 2 * units,
+            lambda jx, jh, s: (((s // 8) * 2 + (jh ^ me_ref[0])) * 8 + s % 8) * 2 + (jx ^ me_ref[1]),
+        )
+        fetch(x_refs, x_s, x_sems)
+        place_quarters(
+            d_refs, d_ref, w_sems.at[1], d_ref.shape[1],
+            lambda jx, jh, s: (s * 2 + (jh ^ me_ref[0])) * 2 + (jx ^ me_ref[1]),
+        )
+        finish(w_ref, w_sems.at[0])
+
+    arrive(x_s, x_sems, tile)
+    p = dot(x_s[tile_rows(tile), :], w_ref[...], 1, 0)
+    gu_ref[...] = p
+    gate = p[:, :units]
+    hidden = (gate * jax.nn.sigmoid(gate) * p[:, units:]).astype(hid_ref.dtype)
+    hid_ref[...] = hidden
+
+    @pl.when(tile == 0)
+    def _():
+        finish(d_ref, w_sems.at[1])
+
+    halves(tile, tiles, dot(hidden, d_ref[...], 1, 0), mine_ref, send_ref)
+
+
+def expand(me, xs, ws, ds, units):
+    rows, d = xs[0].shape[0] * 8, xs[0].shape[1]
+    tiles = rows // TILE
+    bf16, f32 = xs[0].dtype, jnp.float32
+    return pl.pallas_call(
+        functools.partial(expand_kernel, units=units, tiles=tiles),
+        out_shape=(
+            jax.ShapeDtypeStruct((rows, 2 * units), f32),
+            jax.ShapeDtypeStruct((rows, units), bf16),
+            *half_shapes(rows, d),
+            jax.ShapeDtypeStruct((d, 2 * units), bf16),
+            jax.ShapeDtypeStruct((units, d), bf16),
+        ),
+        grid_spec=pltpu.PrefetchScalarGridSpec(
+            num_scalar_prefetch=1,
+            grid=(tiles,),
+            in_specs=[ANY] * 16,
+            out_specs=[
+                by_row(TILE, 2 * units), by_row(TILE, units), *half_specs(tiles, d),
+                fixed(d, 2 * units), fixed(units, d),
+            ],
+            scratch_shapes=[
+                pltpu.VMEM((rows, d), bf16),
+                pltpu.SemaphoreType.DMA((tiles,)),
+                pltpu.SemaphoreType.DMA((2,)),
+            ],
+        ),
+        name="expand",
+    )(me, *xs, *ws, *ds)
+
+
+def contract_kernel(gu_ref, w_ref, d_ref, *refs, units, tiles):
+    x_refs, refs = refs[:8], refs[8:]
+    dgu_ref, mine_ref, send_ref, x_s, x_sems = refs
+    tile = pl.program_id(0)
+
+    @pl.when(tile == 0)
+    def _():
+        fetch(x_refs, x_s, x_sems)
+
+    arrive(x_s, x_sems, tile)
+    dh = dot(x_s[tile_rows(tile), :], d_ref[...], 1, 1)
+    gate, up = gu_ref[:, :units], gu_ref[:, units:]
+    sig = jax.nn.sigmoid(gate)
+    d_gate = (dh * up * sig * (1.0 + gate * (1.0 - sig))).astype(dgu_ref.dtype)
+    d_up = (dh * (gate * sig)).astype(dgu_ref.dtype)
+    dgu_ref[:, :units] = d_gate
+    dgu_ref[:, units:] = d_up
+    part = dot(d_gate, w_ref[:, :units], 1, 1) + dot(d_up, w_ref[:, units:], 1, 1)
+    halves(tile, tiles, part, mine_ref, send_ref)
+
+
+def contract(gu, w_gu, w_d, xs):
+    units, d = w_d.shape
+    rows = gu.shape[0]
+    tiles = rows // TILE
+    bf16 = w_d.dtype
+    return pl.pallas_call(
+        functools.partial(contract_kernel, units=units, tiles=tiles),
+        out_shape=(jax.ShapeDtypeStruct((rows, 2 * units), bf16), *half_shapes(rows, d)),
+        grid=(tiles,),
+        in_specs=[by_row(TILE, 2 * units), fixed(d, 2 * units), fixed(units, d)] + [ANY] * 8,
+        out_specs=[by_row(TILE, 2 * units), *half_specs(tiles, d)],
+        scratch_shapes=[pltpu.VMEM((rows, d), bf16), pltpu.SemaphoreType.DMA((tiles,))],
+        name="contract",
+    )(gu, w_gu, w_d, *xs)
+
+
+def outer_halves(a, b, me, keep_ref, send_ref):
+    half = a.shape[1] // 2
+    window = lambda i: a[:, pl.ds(pl.multiple_of(i * half, half), half)]
+    keep_ref[...] = dot(window(me), b[...], 0, 0)
+    send_ref[...] = dot(window(1 - me), b[...], 0, 0).astype(send_ref.dtype)
+
+
+def grads_kernel(me_ref, hid_ref, dgu_ref, *refs):
+    x_refs, g_refs, refs = refs[:8], refs[8:16], refs[16:]
+    keep_gu, send_gu, keep_d, send_d, x_s, g_s, sems = refs
+    base = 0
+    for x_ref, g_ref in zip(x_refs, g_refs):
+        rows = x_ref.shape[0]
+        pltpu.make_async_copy(x_ref, x_s.at[pl.ds(base, rows), :], sems.at[0]).start()
+        pltpu.make_async_copy(g_ref, g_s.at[pl.ds(base, rows), :], sems.at[1]).start()
+        base += rows
+    finish(x_s, sems.at[0])
+    outer_halves(x_s, dgu_ref, me_ref[0], keep_gu, send_gu)
+    finish(g_s, sems.at[1])
+    outer_halves(hid_ref, g_s, me_ref[0], keep_d, send_d)
+
+
+def split_shapes(rows, cols):
+    return [
+        jax.ShapeDtypeStruct((rows // 2, cols), jnp.float32),
+        jax.ShapeDtypeStruct((rows // 2, cols), jnp.bfloat16),
+    ]
+
+
+def grads(me, hidden, d_gu, xs, gs):
+    rows, units = hidden.shape
+    d = xs[0].shape[1]
+    bf16 = hidden.dtype
+    return pl.pallas_call(
+        grads_kernel,
+        out_shape=(*split_shapes(d, 2 * units), *split_shapes(units, d)),
+        grid_spec=pltpu.PrefetchScalarGridSpec(
+            num_scalar_prefetch=1,
+            grid=(),
+            in_specs=[WHOLE, WHOLE] + [ANY] * 16,
+            out_specs=[WHOLE] * 4,
+            scratch_shapes=[
+                pltpu.VMEM((rows, d), bf16),
+                pltpu.VMEM((rows, d), bf16),
+                pltpu.SemaphoreType.DMA((2,)),
+            ],
+        ),
+        compiler_params=pltpu.CompilerParams(vmem_limit_bytes=40 * 1024 * 1024),
+        name="grads",
+    )(me, hidden, d_gu, *xs, *gs)
+
+
+def project_back_kernel(me_ref, o_ref, w_ref, *refs):
+    g_refs, refs = refs[:8], refs[8:]
+    do_ref, keep_ref, send_ref, g_s, sem = refs
+    base = 0
+    for g_ref in g_refs:
+        pltpu.make_async_copy(g_ref, g_s.at[pl.ds(base, g_ref.shape[0]), :], sem).start()
+        base += g_ref.shape[0]
+    finish(g_s, sem)
+    do_ref[...] = dot(g_s[...], w_ref[...], 1, 1).astype(do_ref.dtype)
+    outer_halves(o_ref, g_s, me_ref[0], keep_ref, send_ref)
+
+
+def project_back(me, attended, w_o, gs):
+    rows, wide = attended.shape
+    d = w_o.shape[1]
+    bf16 = w_o.dtype
+    return pl.pallas_call(
+        project_back_kernel,
+        out_shape=(jax.ShapeDtypeStruct((rows, wide), bf16), *split_shapes(wide, d)),
+        grid_spec=pltpu.PrefetchScalarGridSpec(
+            num_scalar_prefetch=1,
+            grid=(),
+            in_specs=[WHOLE, WHOLE] + [ANY] * 8,
+            out_specs=[WHOLE] * 3,
+            scratch_shapes=[pltpu.VMEM((rows, d), bf16), pltpu.SemaphoreType.DMA],
+        ),
+        name="project_back",
+    )(me, attended, w_o, *gs)
+
+
+def norms_back_kernel(
+    me_ref, ds_ref, sums_ref, dsums_ref, pre_ref, dva_ref, dvb_ref, *refs, wide, width, tiles
+):
+    x_refs, refs = refs[:8], refs[8:]
+    dqkv_ref, keep_ref, send_ref, x_s, acc_s, x_sems = refs
+    tile = pl.program_id(0)
+
+    @pl.when(tile == 0)
+    def _():
+        fetch(x_refs, x_s, x_sems)
+        acc_s[...] = jnp.zeros_like(acc_s)
+
+    for i in range(2):
+        cols = slice(i * wide, (i + 1) * wide)
+        recip = reciprocal_root(sums_ref, i, width)
+        total = column(dsums_ref[i : i + 1, :])
+        value = recip * ds_ref[:, cols] - pre_ref[:, cols] * (recip * recip * recip) * total / width
+        dqkv_ref[:, cols] = value.astype(dqkv_ref.dtype)
+    dv = dva_ref[...] + dvb_ref[...].astype(jnp.float32)
+    dqkv_ref[:, 2 * wide :] = dv.astype(dqkv_ref.dtype)
+    arrive(x_s, x_sems, tile)
+    acc_s[...] += dot(x_s[tile_rows(tile), :], dqkv_ref[...], 0, 0)
+
+    @pl.when(tile == tiles - 1)
+    def _():
+        half = acc_s.shape[0] // 2
+        window = lambda i: acc_s[pl.ds(pl.multiple_of(i * half, half), half), :]
+        keep_ref[...] = window(me_ref[0])
+        send_ref[...] = window(1 - me_ref[0]).astype(send_ref.dtype)
+
+
+def norms_back(me, d_scaled, sums, dsums, pre, dva, dvb, xs, width):
+    rows, wide = dva.shape
+    d = xs[0].shape[1]
+    tiles = rows // TILE
+    bf16 = jnp.bfloat16
+    half = d // 2
+    return pl.pallas_call(
+        functools.partial(norms_back_kernel, wide=wide, width=width, tiles=tiles),
+        out_shape=(jax.ShapeDtypeStruct((rows, 3 * wide), bf16), *split_shapes(d, 3 * wide)),
+        grid_spec=pltpu.PrefetchScalarGridSpec(
+            num_scalar_prefetch=1,
+            grid=(tiles,),
+            in_specs=[
+                by_row(TILE, 2 * wide), by_lane(TILE), by_lane(TILE), by_row(TILE, 2 * wide),
+                by_row(TILE, wide), by_row(TILE, wide),
+            ] + [ANY] * 8,
+            out_specs=[by_row(TILE, 3 * wide), fixed(half, 3 * wide), fixed(half, 3 * wide)],
+            scratch_shapes=[
+                pltpu.VMEM((rows, d), bf16),
+                pltpu.VMEM((d, 3 * wide), jnp.float32),
+                pltpu.SemaphoreType.DMA((tiles,)),
+            ],
+        ),
+        name="norms_back",
+    )(me, d_scaled, sums, dsums, pre, dva, dvb, *xs)
+
+
+def inputs_back_kernel(g_ref, w_ref, mine_ref, send_ref, *, tiles):
+    halves(pl.program_id(0), tiles, dot(g_ref[...], w_ref[...], 1, 1), mine_ref, send_ref)
+
+
+def inputs_back(g, w):
+    rows, cols = g.shape
+    d = w.shape[0]
+    tiles = rows // TILE
+    return pl.pallas_call(
+        functools.partial(inputs_back_kernel, tiles=tiles),
+        out_shape=tuple(half_shapes(rows, d)),
+        grid=(tiles,),
+        in_specs=[by_row(TILE, cols), fixed(d, cols)],
+        out_specs=half_specs(tiles, d),
+        name="inputs_back",
+    )(g, w)
 
 
 def unpack_kernel(src_ref, *refs, plan, pieces, cover):
@@ -404,7 +794,6 @@
     )(src)
 
 
-EPS = 1e-06
 THETA = 500000.0
 HD = 128
 
@@ -430,29 +819,32 @@
     return lax.ppermute(value, axes, [(i, i ^ last) for i in range(last + 1)])
 
 
+def after(value, *others):
+    return lax.optimization_barrier((value, others))[0]
+
+
 def gather8(x, a, b):
-    mine = jnp.stack([x, flip(x, b), flip(x, a), flip(x, a, b)])
-    other = flip(mine, "c")
-    return jnp.concatenate([mine, other]).reshape(8 * x.shape[0], x.shape[1])
-
-
-def scatter8(x, a, b):
-    bf16 = jnp.bfloat16
-    parts = x.astype(bf16).reshape(2, 4, x.shape[0] // 8, x.shape[1])
-    mine = x.reshape(parts.shape)[0] + flip(parts[1], "c").astype(jnp.float32)
-    out = mine.astype(bf16)
+    own = [x, flip(x, b), flip(x, a), flip(x, a, b)]
+    return own + [flip(v, "c") for v in own]
+
+
+def scatter8(own, send, a, b):
+    f32, bf16 = jnp.float32, jnp.bfloat16
+    own = (own + flip(send, "c").astype(f32)).reshape(4, own.shape[0] // 4, own.shape[1])
+    out = own.astype(bf16)
     return (
-        mine[0]
-        + flip(out[1], b).astype(jnp.float32)
-        + flip(out[2], a).astype(jnp.float32)
-        + flip(out[3], a, b).astype(jnp.float32)
+        own[0]
+        + flip(out[1], b).astype(f32)
+        + flip(out[2], a).astype(f32)
+        + flip(out[3], a, b).astype(f32)
     )
 
 
 def sum8(x, a, b):
-    t = x.reshape((2, 2, 2) + x.shape[1:])
-    for axis, name in enumerate(("c", a, b)):
-        t = t + jnp.flip(flip(t, name), axis)
+    t = x.reshape(2, 8, -1)
+    for bit, name in ((4, "c"), (2, a), (1, b)):
+        got = flip(t.reshape(16, -1), name).reshape(t.shape)
+        t = t + jnp.concatenate([got[:, k ^ bit : (k ^ bit) + 1] for k in range(8)], axis=1)
     return t.reshape(x.shape)
 
 
@@ -460,9 +852,13 @@
     return jnp.where(lax.axis_index(name) == 1, jnp.flip(value, axis), value)
 
 
+def quarters(x, a, b):
+    first = flip(x, a)
+    return [x, first, flip(x, b), flip(first, b)]
+
+
 def gather4(x, a, b):
-    pair = jnp.stack([x, flip(x, a)])
-    quad = jnp.stack([pair, flip(pair, b)])
+    quad = jnp.stack(quarters(x, a, b)).reshape((2, 2) + x.shape)
     return in_order(in_order(quad, 1, a), 0, b)
 
 
@@ -516,15 +912,14 @@
         axis=2,
     )
     payload = lax.all_to_all(payload, ("h", "l", "c"), 0, 0, tiled=True)
-    payload = gather4(payload, "y", "x")
+    w_pieces = quarters(payload, "y", "x")
+    gains = jnp.stack([p[:, :, 3 * wide :] for p in w_pieces])
     if outer > 1:
-        payload = lax.all_gather(payload, "o", axis=0)
-    else:
-        payload = payload[None]
-    payload = payload.reshape(outer, 2, 2, 2, 2, 2, drows, 3 * wide + 128)
-    payload = payload.transpose(0, 3, 4, 2, 5, 1, 6, 7).reshape(d, 3 * wide + 128)
-    w_qkv = payload[:, : 3 * wide]
-    gains = payload[:, 3 * wide :].reshape(devices, drows * 128)
+        w_pieces = [lax.all_gather(p, "o", axis=0, tiled=True) for p in w_pieces]
+        gains = lax.all_gather(gains, "o", axis=0)
+    gains = gains.reshape(outer, 2, 2, 2, 2, 2, drows * 128)
+    gains = in_order(in_order(gains, 2, "y"), 1, "x").transpose(0, 3, 4, 2, 5, 1, 6)
+    gains = gains.reshape(devices, drows * 128)
     e_own, d_own = e // devices, d // devices
     full_gq = gains[:, :e_own].reshape(e)
     full_gk = gains[:, e_own : 2 * e_own].reshape(e)
@@ -552,18 +947,13 @@
     def by_unit(w):
         return w.reshape(drows, outer * 2, 8, unit).transpose(2, 0, 1, 3).reshape(8, drows, units)
 
-    ff = jnp.concatenate([by_unit(w_gate), by_unit(w_up)], axis=2)
+    ff = after(jnp.concatenate([by_unit(w_gate), by_unit(w_up)], axis=2), payload)
     ff = lax.all_to_all(ff, ("l", "y", "c"), 0, 0, tiled=True)
-    ff = gather4(ff, "h", "x")
-    w_d = gather4(w_down, "h", "x")
+    f_pieces = quarters(ff, "h", "x")
+    d_pieces = quarters(w_down[None], "h", "x")
     if outer > 1:
-        ff = lax.all_gather(ff, "o", axis=0)
-        w_d = lax.all_gather(w_d, "o", axis=0)
-    else:
-        ff, w_d = ff[None], w_d[None]
-    ff = ff.reshape(outer, 2, 2, 2, 2, 2, drows, 2 * units)
-    w_gu = ff.transpose(0, 2, 3, 4, 5, 1, 6, 7).reshape(d, 2 * units)
-    w_d = w_d.transpose(0, 2, 1, 3, 4).reshape(units, d)
+        f_pieces = [lax.all_gather(p, "o", axis=0, tiled=True) for p in f_pieces]
+        d_pieces = [lax.all_gather(p, "o", axis=0, tiled=True) for p in d_pieces]
 
     table = positions.reshape(outer, 2, 2, 2, 2, 2, rows)[..., ::blk] // blk
     for axis, name in enumerate(every):
@@ -584,50 +974,58 @@
     cosine = jnp.concatenate([cosine, cosine], axis=1)
     sine = jnp.concatenate([-sine, sine], axis=1)
 
-    xg = gather8(layer_input.astype(bf16), "h", "l")
-    group = xg.shape[0]
-    pre = jnp.dot(xg, w_qkv, preferred_element_type=f32)
-    pre_qk, value = pre[:, : 2 * wide], pre[:, 2 * wide :].astype(bf16)
-    squares = jnp.sum((pre_qk * pre_qk).reshape(group, 2, wide), axis=-1).T
-    squares = sum8(squares.reshape(2, 8, rows).transpose(1, 0, 2), "h", "l")
-    recip = lax.rsqrt(squares.transpose(1, 0, 2).reshape(2, group) / e + EPS).T
-    query, key = prepare(pre_qk, recip, gain_qk, cosine, sine, mine, HD)
+    me_yx = jnp.stack([index["y"], index["x"]]).astype(jnp.int32)
+    me_hx = jnp.stack([index["h"], index["x"]]).astype(jnp.int32)
+    me_x = me_yx[1:]
+    xs = gather8(layer_input.astype(bf16), "h", "l")
+    group = 8 * rows
+    pre, value, squares, w_qkv = project(me_yx, xs, w_pieces, wide)
+    squares = sum8(squares, "h", "l")
+    query, key = prepare(pre, squares, gain_qk, cosine, sine, mine, HD, e)
     key_y, value_x = flip(key, "y"), flip(value, "x")
     keys = [key, key_y, flip(key, "x"), flip(key_y, "x")]
     values = [value, flip(value, "y"), value_x, flip(value_x, "y")]
     if outer > 1:
         keys = [lax.all_gather(jnp.stack(keys), "o", axis=0).reshape(-1, wide)]
         values = [lax.all_gather(jnp.stack(values), "o", axis=0).reshape(-1, wide)]
-    attended, lse = attend(place, seq, kslot, query, keys, values, mine, HD, blk)
-    proj = scatter8(jnp.dot(attended, w_o, preferred_element_type=f32), "h", "l")
+    query = after(query, f_pieces, d_pieces)
+    attended, lse, own, send = attend(place, seq, kslot, query, keys, values, w_o, mine, HD, blk)
+    proj = scatter8(own, send, "h", "l")
     attn_branch, a_recip = norm_forward(proj, full_ga)
     mid = layer_input + attn_branch
 
-    mg = gather8(mid.astype(bf16), "l", "y")
-    gate_up = jnp.dot(mg, w_gu, preferred_element_type=f32)
-    gate, up = gate_up[:, :units], gate_up[:, units:]
-    sig = jax.nn.sigmoid(gate)
-    silu = gate * sig
-    hidden = (silu * up).astype(bf16)
-    down = scatter8(jnp.dot(hidden, w_d, preferred_element_type=f32), "l", "y")
+    ms = gather8(mid.astype(bf16), "l", "y")
+    gate_up, hidden, own, send, w_gu, w_d = expand(me_hx, ms, f_pieces, d_pieces, units)
+    down = scatter8(own, send, "l", "y")
     mlp_branch, m_recip = norm_forward(down, full_gm)
     output = mid + mlp_branch
     d_down_f, local_gm = norm_backward(down, m_recip, full_gm, grad_output)
-    dg = gather8(d_down_f.astype(bf16), "l", "y")
-    d_hidden = lax.dot_general(dg, w_d, (((1,), (1,)), ((), ())), preferred_element_type=f32)
-    d_gate = (d_hidden * up * sig * (1.0 + gate * (1.0 - sig))).astype(bf16)
-    d_up = (d_hidden * silu).astype(bf16)
-    d_gu = jnp.concatenate([d_gate, d_up], axis=1)
-    d_mid = grad_output + scatter8(
-        lax.dot_general(d_gu, w_gu, (((1,), (1,)), ((), ())), preferred_element_type=f32), "l", "y"
-    )
-    local_wd = lax.dot_general(hidden, dg, (((0,), (0,)), ((), ())), preferred_element_type=f32)
-    local_wgu = lax.dot_general(mg, d_gu, (((0,), (0,)), ((), ())), preferred_element_type=f32)
+    dgs = gather8(d_down_f.astype(bf16), "l", "y")
+    d_gu, own, send = contract(gate_up, w_gu, w_d, dgs)
+    d_mid = grad_output + scatter8(own, send, "l", "y")
+    keep_gu, send_gu, keep_d, send_d = grads(me_x, hidden, d_gu, ms, dgs)
+
+    ctx = ("o", "h", "l", "y", "c")
+
+    def settle(keep, send, a):
+        cols = keep.shape[1]
+        part = keep + flip(send, "x").astype(f32)
+        part = halve(part.reshape(2, -1, cols), a)
+        if outer > 1:
+            part = lax.psum_scatter(
+                part.astype(bf16).reshape(outer, -1, cols), "o", scatter_dimension=0, tiled=False
+            )
+        return part.astype(bf16)
+
+    part_gu, part_d = settle(keep_gu, send_gu, "h"), settle(keep_d, send_d, "h")
+    part_f = jnp.concatenate([part_gu, part_d]) if outer == 1 else part_gu
 
     d_proj_f, local_ga = norm_backward(proj, a_recip, full_ga, d_mid)
-    pg = gather8(d_proj_f.astype(bf16), "h", "l")
-    d_att = lax.dot_general(pg, w_o, (((1,), (1,)), ((), ())), preferred_element_type=f32).astype(bf16)
-    local_wo = lax.dot_general(attended, pg, (((0,), (0,)), ((), ())), preferred_element_type=f32)
+    pgs = gather8(d_proj_f.astype(bf16), "h", "l")
+    d_att, keep_o, send_o = project_back(me_x, attended, w_o, pgs)
+    d_att = after(d_att, part_f)
+    if outer == 1:
+        first = lax.all_gather(part_f, ctx, axis=0).reshape(16, -1, d)
     dq_rot, dk, dv = attend_back(
         place, seq, kslot, query, keys, values, attended, d_att, lse, mine, HD, blk
     )
@@ -641,38 +1039,16 @@
     dk_b = flip((dk[1].astype(f32) + flip(dk[3], "x").astype(f32)).astype(bf16), "y")
     dv_a = dv[0].astype(f32) + flip(dv[1], "y").astype(f32)
     dv_b = flip((dv[2].astype(f32) + flip(dv[3], "y").astype(f32)).astype(bf16), "x")
-    d_value = (dv_a + dv_b.astype(f32)).astype(bf16)
-    d_scaled, sums, local_gqk = unturn(
-        dq_rot, dk_a, dk_b, pre_qk, recip, gain_qk, cosine, sine, mine, HD
+    d_scaled, dsums, local_gqk = unturn(
+        dq_rot, dk_a, dk_b, pre, squares, gain_qk, cosine, sine, mine, HD, e
     )
-    sums = sum8(sums.reshape(2, 8, rows).transpose(1, 0, 2), "h", "l").transpose(1, 0, 2)
-    sums = sums.reshape(2, group).T
-    cubes = recip * recip * recip * sums / e
-    d_qk = (
-        recip[:, :, None] * d_scaled.reshape(group, 2, wide)
-        - pre_qk.reshape(group, 2, wide) * cubes[:, :, None]
-    ).astype(bf16)
-    d_qkv = jnp.concatenate([d_qk.reshape(group, 2 * wide), d_value], axis=1)
-    grad_input = d_mid + scatter8(
-        lax.dot_general(d_qkv, w_qkv, (((1,), (1,)), ((), ())), preferred_element_type=f32), "h", "l"
-    )
-    local_wqkv = lax.dot_general(xg, d_qkv, (((0,), (0,)), ((), ())), preferred_element_type=f32)
-
-    ctx = ("o", "h", "l", "y", "c")
-
-    def settle(local, a, b):
-        cols = local.shape[1]
-        part = halve(local.reshape(2, -1, cols), b)
-        part = halve(part.reshape(2, -1, cols), a)
-        if outer > 1:
-            part = lax.psum_scatter(
-                part.astype(bf16).reshape(outer, -1, cols), "o", scatter_dimension=0, tiled=False
-            )
-        return part.astype(bf16)
+    dsums = sum8(dsums, "h", "l")
+    d_qkv, keep_qkv, send_qkv = norms_back(me_x, d_scaled, squares, dsums, pre, dv_a, dv_b, xs, e)
+    own, send = inputs_back(d_qkv, w_qkv)
+    grad_input = d_mid + scatter8(own, send, "h", "l")
 
     half_d, half_f = d // 2, f // 2
-    part_gu, part_d, part_o = settle(local_wgu, "h", "x"), settle(local_wd, "h", "x"), settle(local_wo, "y", "x")
-    part_qkv = settle(local_wqkv, "y", "x")
+    part_o, part_qkv = settle(keep_o, send_o, "y"), settle(keep_qkv, send_qkv, "y")
     n_qk, n_am = wide, d
     lines = -(-max(n_qk, n_am) // (3 * wide))
     lines = -(-lines // 16) * 16
@@ -696,9 +1072,10 @@
     n_gu, n_d, n_o, n_qkv = part_gu.shape[0], part_d.shape[0], part_o.shape[0], part_qkv.shape[0] - lines
 
     if outer == 1:
-        first = lax.all_gather(jnp.concatenate([part_gu, part_d, part_o]), ctx, axis=0).reshape(16, -1, d)
+        part_qkv = after(part_qkv, first)
+        middle = lax.all_gather(after(part_o, first), ctx, axis=0).reshape(16, -1, d)
         last = lax.all_gather(part_qkv, ctx, axis=0).reshape(16, -1, 3 * wide)
-        plan_first, plan_last = [], []
+        plan_first, plan_middle, plan_last = [], [], []
         for p in range(16):
             h, l, y, c = p >> 3, (p >> 2) & 1, (p >> 1) & 1, p & 1
             team_f, team_q = 4 * l + 2 * y + c, 4 * h + 2 * l + c
@@ -710,8 +1087,8 @@
                 for m in range(2)
             ]
             downs = [((n_gu, n_d), (0, d), team_f * unit + h * n_d, 0)]
-            os = [((n_gu + n_d, n_o), (0, d), team_q * HD + y * n_o, 0)]
-            plan_first.append([*ups, downs, os])
+            plan_first.append([*ups, downs])
+            plan_middle.append([[((0, n_o), (0, d), team_q * HD + y * n_o, 0)]])
             plan_last.append(
                 [
                     [
@@ -721,9 +1098,10 @@
                     for m in range(3)
                 ]
             )
-        total_wg, total_wu, total_wd, total_wo = unpack(
-            first, [(half_d, f), (half_d, f), (half_f, d), (e // 2, d)], plan_first, n_gu + n_d + n_o
+        total_wg, total_wu, total_wd = unpack(
+            first, [(half_d, f), (half_d, f), (half_f, d)], plan_first, n_gu + n_d
         )
+        (total_wo,) = unpack(middle, [(e // 2, d)], plan_middle, n_o)
         total_wq, total_wk, total_wv = unpack(last, [(half_d, e)] * 3, plan_last, n_qkv)
         got_small = last[:, n_qkv:]
     else:

time: 819 us -> 782 us (0.955)
  waiting for transfers between devices: 495 us -> 430 us
  Pallas kernels: 77.9 us -> 135 us
  matrix products: 37.1 us -> 0 us
  local copies, waits for them, and re-layouts: 44.8 us -> 59.1 us
  other arithmetic: 54.9 us -> 42.9 us
    all_gather x1 -> x2, waiting for transfers between devices: 61.5 us -> 0.02 us  [the longest x1 0.02 us: layer(): lax.all_gather(after(part_o, first), ctx, axis=0).reshape(16, -1, d)]
    pallas_call x0 -> x7, Pallas kernels: none -> 51.7 us  [the longest x1 10.3 us: expand(): pl.pallas_call(functools.partial(expand_kernel, units=units, tiles=tiles)...]
    dot_general x12 -> x0, matrix products: 37.1 us -> none  [the longest x1 13.8 us: layer(): lax.dot_general(d_gu, w_gu, (((1,), (1,)), ((), ())), preferred_element_t...]
    unnamed x137 -> x204, local copies, waits for them, and re-layouts: 18.7 us -> 37.6 us
    all_gather x1, waiting for transfers between devices: 0.01 us -> 12.5 us  [layer(): last = lax.all_gather(part_qkv, ctx, axis=0).reshape(16, -1, 3 * wide)]
    ppermute x68 -> x84, waiting for transfers between devices: 409 us -> 398 us  [flip(): return lax.ppermute(value, axes, [(i, i ^ last) for i in range(last + 1)])]
    rev x1 -> x2, local copies, waits for them, and re-layouts: 0.04 us -> 10.5 us  [in_order(): return jnp.where(lax.axis_index(name) == 1, jnp.flip(value, axis), value)]
    reshape x5 -> x4, local copies, waits for them, and re-layouts: 10.5 us -> 0.47 us  [the longest x2 0.34 us: layer(): gains = gains.reshape(outer, 2, 2, 2, 2, 2, drows * 128)]
  transfers between devices with their start and end apart: 73 -> 90, of which waited for: 42 -> 51; matrix products, arithmetic and copies ran while one was open for 11% -> 6% of each run, Pallas kernels for 5% -> 10%
where the time goes in v3:
time: 782 us; the launch traced here: 773 us
  waiting for transfers between devices  430 us (55%)
  Pallas kernels  135 us (17%)
  starting transfers between devices  90.7 us (12%)
  local copies, waits for them, and re-layouts  59.1 us (8%)
  other arithmetic  42.9 us (5%)
  between operations  15.8 us (2%)
    ppermute x84, waiting for transfers between devices, flip(): return lax.ppermute(value, axes, [(i, i ^ last) for i in range(last + 1)])  398 us
    ppermute x84, starting transfers between devices, flip(): return lax.ppermute(value, axes, [(i, i ^ last) for i in range(last + 1)])  76.3 us
    unnamed x204, local copies, waits for them, and re-layouts  37.6 us
    pallas_call x1, Pallas kernels, attend_back(): pl.pallas_call(functools.partial(attend_back_kernel, heads=heads, head_si...  25.5 us
    pallas_call x3, Pallas kernels, unpack(): pl.pallas_call(functools.partial(unpack_kernel, plan=plan, pieces=pieces,...  24.6 us
    pallas_call x1, Pallas kernels, attend(): pl.pallas_call(functools.partial(attend_kernel, heads=heads, head_size=he...  22.8 us
    all_to_all x1, waiting for transfers between devices, layer(): payload = lax.all_to_all(payload, ('h', 'l', 'c'), 0, 0, tiled=True)  19.5 us
  transfers between devices with their start and end apart: 90, of which 51 were waited for; matrix products, arithmetic and copies ran while one was open for 6% of the time, Pallas kernels for 10%

profile of v3, /device:TPU:0, one launch (start us, length us, event | category | flops | bytes accessed | tf_op | source)
XLA Modules:
  0.0 772.9 jit_solution(10838908854529832103)
XLA Ops:
  26.2 19.5 %all-to-all-done.refs_8_ = bf16[8,32,896]{2,1,0:T(8,128)(2,1)S(1)} async-done(((bf16[8,32,896]{2,1,0:T(8,128)(2,1)}), bf16[8,32,896]{2,1,0:T(8,128)(2,1)S(1)}, u32[]{:S(2)}, u32[]{:S(2)}) %all-to-all-start) | async-done | bytes 458784 | tf_op jit(solution)/shard_map/all_to_all | solution.py:914
  74.5 10.4 %rev.42 = bf16[1,2,2,2,2,2,4096]{6,1,5,2,4,3,0:T(2,128)(2,1)} reverse(bf16[1,2,2,2,2,2,4096]{6,1,5,2,4,3,0:T(2,128)(2,1)S(1)} %broadcast_select_fusion), dimensions={1} | reverse | bytes 524288 | tf_op jit(solution)/shard_map/jit(_flip)/rev | solution.py:852
  101.4 23.5 %collective-permute-done.11 = f32[16,128]{1,0:T(8,128)S(1)} collective-permute-done((f32[16,128]{1,0:T(8,128)S(1)}, f32[16,128]{1,0:T(8,128)S(1)}, u32[]{:S(2)}, u32[]{:S(2)}) %collective-permute-start.11) | collective-permute-done | bytes 8224 | tf_op jit(solution)/shard_map/ppermute | solution.py:819
  141.7 33.8 %collective-permute-done.18.refs_15_ = bf16[1,128,1024]{2,1,0:T(8,128)(2,1)S(1)} collective-permute-done((bf16[1,128,1024]{2,1,0:T(8,128)(2,1)S(1)}, bf16[1,128,1024]{2,1,0:T(8,128)(2,1)S(1)}, u32[]{:S(2)}, u32[]{:S(2)}) %collective-permute-start.18) | collective-permute-done | bytes 262176 | tf_op jit(solution)/shard_map/ppermute | solution.py:819
  187.4 13.1 %collective-permute-done.26.refs_7_.refs_9_ = bf16[1024,256]{1,0:T(8,128)(2,1)S(1)} collective-permute-done((bf16[1024,256]{1,0:T(8,128)(2,1)S(1)}, bf16[1024,256]{1,0:T(8,128)(2,1)S(1)}, u32[]{:S(2)}, u32[]{:S(2)}) %collective-permute-start.26) | collective-permute-done | bytes 524320 | tf_op jit(solution)/shard_map/ppermute | solution.py:819
  200.6 11.1 %collective-permute-done.28.refs_9_.refs_11_ = bf16[1024,256]{1,0:T(8,128)(2,1)} collective-permute-done((bf16[1024,256]{1,0:T(8,128)(2,1)S(1)}, bf16[1024,256]{1,0:T(8,128)(2,1)}, u32[]{:S(2)}, u32[]{:S(2)}) %collective-permute-start.28) | collective-permute-done | bytes 524320 | tf_op jit(solution)/shard_map/ppermute | solution.py:819
  211.7 22.8 %attend.1 = (bf16[1024,256]{1,0:T(8,128)(2,1)}, f32[8,256]{1,0:T(8,128)}, f32[512,1024]{1,0:T(8,128)}, bf16[512,1024]{1,0:T(8,128)(2,1)}) custom-call(s32[16]{0:T(128)} %copy-done.92, s32[16]{0:T(128)} %select_reduce_fusion.seq_ref, s32[64]{0:T(128)} %reshape.287.kslot_ref, bf16[1024,256]{1,0:T(8,128)(2,1)} %get-tuple-element.71.refs_0_, ...), custom_call_target="tpu_custom_call" | custom-call | tf_op jit(solution)/shard_map/attend/pallas_call | solution.py:145
  257.1 11.0 %collective-permute-done.31 = bf16[128,1024]{1,0:T(8,128)(2,1)} collective-permute-done((bf16[128,1024]{1,0:T(8,128)(2,1)S(1)}, bf16[128,1024]{1,0:T(8,128)(2,1)}, u32[]{:S(2)}, u32[]{:S(2)}) %collective-permute-start.31) | collective-permute-done | bytes 262176 | tf_op jit(solution)/shard_map/ppermute | solution.py:819
  285.8 10.3 %expand.1 = (f32[1024,1024]{1,0:T(8,128)}, bf16[1024,512]{1,0:T(8,128)(2,1)}, f32[512,1024]{1,0:T(8,128)}, bf16[512,1024]{1,0:T(8,128)(2,1)}, bf16[1024,1024]{1,0:T(8,128)(2,1)}, /*index=5*/bf16[512,1024]{1,0:T(8,128)(2,1)}) custom-call(s32[2]{0:T(128)} %pad_add_fusion.1.me_ref, bf16[128,1024]{1,0:T(8,128)(2,1)} %copy-done.4, bf16[128,1024]{1,0:T(8,128)(2,1)} %copy-done.27, ...), custom_call_target="tpu_custom_call" | custom-call | tf_op jit(solution)/shard_map/expand/pallas_call | solution.py:519
  305.6 10.9 %collective-permute-done.41 = bf16[128,1024]{1,0:T(8,128)(2,1)S(1)} collective-permute-done((bf16[128,1024]{1,0:T(8,128)(2,1)}, bf16[128,1024]{1,0:T(8,128)(2,1)S(1)}, u32[]{:S(2)}, u32[]{:S(2)}) %collective-permute-start.41) | collective-permute-done | bytes 262176 | tf_op jit(solution)/shard_map/ppermute | solution.py:819
  335.7 10.3 %contract.1 = (bf16[1024,1024]{1,0:T(8,128)(2,1)}, f32[512,1024]{1,0:T(8,128)}, bf16[512,1024]{1,0:T(8,128)(2,1)}) custom-call(f32[1024,1024]{1,0:T(8,128)} %get-tuple-element.78.gu_ref, bf16[1024,1024]{1,0:T(8,128)(2,1)} %get-tuple-element.79.w_ref, bf16[512,1024]{1,0:T(8,128)(2,1)} %get-tuple-element.80.d_ref, bf16[128,1024]{1,0:T(8,128)(2,1)} %copy-done.2, ...), custom_call_target="tpu_custom_call" | custom-call | tf_op jit(solution)/shard_map/contract/pallas_call | solution.py:572
  370.0 34.8 %collective-permute-done.64 = bf16[256,1024]{1,0:T(8,128)(2,1)} collective-permute-done((bf16[256,1024]{1,0:T(8,128)(2,1)}, bf16[256,1024]{1,0:T(8,128)(2,1)}, u32[]{:S(2)}, u32[]{:S(2)}) %collective-permute-start.64) | collective-permute-done | bytes 524320 | tf_op jit(solution)/shard_map/ppermute | solution.py:819
  412.3 33.1 %collective-permute-done.65 = bf16[128,1024]{1,0:T(8,128)(2,1)S(1)} collective-permute-done((bf16[128,1024]{1,0:T(8,128)(2,1)S(1)}, bf16[128,1024]{1,0:T(8,128)(2,1)S(1)}, u32[]{:S(2)}, u32[]{:S(2)}) %collective-permute-start.65) | collective-permute-done | bytes 262176 | tf_op jit(solution)/shard_map/ppermute | solution.py:819
  456.4 14.8 %collective-permute-done.52 = bf16[128,1024]{1,0:T(8,128)(2,1)S(1)} collective-permute-done((bf16[128,1024]{1,0:T(8,128)(2,1)S(1)}, bf16[128,1024]{1,0:T(8,128)(2,1)S(1)}, u32[]{:S(2)}, u32[]{:S(2)}) %collective-permute-start.52) | collective-permute-done | bytes 262176 | tf_op jit(solution)/shard_map/ppermute | solution.py:819
  473.2 17.1 %collective-permute-done.53 = bf16[128,1024]{1,0:T(8,128)(2,1)S(1)} collective-permute-done((bf16[128,1024]{1,0:T(8,128)(2,1)S(1)}, bf16[128,1024]{1,0:T(8,128)(2,1)S(1)}, u32[]{:S(2)}, u32[]{:S(2)}) %collective-permute-start.53) | collective-permute-done | bytes 262176 | tf_op jit(solution)/shard_map/ppermute | solution.py:819
  502.7 29.1 %collective-permute-done.56.refs_2_ = bf16[128,1024]{1,0:T(8,128)(2,1)S(1)} collective-permute-done((bf16[128,1024]{1,0:T(8,128)(2,1)S(1)}, bf16[128,1024]{1,0:T(8,128)(2,1)S(1)}, u32[]{:S(2)}, u32[]{:S(2)}) %collective-permute-start.56) | collective-permute-done | bytes 262176 | tf_op jit(solution)/shard_map/ppermute | solution.py:819
  540.8 25.5 %attend_back.1 = (f32[1024,256]{1,0:T(8,128)}, bf16[1024,256]{1,0:T(8,128)(2,1)}, bf16[1024,256]{1,0:T(8,128)(2,1)}, bf16[1024,256]{1,0:T(8,128)(2,1)}, bf16[102...) custom-call(s32[16]{0:T(128)} %copy-done.92, ...), custom_call_target="tpu_custom_call" | custom-call | tf_op jit(solution)/shard_map/attend_back/pallas_call | solution.py:257
  625.6 8.6 %norms_back.1 = (bf16[1024,768]{1,0:T(8,128)(2,1)}, f32[512,768]{1,0:T(8,128)}, bf16[512,768]{1,0:T(8,128)(2,1)}) custom-call(s32[1]{0:T(128)} %bitcast.4.me_ref, f32[1024,512]{1,0:T(8,128)} %get-tuple-element.98.ds_ref, f32[2,1024]{1,0:T(2,128)} %bitcast_add_fusion.7.sums_ref, f32[2,1024]{1,0:T(2,128)} %bitcast_add_fusion.4.dsums_ref, ...), custom_call_target="tpu_custom_call" | custom-call | tf_op jit(solution)/shard_map/norms_back/pallas_call | solution.py:702
  636.1 15.7 %collective-permute-done.79 = bf16[512,768]{1,0:T(8,128)(2,1)S(1)} collective-permute-done((bf16[512,768]{1,0:T(8,128)(2,1)}, bf16[512,768]{1,0:T(8,128)(2,1)S(1)}, u32[]{:S(2)}, u32[]{:S(2)}) %collective-permute-start.79) | collective-permute-done | bytes 786464 | tf_op jit(solution)/shard_map/ppermute | solution.py:819
  682.3 8.7 %collective-permute-done.78 = bf16[128,1024]{1,0:T(8,128)(2,1)S(1)} collective-permute-done((bf16[128,1024]{1,0:T(8,128)(2,1)S(1)}, bf16[128,1024]{1,0:T(8,128)(2,1)S(1)}, u32[]{:S(2)}, u32[]{:S(2)}) %collective-permute-start.78) | collective-permute-done | bytes 262176 | tf_op jit(solution)/shard_map/ppermute | solution.py:819
  691.0 24.0 %collective-permute-done.77 = bf16[128,1024]{1,0:T(8,128)(2,1)S(1)} collective-permute-done((bf16[128,1024]{1,0:T(8,128)(2,1)S(1)}, bf16[128,1024]{1,0:T(8,128)(2,1)S(1)}, u32[]{:S(2)}, u32[]{:S(2)}) %collective-permute-start.77) | collective-permute-done | bytes 262176 | tf_op jit(solution)/shard_map/ppermute | solution.py:819
  721.4 10.3 %unpack.5 = (f32[512,4096]{1,0:T(8,128)}, f32[512,4096]{1,0:T(8,128)}, f32[2048,1024]{1,0:T(8,128)}) custom-call(bf16[16,384,1024]{2,1,0:T(8,128)(2,1)S(1)} %bitcast.159), custom_call_target="tpu_custom_call" | custom-call | tf_op jit(solution)/shard_map/unpack/pallas_call | solution.py:781
  739.6 12.5 %all-gather.9.cloned.1.call-done = bf16[4352,768]{1,0:T(8,128)(2,1)} async-done(((bf16[272,768]{1,0:T(8,128)(2,1)}), bf16[4352,768]{1,0:T(8,128)(2,1)}) %all-gather.9.cloned.1.call-update) | async-done | bytes 6684688 | tf_op jit(solution)/shard_map/all_gather | solution.py:1077
  756.6 8.0 %unpack.3 = (f32[512,2048]{1,0:T(8,128)}, f32[512,2048]{1,0:T(8,128)}, f32[512,2048]{1,0:T(8,128)}) custom-call(bf16[16,272,768]{2,1,0:T(8,128)(2,1)S(1)} %bitcast.161), custom_call_target="tpu_custom_call" | custom-call | tf_op jit(solution)/shard_map/unpack/pallas_call | solution.py:781
  (512 shorter events, 338.2 us)
Async XLA Ops:
  8.4 56.4 %collective-permute-start.2 = (bf16[128,1024]{1,0:T(8,128)(2,1)S(1)}, bf16[128,1024]{1,0:T(8,128)(2,1)S(1)}, u32[]{:S(2)}, u32[]{:S(2)}) collective-permute-start(bf16[128,1024]{1,0:T(8,128)(2,1)S(1)} %convert_element_type.236.refs_0_), channel_id=1, source_target_pairs={{0,24},{8,16},{16,8},{24,0},{1,25},{9,17},{17,9},{25,1},{2,26},{10... | collective-permute-start | bytes 786440 | tf_op jit(solution)/shard_map/ppermute | solution.py:819
  13.5 52.9 %collective-permute-start.1 = (bf16[128,1024]{1,0:T(8,128)(2,1)S(1)}, bf16[128,1024]{1,0:T(8,128)(2,1)S(1)}, u32[]{:S(2)}, u32[]{:S(2)}) collective-permute-start(bf16[128,1024]{1,0:T(8,128)(2,1)S(1)} %convert_element_type.236.refs_0_), channel_id=1, source_target_pairs={{0,16},{16,0},{1,17},{17,1},{2,18},{18,2},{3,19},{19,3},{4,20},{20... | collective-permute-start | bytes 786440 | tf_op jit(solution)/shard_map/ppermute | solution.py:819
  13.5 53.1 %collective-permute-start = (bf16[128,1024]{1,0:T(8,128)(2,1)S(1)}, bf16[128,1024]{1,0:T(8,128)(2,1)S(1)}, u32[]{:S(2)}, u32[]{:S(2)}) collective-permute-start(bf16[128,1024]{1,0:T(8,128)(2,1)S(1)} %convert_element_type.236.refs_0_), channel_id=1, source_target_pairs={{0,8},{8,0},{1,9},{9,1},{2,10},{10,2},{3,11},{11,3},{4,12},{12,4},... | collective-permute-start | bytes 786440 | tf_op jit(solution)/shard_map/ppermute | solution.py:819
  52.6 45.3 %all-to-all-start.1 = ((bf16[8,32,1024]{2,1,0:T(8,128)(2,1)}), bf16[8,32,1024]{2,1,0:T(8,128)(2,1)S(1)}, u32[]{:S(2)}, u32[]{:S(2)}) async-start(bf16[8,32,1024]{2,1,0:T(8,128)(2,1)} %pad_maximum_fusion.3), calls=%async_computation.1 | async-start | bytes 1048576 | tf_op jit(solution)/shard_map/all_to_all | solution.py:951
  56.1 579.1 %all-gather.7.cloned.1.call-start = ((), (), s32[]{:S(2)}) async-start(), calls=%async_computation.2 | async-start | bytes 13369344 | tf_op jit(solution)/shard_map/all_gather | solution.py:1028
  64.9 70.0 %collective-permute-start.20 = (bf16[64,1024]{1,0:T(8,128)(2,1)S(1)}, bf16[64,1024]{1,0:T(8,128)(2,1)}, u32[]{:S(2)}, u32[]{:S(2)}) collective-permute-start(bf16[64,1024]{1,0:T(8,128)(2,1)S(1)} %copy-done.89), channel_id=1, source_target_pairs={{0,1},{1,0},{2,3},{3,2},{4,5},{5,4},{6,7},{7,6},{8,9},{9,8},{10,11... | collective-permute-start | bytes 393224 | tf_op jit(solution)/shard_map/ppermute | solution.py:819
  85.7 39.4 %collective-permute-start.19 = (bf16[64,1024]{1,0:T(8,128)(2,1)S(1)}, bf16[64,1024]{1,0:T(8,128)(2,1)S(1)}, u32[]{:S(2)}, u32[]{:S(2)}) collective-permute-start(bf16[64,1024]{1,0:T(8,128)(2,1)S(1)} %copy-done.89), channel_id=1, source_target_pairs={{0,16},{16,0},{1,17},{17,1},{2,18},{18,2},{3,19},{19,3},{4,20},{20... | collective-permute-start | bytes 393224 | tf_op jit(solution)/shard_map/ppermute | solution.py:819
  85.7 51.2 %collective-permute-start.17 = (bf16[1,128,1024]{2,1,0:T(8,128)(2,1)}, bf16[1,128,1024]{2,1,0:T(8,128)(2,1)}, u32[]{:S(2)}, u32[]{:S(2)}) collective-permute-start(bf16[1,128,1024]{2,1,0:T(8,128)(2,1)} %bitcast.184), channel_id=1, source_target_pairs={{0,1},{1,0},{2,3},{3,2},{4,5},{5,4},{6,7},{7,6},{8,9},{9,8},{10,11... | collective-permute-start | bytes 786440 | tf_op jit(solution)/shard_map/ppermute | solution.py:819
  97.9 39.5 %collective-permute-start.13 = (bf16[8,32,1024]{2,1,0:T(8,128)(2,1)S(1)}, bf16[8,32,1024]{2,1,0:T(8,128)(2,1)}, u32[]{:S(2)}, u32[]{:S(2)}) collective-permute-start(bf16[8,32,1024]{2,1,0:T(8,128)(2,1)S(1)} %all-to-all-done.1.refs_8_), channel_id=1, source_target_pairs={{0,16},{16,0},{1,17},{17,1},{2,18},{18,2},{3,19},{19,3},{4,20},{20... | collective-permute-start | bytes 1572872 | tf_op jit(solution)/shard_map/ppermute | solution.py:819
  134.8 46.1 %collective-permute-start.27 = (bf16[1024,256]{1,0:T(8,128)(2,1)S(1)}, bf16[1024,256]{1,0:T(8,128)(2,1)S(1)}, u32[]{:S(2)}, u32[]{:S(2)}) collective-permute-start(bf16[1024,256]{1,0:T(8,128)(2,1)S(1)} %copy-done.50), channel_id=1, source_target_pairs={{0,1},{1,0},{2,3},{3,2},{4,5},{5,4},{6,7},{7,6},{8,9},{9,8},{10,11... | collective-permute-start | bytes 1572872 | tf_op jit(solution)/shard_map/ppermute | solution.py:819
  136.8 44.1 %collective-permute-start.14 = (bf16[8,32,1024]{2,1,0:T(8,128)(2,1)S(1)}, bf16[8,32,1024]{2,1,0:T(8,128)(2,1)S(1)}, u32[]{:S(2)}, u32[]{:S(2)}) collective-permute-start(bf16[8,32,1024]{2,1,0:T(8,128)(2,1)S(1)} %all-to-all-done.1.refs_8_), channel_id=1, source_target_pairs={{0,1},{1,0},{2,3},{3,2},{4,5},{5,4},{6,7},{7,6},{8,9},{9,8},{10,11... | collective-permute-start | bytes 1572872 | tf_op jit(solution)/shard_map/ppermute | solution.py:819
  136.9 45.9 %collective-permute-start.23 = (bf16[1024,256]{1,0:T(8,128)(2,1)}, bf16[1024,256]{1,0:T(8,128)(2,1)S(1)}, u32[]{:S(2)}, u32[]{:S(2)}) collective-permute-start(bf16[1024,256]{1,0:T(8,128)(2,1)} %get-tuple-element.72.refs_2_.refs_4_), channel_id=1, source_target_pairs={{0,4},{4,0},{1,5},{5,1},{2,6},{6,2},{3,7},{7,3},{8,12},{12,8},{9,1... | collective-permute-start | bytes 1572872 | tf_op jit(solution)/shard_map/ppermute | solution.py:819
  137.4 47.4 %collective-permute-start.15 = (bf16[8,32,1024]{2,1,0:T(8,128)(2,1)}, bf16[8,32,1024]{2,1,0:T(8,128)(2,1)S(1)}, u32[]{:S(2)}, u32[]{:S(2)}) collective-permute-start(bf16[8,32,1024]{2,1,0:T(8,128)(2,1)} %collective-permute-done.13.refs_9_), channel_id=1, source_target_pairs={{0,1},{1,0},{2,3},{3,2},{4,5},{5,4},{6,7},{7,6},{8,9},{9,8},{10,11... | collective-permute-start | bytes 1572872 | tf_op jit(solution)/shard_map/ppermute | solution.py:819
  367.9 38.0 %collective-permute-start.62 = (bf16[512,1024]{1,0:T(8,128)(2,1)}, bf16[512,1024]{1,0:T(8,128)(2,1)}, u32[]{:S(2)}, u32[]{:S(2)}) collective-permute-start(bf16[512,1024]{1,0:T(8,128)(2,1)} %get-tuple-element.88), channel_id=1, source_target_pairs={{0,1},{1,0},{2,3},{3,2},{4,5},{5,4},{6,7},{7,6},{8,9},{9,8},{10,11... | collective-permute-start | bytes 3145736 | tf_op jit(solution)/shard_map/ppermute | solution.py:819
  409.2 37.3 %collective-permute-start.63 = (bf16[256,1024]{1,0:T(8,128)(2,1)S(1)}, bf16[256,1024]{1,0:T(8,128)(2,1)S(1)}, u32[]{:S(2)}, u32[]{:S(2)}) collective-permute-start(bf16[256,1024]{1,0:T(8,128)(2,1)S(1)} %fusion.2), channel_id=1, source_target_pairs={{0,16},{16,0},{1,17},{17,1},{2,18},{18,2},{3,19},{19,3},{4,20},{20... | collective-permute-start | bytes 1572872 | tf_op jit(solution)/shard_map/ppermute | solution.py:819
  410.0 35.4 %collective-permute-start.65 = (bf16[128,1024]{1,0:T(8,128)(2,1)S(1)}, bf16[128,1024]{1,0:T(8,128)(2,1)S(1)}, u32[]{:S(2)}, u32[]{:S(2)}) collective-permute-start(bf16[128,1024]{1,0:T(8,128)(2,1)S(1)} %fusion.16), channel_id=1, source_target_pairs={{0,16},{16,0},{1,17},{17,1},{2,18},{18,2},{3,19},{19,3},{4,20},{20... | collective-permute-start | bytes 786440 | tf_op jit(solution)/shard_map/ppermute | solution.py:819
  449.1 282.7 %all-gather.11.cloned.1.call-start = ((), (), s32[]{:S(2)}) async-start(), calls=%async_computation.4 | async-start | bytes 2228224 | tf_op jit(solution)/shard_map/all_gather | solution.py:1076
  453.9 36.4 %collective-permute-start.53 = (bf16[128,1024]{1,0:T(8,128)(2,1)S(1)}, bf16[128,1024]{1,0:T(8,128)(2,1)S(1)}, u32[]{:S(2)}, u32[]{:S(2)}) collective-permute-start(bf16[128,1024]{1,0:T(8,128)(2,1)S(1)} %get-tuple-element.143), channel_id=1, source_target_pairs={{0,8},{8,0},{1,9},{9,1},{2,10},{10,2},{3,11},{11,3},{4,12},{12,4},... | collective-permute-start | bytes 786440 | tf_op jit(solution)/shard_map/ppermute | solution.py:819
  493.2 38.6 %collective-permute-start.56 = (bf16[128,1024]{1,0:T(8,128)(2,1)S(1)}, bf16[128,1024]{1,0:T(8,128)(2,1)S(1)}, u32[]{:S(2)}, u32[]{:S(2)}) collective-permute-start(bf16[128,1024]{1,0:T(8,128)(2,1)S(1)} %get-tuple-element.150.refs_0_), channel_id=1, source_target_pairs={{0,16},{16,0},{1,17},{17,1},{2,18},{18,2},{3,19},{19,3},{4,20},{20... | collective-permute-start | bytes 786440 | tf_op jit(solution)/shard_map/ppermute | solution.py:819
  493.2 38.6 %collective-permute-start.55 = (bf16[128,1024]{1,0:T(8,128)(2,1)S(1)}, bf16[128,1024]{1,0:T(8,128)(2,1)S(1)}, u32[]{:S(2)}, u32[]{:S(2)}) collective-permute-start(bf16[128,1024]{1,0:T(8,128)(2,1)S(1)} %get-tuple-element.150.refs_0_), channel_id=1, source_target_pairs={{0,8},{8,0},{1,9},{9,1},{2,10},{10,2},{3,11},{11,3},{4,12},{12,4},... | collective-permute-start | bytes 786440 | tf_op jit(solution)/shard_map/ppermute | solution.py:819
  496.1 36.2 %collective-permute-start.58 = (bf16[128,1024]{1,0:T(8,128)(2,1)S(1)}, bf16[128,1024]{1,0:T(8,128)(2,1)S(1)}, u32[]{:S(2)}, u32[]{:S(2)}) collective-permute-start(bf16[128,1024]{1,0:T(8,128)(2,1)S(1)} %get-tuple-element.150.refs_0_), channel_id=1, source_target_pairs={{0,2},{2,0},{1,3},{3,1},{4,6},{6,4},{5,7},{7,5},{8,10},{10,8},{9,1... | collective-permute-start | bytes 786440 | tf_op jit(solution)/shard_map/ppermute | solution.py:819
  584.9 39.9 %collective-permute-start.74 = (bf16[1024,256]{1,0:T(8,128)(2,1)S(1)}, bf16[1024,256]{1,0:T(8,128)(2,1)S(1)}, u32[]{:S(2)}, u32[]{:S(2)}) collective-permute-start(bf16[1024,256]{1,0:T(8,128)(2,1)S(1)} %add_convert_fusion), channel_id=1, source_target_pairs={{0,1},{1,0},{2,3},{3,2},{4,5},{5,4},{6,7},{7,6},{8,9},{9,8},{10,11... | collective-permute-start | bytes 1572872 | tf_op jit(solution)/shard_map/ppermute | solution.py:819
  635.2 116.9 %all-gather.9.cloned.1.call-start = ((), (), s32[]{:S(2)}) async-start(), calls=%async_computation.3 | async-start | bytes 7102464 | tf_op jit(solution)/shard_map/all_gather | solution.py:1077
  678.2 36.8 %collective-permute-start.77 = (bf16[128,1024]{1,0:T(8,128)(2,1)S(1)}, bf16[128,1024]{1,0:T(8,128)(2,1)S(1)}, u32[]{:S(2)}, u32[]{:S(2)}) collective-permute-start(bf16[128,1024]{1,0:T(8,128)(2,1)S(1)} %get-tuple-element.140), channel_id=1, source_target_pairs={{0,16},{16,0},{1,17},{17,1},{2,18},{18,2},{3,19},{19,3},{4,20},{20... | collective-permute-start | bytes 786440 | tf_op jit(solution)/shard_map/ppermute | solution.py:819
  (165 other events, 2028.6 us)
Sparse Core Ops, SparseCore 0:
  449.2 116.8 all-gather.6
  635.3 41.6 all-gather.10
  679.8 72.2 all-gather.8

commit v4 on v3

--- a/solution.py
+++ b/solution.py
@@ -862,11 +862,12 @@
     return in_order(in_order(quad, 1, a), 0, b)
 
 
-def halve(x, name):
+def halve(x, name, gate=()):
     me = lax.axis_index(name)
     keep = lax.dynamic_index_in_dim(x, me, 0, keepdims=False)
     send = lax.dynamic_index_in_dim(x, 1 - me, 0, keepdims=False)
-    return keep.astype(jnp.float32) + flip(send.astype(jnp.bfloat16), name).astype(jnp.float32)
+    got = after(flip(send.astype(jnp.bfloat16), name), gate)
+    return keep.astype(jnp.float32) + got.astype(jnp.float32)
 
 
 def layer(
@@ -905,7 +906,8 @@
         return w.reshape(drows, mine, 8, HD).transpose(2, 0, 1, 3).reshape(8, drows, wide)
 
     gains = jnp.concatenate([gain_query, gain_key, gain_attn, gain_mlp])
-    pad = drows * 128 - gains.shape[0]
+    n_gains = gains.shape[0]
+    pad = drows * 128 - n_gains
     gains = jnp.pad(gains, (0, pad)).reshape(1, drows, 128)
     payload = jnp.concatenate(
         [by_team(w_query), by_team(w_key), by_team(w_value), jnp.broadcast_to(gains, (8, drows, 128))],
@@ -913,13 +915,14 @@
     )
     payload = lax.all_to_all(payload, ("h", "l", "c"), 0, 0, tiled=True)
     w_pieces = quarters(payload, "y", "x")
-    gains = jnp.stack([p[:, :, 3 * wide :] for p in w_pieces])
+    lines = -(-(n_gains) // 128)
+    gains = jnp.stack([p[:, :lines, 3 * wide :].reshape(8, lines * 128) for p in w_pieces]).astype(f32)
     if outer > 1:
         w_pieces = [lax.all_gather(p, "o", axis=0, tiled=True) for p in w_pieces]
         gains = lax.all_gather(gains, "o", axis=0)
-    gains = gains.reshape(outer, 2, 2, 2, 2, 2, drows * 128)
-    gains = in_order(in_order(gains, 2, "y"), 1, "x").transpose(0, 3, 4, 2, 5, 1, 6)
-    gains = gains.reshape(devices, drows * 128)
+    gains = gains.reshape(outer, 2, 2, 8, lines * 128)
+    gains = in_order(in_order(gains, 2, "y"), 1, "x").reshape(outer, 2, 2, 2, 2, 2, lines * 128)
+    gains = gains.transpose(0, 3, 4, 2, 5, 1, 6).reshape(devices, lines * 128)
     e_own, d_own = e // devices, d // devices
     full_gq = gains[:, :e_own].reshape(e)
     full_gk = gains[:, e_own : 2 * e_own].reshape(e)
@@ -949,12 +952,6 @@
 
     ff = after(jnp.concatenate([by_unit(w_gate), by_unit(w_up)], axis=2), payload)
     ff = lax.all_to_all(ff, ("l", "y", "c"), 0, 0, tiled=True)
-    f_pieces = quarters(ff, "h", "x")
-    d_pieces = quarters(w_down[None], "h", "x")
-    if outer > 1:
-        f_pieces = [lax.all_gather(p, "o", axis=0, tiled=True) for p in f_pieces]
-        d_pieces = [lax.all_gather(p, "o", axis=0, tiled=True) for p in d_pieces]
-
     table = positions.reshape(outer, 2, 2, 2, 2, 2, rows)[..., ::blk] // blk
     for axis, name in enumerate(every):
         if name != "o":
@@ -981,6 +978,13 @@
     group = 8 * rows
     pre, value, squares, w_qkv = project(me_yx, xs, w_pieces, wide)
     squares = sum8(squares, "h", "l")
+    ff = after(ff, squares)
+    w_down = after(w_down[None], squares)
+    f_pieces = quarters(ff, "h", "x")
+    d_pieces = quarters(w_down, "h", "x")
+    if outer > 1:
+        f_pieces = [lax.all_gather(p, "o", axis=0, tiled=True) for p in f_pieces]
+        d_pieces = [lax.all_gather(p, "o", axis=0, tiled=True) for p in d_pieces]
     query, key = prepare(pre, squares, gain_qk, cosine, sine, mine, HD, e)
     key_y, value_x = flip(key, "y"), flip(value, "x")
     keys = [key, key_y, flip(key, "x"), flip(key_y, "x")]
@@ -988,7 +992,7 @@
     if outer > 1:
         keys = [lax.all_gather(jnp.stack(keys), "o", axis=0).reshape(-1, wide)]
         values = [lax.all_gather(jnp.stack(values), "o", axis=0).reshape(-1, wide)]
-    query = after(query, f_pieces, d_pieces)
+    query = after(query, f_pieces[1], d_pieces[1])
     attended, lse, own, send = attend(place, seq, kslot, query, keys, values, w_o, mine, HD, blk)
     proj = scatter8(own, send, "h", "l")
     attn_branch, a_recip = norm_forward(proj, full_ga)
@@ -1007,25 +1011,21 @@
 
     ctx = ("o", "h", "l", "y", "c")
 
-    def settle(keep, send, a):
-        cols = keep.shape[1]
-        part = keep + flip(send, "x").astype(f32)
-        part = halve(part.reshape(2, -1, cols), a)
+    def fold(part, a, gate=()):
+        cols = part.shape[1]
+        part = halve(part.reshape(2, -1, cols), a, gate)
         if outer > 1:
             part = lax.psum_scatter(
                 part.astype(bf16).reshape(outer, -1, cols), "o", scatter_dimension=0, tiled=False
             )
         return part.astype(bf16)
 
-    part_gu, part_d = settle(keep_gu, send_gu, "h"), settle(keep_d, send_d, "h")
-    part_f = jnp.concatenate([part_gu, part_d]) if outer == 1 else part_gu
-
     d_proj_f, local_ga = norm_backward(proj, a_recip, full_ga, d_mid)
     pgs = gather8(d_proj_f.astype(bf16), "h", "l")
+    got_gu, got_d = after((flip(send_gu, "x"), flip(send_d, "x")), pgs)
+    sum_gu, sum_d = keep_gu + got_gu.astype(f32), keep_d + got_d.astype(f32)
     d_att, keep_o, send_o = project_back(me_x, attended, w_o, pgs)
-    d_att = after(d_att, part_f)
-    if outer == 1:
-        first = lax.all_gather(part_f, ctx, axis=0).reshape(16, -1, d)
+    d_att = after(d_att, sum_gu, sum_d)
     dq_rot, dk, dv = attend_back(
         place, seq, kslot, query, keys, values, attended, d_att, lse, mine, HD, blk
     )
@@ -1048,7 +1048,9 @@
     grad_input = d_mid + scatter8(own, send, "h", "l")
 
     half_d, half_f = d // 2, f // 2
-    part_o, part_qkv = settle(keep_o, send_o, "y"), settle(keep_qkv, send_qkv, "y")
+    part_gu, part_d = fold(sum_gu, "h", dq_rot), fold(sum_d, "h", dq_rot)
+    part_o = fold(keep_o + flip(send_o, "x").astype(f32), "y")
+    part_qkv = fold(keep_qkv + flip(send_qkv, "x").astype(f32), "y")
     n_qk, n_am = wide, d
     lines = -(-max(n_qk, n_am) // (3 * wide))
     lines = -(-lines // 16) * 16
@@ -1072,10 +1074,10 @@
     n_gu, n_d, n_o, n_qkv = part_gu.shape[0], part_d.shape[0], part_o.shape[0], part_qkv.shape[0] - lines
 
     if outer == 1:
+        first = lax.all_gather(jnp.concatenate([part_gu, part_d, part_o]), ctx, axis=0).reshape(16, -1, d)
         part_qkv = after(part_qkv, first)
-        middle = lax.all_gather(after(part_o, first), ctx, axis=0).reshape(16, -1, d)
         last = lax.all_gather(part_qkv, ctx, axis=0).reshape(16, -1, 3 * wide)
-        plan_first, plan_middle, plan_last = [], [], []
+        plan_first, plan_last = [], []
         for p in range(16):
             h, l, y, c = p >> 3, (p >> 2) & 1, (p >> 1) & 1, p & 1
             team_f, team_q = 4 * l + 2 * y + c, 4 * h + 2 * l + c
@@ -1087,8 +1089,8 @@
                 for m in range(2)
             ]
             downs = [((n_gu, n_d), (0, d), team_f * unit + h * n_d, 0)]
-            plan_first.append([*ups, downs])
-            plan_middle.append([[((0, n_o), (0, d), team_q * HD + y * n_o, 0)]])
+            outs = [((n_gu + n_d, n_o), (0, d), team_q * HD + y * n_o, 0)]
+            plan_first.append([*ups, downs, outs])
             plan_last.append(
                 [
                     [
@@ -1098,10 +1100,9 @@
                     for m in range(3)
                 ]
             )
-        total_wg, total_wu, total_wd = unpack(
-            first, [(half_d, f), (half_d, f), (half_f, d)], plan_first, n_gu + n_d
+        total_wg, total_wu, total_wd, total_wo = unpack(
+            first, [(half_d, f), (half_d, f), (half_f, d), (e // 2, d)], plan_first, n_gu + n_d + n_o
         )
-        (total_wo,) = unpack(middle, [(e // 2, d)], plan_middle, n_o)
         total_wq, total_wk, total_wv = unpack(last, [(half_d, e)] * 3, plan_last, n_qkv)
         got_small = last[:, n_qkv:]
     else:

time: 782 us -> 628 us (0.80)
  waiting for transfers between devices: 430 us -> 311 us
  local copies, waits for them, and re-layouts: 59.1 us -> 21.4 us
    ppermute x84, waiting for transfers between devices: 398 us -> 263 us  [flip(): return lax.ppermute(value, axes, [(i, i ^ last) for i in range(last + 1)])]
    unnamed x204 -> x182, local copies, waits for them, and re-layouts: 37.6 us -> 10.8 us
    rev x2 -> x1, local copies, waits for them, and re-layouts: 10.5 us -> 0.04 us  [in_order(): return jnp.where(lax.axis_index(name) == 1, jnp.flip(value, axis), value)]
    all_gather x2 -> x1, waiting for transfers between devices: 0.02 us -> 9.64 us  [layer(): lax.all_gather(jnp.concatenate([part_gu, part_d, part_o]), ctx, axis=0)]
    pallas_call x3 -> x2, Pallas kernels: 24.6 us -> 24.5 us  [unpack(): pl.pallas_call(functools.partial(unpack_kernel, plan=plan, pieces=pieces,...]
  transfers between devices with their start and end apart: 90 -> 89, of which waited for: 51 -> 50; matrix products, arithmetic and copies ran while one was open for 6% -> 6% of each run, Pallas kernels for 10% -> 14%
where the time goes in v4:
time: 628 us; the launch traced here: 620 us
  waiting for transfers between devices  311 us (50%)
  Pallas kernels  135 us (21%)
  starting transfers between devices  97.3 us (15%)
  other arithmetic  38.3 us (6%)
  local copies, waits for them, and re-layouts  21.4 us (3%)
  between operations  16.1 us (3%)
    ppermute x84, waiting for transfers between devices, flip(): return lax.ppermute(value, axes, [(i, i ^ last) for i in range(last + 1)])  263 us
    ppermute x84, starting transfers between devices, flip(): return lax.ppermute(value, axes, [(i, i ^ last) for i in range(last + 1)])  82.5 us
    pallas_call x1, Pallas kernels, attend_back(): pl.pallas_call(functools.partial(attend_back_kernel, heads=heads, head_si...  25.3 us
    pallas_call x2, Pallas kernels, unpack(): pl.pallas_call(functools.partial(unpack_kernel, plan=plan, pieces=pieces,...  24.5 us
    pallas_call x1, Pallas kernels, attend(): pl.pallas_call(functools.partial(attend_kernel, heads=heads, head_size=he...  22.6 us
    all_to_all x1, waiting for transfers between devices, layer(): payload = lax.all_to_all(payload, ('h', 'l', 'c'), 0, 0, tiled=True)  21.9 us
    all_gather x1, waiting for transfers between devices, layer(): last = lax.all_gather(part_qkv, ctx, axis=0).reshape(16, -1, 3 * wide)  16.7 us
  transfers between devices with their start and end apart: 89, of which 50 were waited for; matrix products, arithmetic and copies ran while one was open for 6% of the time, Pallas kernels for 14%

profile of v4, /device:TPU:0, one launch (start us, length us, event | category | flops | bytes accessed | tf_op | source)
XLA Modules:
  0.0 619.6 jit_solution(8165384266371272258)
XLA Ops:
  23.7 21.9 %all-to-all-done.refs_8_ = bf16[8,32,896]{2,1,0:T(8,128)(2,1)S(1)} async-done(((bf16[8,32,896]{2,1,0:T(8,128)(2,1)}), bf16[8,32,896]{2,1,0:T(8,128)(2,1)S(1)}, u32[]{:S(2)}, u32[]{:S(2)}) %all-to-all-start) | async-done | bytes 458784 | tf_op jit(solution)/shard_map/all_to_all | solution.py:916
  50.3 7.0 %collective-permute-done.7.refs_9_ = bf16[8,32,896]{2,1,0:T(8,128)(2,1)S(1)} collective-permute-done((bf16[8,32,896]{2,1,0:T(8,128)(2,1)S(1)}, bf16[8,32,896]{2,1,0:T(8,128)(2,1)S(1)}, u32[]{:S(2)}, u32[]{:S(2)}) %collective-permute-start.7) | collective-permute-done | bytes 458784 | tf_op jit(solution)/shard_map/ppermute | solution.py:819
  116.9 20.4 %collective-permute-done.14.refs_13_ = bf16[1,128,1024]{2,1,0:T(8,128)(2,1)} collective-permute-done((bf16[1,128,1024]{2,1,0:T(8,128)(2,1)}, bf16[1,128,1024]{2,1,0:T(8,128)(2,1)}, u32[]{:S(2)}, u32[]{:S(2)}) %collective-permute-start.14) | collective-permute-done | bytes 262176 | tf_op jit(solution)/shard_map/ppermute | solution.py:819
  142.8 14.7 %collective-permute-done.22.refs_7_.refs_9_ = bf16[1024,256]{1,0:T(8,128)(2,1)S(1)} collective-permute-done((bf16[1024,256]{1,0:T(8,128)(2,1)S(1)}, bf16[1024,256]{1,0:T(8,128)(2,1)S(1)}, u32[]{:S(2)}, u32[]{:S(2)}) %collective-permute-start.22) | collective-permute-done | bytes 524320 | tf_op jit(solution)/shard_map/ppermute | solution.py:819
  157.5 11.1 %collective-permute-done.24.refs_9_.refs_11_ = bf16[1024,256]{1,0:T(8,128)(2,1)} collective-permute-done((bf16[1024,256]{1,0:T(8,128)(2,1)S(1)}, bf16[1024,256]{1,0:T(8,128)(2,1)}, u32[]{:S(2)}, u32[]{:S(2)}) %collective-permute-start.24) | collective-permute-done | bytes 524320 | tf_op jit(solution)/shard_map/ppermute | solution.py:819
  168.6 22.6 %attend.1 = (bf16[1024,256]{1,0:T(8,128)(2,1)}, f32[8,256]{1,0:T(8,128)}, f32[512,1024]{1,0:T(8,128)}, bf16[512,1024]{1,0:T(8,128)(2,1)}) custom-call(s32[16]{0:T(128)} %copy-done.82, s32[16]{0:T(128)} %select_reduce_fusion.seq_ref, s32[64]{0:T(128)} %reshape.284.kslot_ref, bf16[1024,256]{1,0:T(8,128)(2,1)} %get-tuple-element.79.refs_0_, ...), custom_call_target="tpu_custom_call" | custom-call | tf_op jit(solution)/shard_map/attend/pallas_call | solution.py:145
  215.1 9.4 %collective-permute-done.27 = bf16[128,1024]{1,0:T(8,128)(2,1)} collective-permute-done((bf16[128,1024]{1,0:T(8,128)(2,1)}, bf16[128,1024]{1,0:T(8,128)(2,1)}, u32[]{:S(2)}, u32[]{:S(2)}) %collective-permute-start.27) | collective-permute-done | bytes 262176 | tf_op jit(solution)/shard_map/ppermute | solution.py:819
  242.9 10.3 %expand.1 = (f32[1024,1024]{1,0:T(8,128)}, bf16[1024,512]{1,0:T(8,128)(2,1)}, f32[512,1024]{1,0:T(8,128)}, bf16[512,1024]{1,0:T(8,128)(2,1)}, bf16[1024,1024]{1,0:T(8,128)(2,1)}, /*index=5*/bf16[512,1024]{1,0:T(8,128)(2,1)}) custom-call(s32[2]{0:T(128)} %pad_add_fusion.1.me_ref, bf16[128,1024]{1,0:T(8,128)(2,1)} %copy-done.3, bf16[128,1024]{1,0:T(8,128)(2,1)} %copy-done.25, ...), custom_call_target="tpu_custom_call" | custom-call | tf_op jit(solution)/shard_map/expand/pallas_call | solution.py:519
  262.7 10.9 %collective-permute-done.41 = bf16[128,1024]{1,0:T(8,128)(2,1)S(1)} collective-permute-done((bf16[128,1024]{1,0:T(8,128)(2,1)}, bf16[128,1024]{1,0:T(8,128)(2,1)S(1)}, u32[]{:S(2)}, u32[]{:S(2)}) %collective-permute-start.41) | collective-permute-done | bytes 262176 | tf_op jit(solution)/shard_map/ppermute | solution.py:819
  292.7 10.3 %contract.1 = (bf16[1024,1024]{1,0:T(8,128)(2,1)}, f32[512,1024]{1,0:T(8,128)}, bf16[512,1024]{1,0:T(8,128)(2,1)}) custom-call(f32[1024,1024]{1,0:T(8,128)} %get-tuple-element.86.gu_ref, bf16[1024,1024]{1,0:T(8,128)(2,1)} %get-tuple-element.87.w_ref, bf16[512,1024]{1,0:T(8,128)(2,1)} %get-tuple-element.88.d_ref, bf16[128,1024]{1,0:T(8,128)(2,1)} %copy-done.1, ...), custom_call_target="tpu_custom_call" | custom-call | tf_op jit(solution)/shard_map/contract/pallas_call | solution.py:572
  336.5 13.6 %collective-permute-done.56.refs_2_ = bf16[128,1024]{1,0:T(8,128)(2,1)} collective-permute-done((bf16[128,1024]{1,0:T(8,128)(2,1)S(1)}, bf16[128,1024]{1,0:T(8,128)(2,1)}, u32[]{:S(2)}, u32[]{:S(2)}) %collective-permute-start.56) | collective-permute-done | bytes 262176 | tf_op jit(solution)/shard_map/ppermute | solution.py:819
  365.1 25.3 %attend_back.1 = (f32[1024,256]{1,0:T(8,128)}, bf16[1024,256]{1,0:T(8,128)(2,1)}, bf16[1024,256]{1,0:T(8,128)(2,1)}, bf16[1024,256]{1,0:T(8,128)(2,1)}, bf16[102...) custom-call(s32[16]{0:T(128)} %copy-done.82, ...), custom_call_target="tpu_custom_call" | custom-call | tf_op jit(solution)/shard_map/attend_back/pallas_call | solution.py:257
  404.4 10.7 %collective-permute-done.65 = bf16[1024,256]{1,0:T(8,128)(2,1)S(1)} collective-permute-done((bf16[1024,256]{1,0:T(8,128)(2,1)}, bf16[1024,256]{1,0:T(8,128)(2,1)S(1)}, u32[]{:S(2)}, u32[]{:S(2)}) %collective-permute-start.65) | collective-permute-done | bytes 524320 | tf_op jit(solution)/shard_map/ppermute | solution.py:819
  427.4 9.3 %collective-permute-done.70 = bf16[1024,256]{1,0:T(8,128)(2,1)S(1)} collective-permute-done((bf16[1024,256]{1,0:T(8,128)(2,1)S(1)}, bf16[1024,256]{1,0:T(8,128)(2,1)S(1)}, u32[]{:S(2)}, u32[]{:S(2)}) %collective-permute-start.70) | collective-permute-done | bytes 524320 | tf_op jit(solution)/shard_map/ppermute | solution.py:819
  437.8 8.9 %collective-permute-done.66.dkb_ref = bf16[1024,256]{1,0:T(8,128)(2,1)S(1)} collective-permute-done((bf16[1024,256]{1,0:T(8,128)(2,1)S(1)}, bf16[1024,256]{1,0:T(8,128)(2,1)S(1)}, u32[]{:S(2)}, u32[]{:S(2)}) %collective-permute-start.66) | collective-permute-done | bytes 524320 | tf_op jit(solution)/shard_map/ppermute | solution.py:819
  470.0 8.7 %norms_back.1 = (bf16[1024,768]{1,0:T(8,128)(2,1)}, f32[512,768]{1,0:T(8,128)}, bf16[512,768]{1,0:T(8,128)(2,1)}) custom-call(s32[1]{0:T(128)} %bitcast.4.me_ref, f32[1024,512]{1,0:T(8,128)} %get-tuple-element.108.ds_ref, f32[2,1024]{1,0:T(2,128)} %bitcast_add_fusion.7.sums_ref, f32[2,1024]{1,0:T(2,128)} %bitcast_add_fusion.4.dsums_ref, ...), custom_call_target="tpu_custom_call" | custom-call | tf_op jit(solution)/shard_map/norms_back/pallas_call | solution.py:702
  485.0 10.5 %collective-permute-done.77 = bf16[512,768]{1,0:T(8,128)(2,1)S(1)} collective-permute-done((bf16[512,768]{1,0:T(8,128)(2,1)}, bf16[512,768]{1,0:T(8,128)(2,1)S(1)}, u32[]{:S(2)}, u32[]{:S(2)}) %collective-permute-start.77) | collective-permute-done | bytes 786464 | tf_op jit(solution)/shard_map/ppermute | solution.py:819
  498.1 6.9 %collective-permute-done.78 = bf16[256,768]{1,0:T(8,128)(2,1)S(1)} collective-permute-done((bf16[256,768]{1,0:T(8,128)(2,1)S(1)}, bf16[256,768]{1,0:T(8,128)(2,1)S(1)}, u32[]{:S(2)}, u32[]{:S(2)}) %collective-permute-start.78) | collective-permute-done | bytes 393248 | tf_op jit(solution)/shard_map/ppermute | solution.py:819
  505.8 9.6 %all-gather.5.cloned.1.call-done = bf16[7168,1024]{1,0:T(8,128)(2,1)} async-done(((bf16[448,1024]{1,0:T(8,128)(2,1)}), bf16[7168,1024]{1,0:T(8,128)(2,1)}) %all-gather.5.cloned.1.call-update) | async-done | bytes 14680080 | tf_op jit(solution)/shard_map/all_gather | solution.py:1077
  530.2 17.5 %collective-permute-done.74 = bf16[128,1024]{1,0:T(8,128)(2,1)S(1)} collective-permute-done((bf16[128,1024]{1,0:T(8,128)(2,1)S(1)}, bf16[128,1024]{1,0:T(8,128)(2,1)S(1)}, u32[]{:S(2)}, u32[]{:S(2)}) %collective-permute-start.74) | collective-permute-done | bytes 262176 | tf_op jit(solution)/shard_map/ppermute | solution.py:819
  553.7 10.6 %collective-permute-done.75 = bf16[128,1024]{1,0:T(8,128)(2,1)S(1)} collective-permute-done((bf16[128,1024]{1,0:T(8,128)(2,1)S(1)}, bf16[128,1024]{1,0:T(8,128)(2,1)S(1)}, u32[]{:S(2)}, u32[]{:S(2)}) %collective-permute-start.75) | collective-permute-done | bytes 262176 | tf_op jit(solution)/shard_map/ppermute | solution.py:819
  565.4 16.5 %unpack.3 = (f32[512,4096]{1,0:T(8,128)}, f32[512,4096]{1,0:T(8,128)}, f32[2048,1024]{1,0:T(8,128)}, f32[1024,1024]{1,0:T(8,128)}) custom-call(bf16[16,448,1024]{2,1,0:T(8,128)(2,1)} %bitcast.153), custom_call_target="tpu_custom_call" | custom-call | tf_op jit(solution)/shard_map/unpack/pallas_call | solution.py:781
  581.9 16.7 %all-gather.7.cloned.1.call-done = bf16[4352,768]{1,0:T(8,128)(2,1)} async-done(((bf16[272,768]{1,0:T(8,128)(2,1)}), bf16[4352,768]{1,0:T(8,128)(2,1)}) %all-gather.7.cloned.1.call-update) | async-done | bytes 6684688 | tf_op jit(solution)/shard_map/all_gather | solution.py:1079
  603.1 8.0 %unpack.2 = (f32[512,2048]{1,0:T(8,128)}, f32[512,2048]{1,0:T(8,128)}, f32[512,2048]{1,0:T(8,128)}) custom-call(bf16[16,272,768]{2,1,0:T(8,128)(2,1)S(1)} %bitcast.152), custom_call_target="tpu_custom_call" | custom-call | tf_op jit(solution)/shard_map/unpack/pallas_call | solution.py:781
  (490 shorter events, 292.1 us)
Async XLA Ops:
  8.4 59.3 %collective-permute-start.2 = (bf16[128,1024]{1,0:T(8,128)(2,1)S(1)}, bf16[128,1024]{1,0:T(8,128)(2,1)S(1)}, u32[]{:S(2)}, u32[]{:S(2)}) collective-permute-start(bf16[128,1024]{1,0:T(8,128)(2,1)S(1)} %convert_element_type.224.refs_0_), channel_id=1, source_target_pairs={{0,24},{8,16},{16,8},{24,0},{1,25},{9,17},{17,9},{25,1},{2,26},{10... | collective-permute-start | bytes 786440 | tf_op jit(solution)/shard_map/ppermute | solution.py:819
  13.5 55.5 %collective-permute-start.1 = (bf16[128,1024]{1,0:T(8,128)(2,1)S(1)}, bf16[128,1024]{1,0:T(8,128)(2,1)S(1)}, u32[]{:S(2)}, u32[]{:S(2)}) collective-permute-start(bf16[128,1024]{1,0:T(8,128)(2,1)S(1)} %convert_element_type.224.refs_0_), channel_id=1, source_target_pairs={{0,16},{16,0},{1,17},{17,1},{2,18},{18,2},{3,19},{19,3},{4,20},{20... | collective-permute-start | bytes 786440 | tf_op jit(solution)/shard_map/ppermute | solution.py:819
  13.5 55.5 %collective-permute-start = (bf16[128,1024]{1,0:T(8,128)(2,1)S(1)}, bf16[128,1024]{1,0:T(8,128)(2,1)S(1)}, u32[]{:S(2)}, u32[]{:S(2)}) collective-permute-start(bf16[128,1024]{1,0:T(8,128)(2,1)S(1)} %convert_element_type.224.refs_0_), channel_id=1, source_target_pairs={{0,8},{8,0},{1,9},{9,1},{2,10},{10,2},{3,11},{11,3},{4,12},{12,4},... | collective-permute-start | bytes 786440 | tf_op jit(solution)/shard_map/ppermute | solution.py:819
  17.7 28.0 %all-to-all-start = ((bf16[8,32,896]{2,1,0:T(8,128)(2,1)}), bf16[8,32,896]{2,1,0:T(8,128)(2,1)S(1)}, u32[]{:S(2)}, u32[]{:S(2)}) async-start(bf16[8,32,896]{2,1,0:T(8,128)(2,1)} %pad_maximum_fusion.5), calls=%async_computation | async-start | bytes 917504 | tf_op jit(solution)/shard_map/all_to_all | solution.py:916
  63.0 37.1 %all-to-all-start.1 = ((bf16[8,32,1024]{2,1,0:T(8,128)(2,1)}), bf16[8,32,1024]{2,1,0:T(8,128)(2,1)}, u32[]{:S(2)}, u32[]{:S(2)}) async-start(bf16[8,32,1024]{2,1,0:T(8,128)(2,1)} %pad_maximum_fusion.3), calls=%async_computation.1 | async-start | bytes 1048576 | tf_op jit(solution)/shard_map/all_to_all | solution.py:954
  67.1 448.3 %all-gather.5.cloned.1.call-start = ((), (), s32[]{:S(2)}) async-start(), calls=%async_computation.2 | async-start | bytes 15597568 | tf_op jit(solution)/shard_map/all_gather | solution.py:1077
  76.6 31.9 %collective-permute-start.16 = (bf16[64,1024]{1,0:T(8,128)(2,1)S(1)}, bf16[64,1024]{1,0:T(8,128)(2,1)S(1)}, u32[]{:S(2)}, u32[]{:S(2)}) collective-permute-start(bf16[64,1024]{1,0:T(8,128)(2,1)S(1)} %copy-done.80), channel_id=1, source_target_pairs={{0,1},{1,0},{2,3},{3,2},{4,5},{5,4},{6,7},{7,6},{8,9},{9,8},{10,11... | collective-permute-start | bytes 393224 | tf_op jit(solution)/shard_map/ppermute | solution.py:819
  77.1 31.3 %collective-permute-start.17 = (bf16[64,1024]{1,0:T(8,128)(2,1)}, bf16[64,1024]{1,0:T(8,128)(2,1)S(1)}, u32[]{:S(2)}, u32[]{:S(2)}) collective-permute-start(bf16[64,1024]{1,0:T(8,128)(2,1)} %collective-permute-done.15), channel_id=1, source_target_pairs={{0,1},{1,0},{2,3},{3,2},{4,5},{5,4},{6,7},{7,6},{8,9},{9,8},{10,11... | collective-permute-start | bytes 393224 | tf_op jit(solution)/shard_map/ppermute | solution.py:819
  87.7 51.0 %collective-permute-start.23 = (bf16[1024,256]{1,0:T(8,128)(2,1)}, bf16[1024,256]{1,0:T(8,128)(2,1)S(1)}, u32[]{:S(2)}, u32[]{:S(2)}) collective-permute-start(bf16[1024,256]{1,0:T(8,128)(2,1)} %get-tuple-element.81.refs_6_.refs_8_), channel_id=1, source_target_pairs={{0,1},{1,0},{2,3},{3,2},{4,5},{5,4},{6,7},{7,6},{8,9},{9,8},{10,11... | collective-permute-start | bytes 1572872 | tf_op jit(solution)/shard_map/ppermute | solution.py:819
  100.1 40.3 %collective-permute-start.13 = (bf16[8,32,1024]{2,1,0:T(8,128)(2,1)}, bf16[8,32,1024]{2,1,0:T(8,128)(2,1)}, u32[]{:S(2)}, u32[]{:S(2)}) collective-permute-start(bf16[8,32,1024]{2,1,0:T(8,128)(2,1)} %all-to-all-done.1.refs_8_), channel_id=1, source_target_pairs={{0,16},{16,0},{1,17},{17,1},{2,18},{18,2},{3,19},{19,3},{4,20},{20... | collective-permute-start | bytes 1572872 | tf_op jit(solution)/shard_map/ppermute | solution.py:819
  106.8 34.1 %collective-permute-start.19 = (bf16[1024,256]{1,0:T(8,128)(2,1)}, bf16[1024,256]{1,0:T(8,128)(2,1)S(1)}, u32[]{:S(2)}, u32[]{:S(2)}) collective-permute-start(bf16[1024,256]{1,0:T(8,128)(2,1)} %get-tuple-element.80.refs_2_.refs_4_), channel_id=1, source_target_pairs={{0,4},{4,0},{1,5},{5,1},{2,6},{6,2},{3,7},{7,3},{8,12},{12,8},{9,1... | collective-permute-start | bytes 1572872 | tf_op jit(solution)/shard_map/ppermute | solution.py:819
  111.4 31.4 %collective-permute-start.18 = (bf16[256,1024]{1,0:T(8,128)(2,1)}, bf16[256,1024]{1,0:T(8,128)(2,1)}, u32[]{:S(2)}, u32[]{:S(2)}) collective-permute-start(bf16[256,1024]{1,0:T(8,128)(2,1)} %bitcast.28), channel_id=1, source_target_pairs={{0,0},{4,8},{8,16},{12,24},{16,4},{20,12},{24,20},{28,28},{1,1},{5... | collective-permute-start | bytes 1572872 | tf_op jit(solution)/shard_map/ppermute | solution.py:940
  140.3 28.3 %collective-permute-start.24 = (bf16[1024,256]{1,0:T(8,128)(2,1)S(1)}, bf16[1024,256]{1,0:T(8,128)(2,1)}, u32[]{:S(2)}, u32[]{:S(2)}) collective-permute-start(bf16[1024,256]{1,0:T(8,128)(2,1)S(1)} %collective-permute-done.23.refs_8_.refs_10_), channel_id=1, source_target_pairs={{0,4},{4,0},{1,5},{5,1},{2,6},{6,2},{3,7},{7,3},{8,12},{12,8},{9,1... | collective-permute-start | bytes 1572872 | tf_op jit(solution)/shard_map/ppermute | solution.py:819
  140.9 27.7 %collective-permute-start.21 = (bf16[1024,256]{1,0:T(8,128)(2,1)S(1)}, bf16[1024,256]{1,0:T(8,128)(2,1)}, u32[]{:S(2)}, u32[]{:S(2)}) collective-permute-start(bf16[1024,256]{1,0:T(8,128)(2,1)S(1)} %collective-permute-done.19.refs_3_.refs_5_), channel_id=1, source_target_pairs={{0,1},{1,0},{2,3},{3,2},{4,5},{5,4},{6,7},{7,6},{8,9},{9,8},{10,11... | collective-permute-start | bytes 1572872 | tf_op jit(solution)/shard_map/ppermute | solution.py:819
  317.2 41.5 %collective-permute-start.62 = (bf16[512,1024]{1,0:T(8,128)(2,1)}, bf16[512,1024]{1,0:T(8,128)(2,1)}, u32[]{:S(2)}, u32[]{:S(2)}) collective-permute-start(bf16[512,1024]{1,0:T(8,128)(2,1)} %get-tuple-element.96), channel_id=1, source_target_pairs={{0,1},{1,0},{2,3},{3,2},{4,5},{5,4},{6,7},{7,6},{8,9},{9,8},{10,11... | collective-permute-start | bytes 3145736 | tf_op jit(solution)/shard_map/ppermute | solution.py:819
  329.6 29.1 %collective-permute-start.63 = (bf16[256,1024]{1,0:T(8,128)(2,1)}, bf16[256,1024]{1,0:T(8,128)(2,1)}, u32[]{:S(2)}, u32[]{:S(2)}) collective-permute-start(bf16[256,1024]{1,0:T(8,128)(2,1)} %get-tuple-element.97), channel_id=1, source_target_pairs={{0,1},{1,0},{2,3},{3,2},{4,5},{5,4},{6,7},{7,6},{8,9},{9,8},{10,11... | collective-permute-start | bytes 1572872 | tf_op jit(solution)/shard_map/ppermute | solution.py:819
  357.2 33.2 %collective-permute-start.83 = (bf16[128,1024]{1,0:T(8,128)(2,1)}, bf16[128,1024]{1,0:T(8,128)(2,1)S(1)}, u32[]{:S(2)}, u32[]{:S(2)}) collective-permute-start(bf16[128,1024]{1,0:T(8,128)(2,1)} %get-tuple-element.124), channel_id=1, source_target_pairs={{0,1},{1,0},{2,3},{3,2},{4,5},{5,4},{6,7},{7,6},{8,9},{9,8},{10,11... | collective-permute-start | bytes 786440 | tf_op jit(solution)/shard_map/ppermute | solution.py:819
  362.0 28.9 %collective-permute-start.82 = (bf16[128,1024]{1,0:T(8,128)(2,1)S(1)}, bf16[128,1024]{1,0:T(8,128)(2,1)S(1)}, u32[]{:S(2)}, u32[]{:S(2)}) collective-permute-start(bf16[128,1024]{1,0:T(8,128)(2,1)S(1)} %fusion.15), channel_id=1, source_target_pairs={{0,16},{16,0},{1,17},{17,1},{2,18},{18,2},{3,19},{19,3},{4,20},{20... | collective-permute-start | bytes 786440 | tf_op jit(solution)/shard_map/ppermute | solution.py:819
  362.2 36.7 %collective-permute-start.81 = (bf16[256,1024]{1,0:T(8,128)(2,1)S(1)}, bf16[256,1024]{1,0:T(8,128)(2,1)S(1)}, u32[]{:S(2)}, u32[]{:S(2)}) collective-permute-start(bf16[256,1024]{1,0:T(8,128)(2,1)S(1)} %fusion.2), channel_id=1, source_target_pairs={{0,16},{16,0},{1,17},{17,1},{2,18},{18,2},{3,19},{19,3},{4,20},{20... | collective-permute-start | bytes 1572872 | tf_op jit(solution)/shard_map/ppermute | solution.py:819
  400.0 198.5 %all-gather.7.cloned.1.call-start = ((), (), s32[]{:S(2)}) async-start(), calls=%async_computation.3 | async-start | bytes 7102464 | tf_op jit(solution)/shard_map/all_gather | solution.py:1079
  403.4 33.3 %collective-permute-start.70 = (bf16[1024,256]{1,0:T(8,128)(2,1)S(1)}, bf16[1024,256]{1,0:T(8,128)(2,1)S(1)}, u32[]{:S(2)}, u32[]{:S(2)}) collective-permute-start(bf16[1024,256]{1,0:T(8,128)(2,1)S(1)} %copy-done.87), channel_id=1, source_target_pairs={{0,4},{4,0},{1,5},{5,1},{2,6},{6,2},{3,7},{7,3},{8,12},{12,8},{9,1... | collective-permute-start | bytes 1572872 | tf_op jit(solution)/shard_map/ppermute | solution.py:819
  415.3 31.5 %collective-permute-start.66 = (bf16[1024,256]{1,0:T(8,128)(2,1)S(1)}, bf16[1024,256]{1,0:T(8,128)(2,1)S(1)}, u32[]{:S(2)}, u32[]{:S(2)}) collective-permute-start(bf16[1024,256]{1,0:T(8,128)(2,1)S(1)} %add_convert_fusion.1), channel_id=1, source_target_pairs={{0,4},{4,0},{1,5},{5,1},{2,6},{6,2},{3,7},{7,3},{8,12},{12,8},{9,1... | collective-permute-start | bytes 1572872 | tf_op jit(solution)/shard_map/ppermute | solution.py:819
  422.6 46.6 %collective-permute-start.72 = (bf16[1024,256]{1,0:T(8,128)(2,1)S(1)}, bf16[1024,256]{1,0:T(8,128)(2,1)S(1)}, u32[]{:S(2)}, u32[]{:S(2)}) collective-permute-start(bf16[1024,256]{1,0:T(8,128)(2,1)S(1)} %add_convert_fusion), channel_id=1, source_target_pairs={{0,1},{1,0},{2,3},{3,2},{4,5},{5,4},{6,7},{7,6},{8,9},{9,8},{10,11... | collective-permute-start | bytes 1572872 | tf_op jit(solution)/shard_map/ppermute | solution.py:819
  529.7 34.6 %collective-permute-start.75 = (bf16[128,1024]{1,0:T(8,128)(2,1)S(1)}, bf16[128,1024]{1,0:T(8,128)(2,1)S(1)}, u32[]{:S(2)}, u32[]{:S(2)}) collective-permute-start(bf16[128,1024]{1,0:T(8,128)(2,1)S(1)} %get-tuple-element.152), channel_id=1, source_target_pairs={{0,16},{16,0},{1,17},{17,1},{2,18},{18,2},{3,19},{19,3},{4,20},{20... | collective-permute-start | bytes 786440 | tf_op jit(solution)/shard_map/ppermute | solution.py:819
  (153 other events, 1748.0 us)
Sparse Core Ops, SparseCore 0:
  400.1 115.2 all-gather.4
  518.3 80.2 all-gather.6
